TPU v7x, 32 devices: a whole 2x2x4 slice. The times are simulated.
32 devices in a mesh: rep: 16 (over z, y, core), shard: 2 (over x).
Axes of the slice: x: 2, y: 2, z: 4, core: 2. Of those that a mesh axis runs over, the one named last changes fastest.
Arguments:
- token_in: bfloat16 [16384, 768], P(('rep', 'shard')), may hold values from -6 to 6
- char_in: bfloat16 [16384, 768], P(('rep', 'shard')), may hold values from -6 to 6
- char_ids: int32 [16384, 5], P(('rep', 'shard')), may hold values from 0 to 1023
- char_counts: int32 [16384], P(('rep', 'shard')), may hold values from 2 to 5
- segments: int32 [16384], P('rep'), may hold values from 0 to 63, never falling along the last dimension, each value on 1 to 512 neighbouring positions
- token_cot: bfloat16 [16384, 768], P(('rep', 'shard')), may hold values from -6 to 6
- char_cot: bfloat16 [16384, 768], P(('rep', 'shard')), may hold values from -6 to 6
- query_proj: float32 [768, 768], P('shard'), may hold values from -0.21875 to 0.21875
- key_proj: float32 [768, 768], P('shard'), may hold values from -0.21875 to 0.21875
- value_proj: float32 [768, 768], P('shard'), may hold values from -0.21875 to 0.21875
- output_proj: float32 [768, 768], P('shard'), may hold values from -1.75 to 1.75
- query_bias: float32 [768], P('shard'), may hold values from -1.2 to 1.2
- value_bias: float32 [768], P('shard'), may hold values from -1.2 to 1.2
- output_bias: float32 [768], P('shard'), may hold values from -1.2 to 1.2
- first_gain: float32 [768], P('shard'), may hold values from 0.5 to 1.5
- first_shift: float32 [768], P('shard'), may hold values from -1.2 to 1.2
- expand_proj: float32 [768, 3072], P('shard'), may hold values from -0.21875 to 0.21875
- expand_bias: float32 [3072], P('shard'), may hold values from -1.2 to 1.2
- shrink_proj: float32 [3072, 768], P('shard'), may hold values from -0.109375 to 0.109375
- shrink_bias: float32 [768], P('shard'), may hold values from -1.2 to 1.2
- char_table: float32 [1024, 256], P('shard'), may hold values from -6 to 6
- gate_input: float32 [2, 256, 1152], P(None, 'shard'), may hold values from -0.375 to 0.375
- input_bias: float32 [2, 1152], P(None, 'shard'), may hold values from -1.2 to 1.2
- gate_recur: float32 [2, 384, 1152], P(None, 'shard'), may hold values from -0.3125 to 0.3125
- recur_bias: float32 [2, 1152], P(None, 'shard'), may hold values from -1.2 to 1.2
- token_proj: float32 [768, 768], P('shard'), may hold values from -0.21875 to 0.21875
- token_bias: float32 [768], P('shard'), may hold values from -1.2 to 1.2
- char_proj: float32 [768, 768], P('shard'), may hold values from -0.21875 to 0.21875
- char_bias: float32 [768], P('shard'), may hold values from -1.2 to 1.2
- merging_kernel: float32 [3, 1536, 1536], P(None, 'shard'), may hold values from -0.09375 to 0.09375
- merging_bias: float32 [1536], P('shard'), may hold values from -1.2 to 1.2
- token_gain: float32 [768], P('shard'), may hold values from 0.5 to 1.5
- token_shift: float32 [768], P('shard'), may hold values from -1.2 to 1.2
- char_gain: float32 [768], P('shard'), may hold values from 0.5 to 1.5
- char_shift: float32 [768], P('shard'), may hold values from -1.2 to 1.2
Outputs:
- token_out: bfloat16 [16384, 768], P(('rep', 'shard'))
- char_out: bfloat16 [16384, 768], P(('rep', 'shard'))
- token_grad: float32 [16384, 768], P(('rep', 'shard'))
- char_grad: float32 [16384, 768], P(('rep', 'shard'))
- query_proj_grad: float32 [768, 768], P('shard')
- key_proj_grad: float32 [768, 768], P('shard')
- value_proj_grad: float32 [768, 768], P('shard')
- output_proj_grad: float32 [768, 768], P('shard')
- query_bias_grad: float32 [768], P('shard')
- value_bias_grad: float32 [768], P('shard')
- output_bias_grad: float32 [768], P('shard')
- first_gain_grad: float32 [768], P('shard')
- first_shift_grad: float32 [768], P('shard')
- expand_proj_grad: float32 [768, 3072], P('shard')
- expand_bias_grad: float32 [3072], P('shard')
- shrink_proj_grad: float32 [3072, 768], P('shard')
- shrink_bias_grad: float32 [768], P('shard')
- char_table_grad: float32 [1024, 256], P('shard')
- gate_input_grad: float32 [2, 256, 1152], P(None, 'shard')
- input_bias_grad: float32 [2, 1152], P(None, 'shard')
- gate_recur_grad: float32 [2, 384, 1152], P(None, 'shard')
- recur_bias_grad: float32 [2, 1152], P(None, 'shard')
- token_proj_grad: float32 [768, 768], P('shard')
- token_bias_grad: float32 [768], P('shard')
- char_proj_grad: float32 [768, 768], P('shard')
- char_bias_grad: float32 [768], P('shard')
- merging_kernel_grad: float32 [3, 1536, 1536], P(None, 'shard')
- merging_bias_grad: float32 [1536], P('shard')
- token_gain_grad: float32 [768], P('shard')
- token_shift_grad: float32 [768], P('shard')
- char_gain_grad: float32 [768], P('shard')
- char_shift_grad: float32 [768], P('shard')
Inputs may be any that keep to these rules, and one draw needn't show every extreme that they name: `char_ids`: slots at or beyond a token's count in char_counts are never read. `segments`: segment numbers never fall along the tokens.
All inputs are finite; a program needn't handle non-finite values.
Results may differ from a plain program's by a relative error of at most 0.017.
The roundings to bfloat16 on the way count: a program that leaves them out, or rounds other values in their place, can miss the bound.
Values may be sent and summed in bfloat16 or wider, within the bound.
No kernel may reach another device: no remote copies, remote signals or barrier semaphores. Data moves between devices by JAX's collectives and lax.ppermute only.
A program may use at most 640 MiB of HBM per device.

v0:
```python
import jax
import jax.numpy as jnp
from jax import lax
from jax.sharding import PartitionSpec as P

HEADS = 12
HEAD_DIM = 64


norm_eps = 1e-05
masked_score = -1000000000.0
exact_mode = lax.Precision.HIGHEST


def with_halo(value, sides, width):
    for axis, dim in sides:
        count, length = (lax.axis_size(axis), value.shape[dim])
        up = [(i, (i + 1) % count) for i in range(count - 1)]
        down = [(j, i) for i, j in up]
        last = lax.slice_in_dim(value, length - width, length, axis=dim)
        first = lax.slice_in_dim(value, 0, width, axis=dim)
        before = lax.ppermute(last, axis, up)
        after = lax.ppermute(first, axis, down)
        value = jnp.concatenate([before, value, after], axis=dim)
    return value


def layer_norm(values, gain, shift):
    centre = jnp.mean(values, axis=-1, keepdims=True)
    centred = values - centre
    spread = jnp.mean(centred * centred, axis=-1, keepdims=True)
    return centred * lax.rsqrt(spread + norm_eps) * gain + shift


def gelu_exact(values):
    return jax.nn.gelu(values, approximate=False)


def matmul(left, right):
    return jnp.dot(left, right, preferred_element_type=jnp.float32)


def widen(values):
    return values.astype(jnp.float32)


def gates(step_in, recur):
    width = recur.shape[-1] // 3
    reset = jax.nn.sigmoid(step_in[..., :width] + recur[..., :width])
    update = jax.nn.sigmoid(step_in[..., width : 2 * width] + recur[..., width : 2 * width])
    candidate = jnp.tanh(step_in[..., 2 * width :] + reset * recur[..., 2 * width :])
    return (reset, update, candidate)


def letter_steps(ext_inputs, ext_counts, rows, slots):
    order = jnp.arange(slots)
    ahead = jnp.concatenate([ext_inputs[0, :rows], ext_inputs[0, 1 : rows + 1]], axis=1)
    behind = jnp.concatenate([ext_inputs[1, 2:, ::-1], ext_inputs[1, 1 : rows + 1, ::-1]], axis=1)
    step_in = jnp.stack([ahead, behind]).transpose(2, 0, 1, 3)
    ahead_mask = jnp.concatenate(
        [order[None, :] < ext_counts[:rows, None], order[None, :] < ext_counts[1 : rows + 1, None]],
        axis=1,
    )
    reverse_order = order[::-1]
    behind_mask = jnp.concatenate(
        [
            reverse_order[None, :] < ext_counts[2:, None],
            reverse_order[None, :] < ext_counts[1 : rows + 1, None],
        ],
        axis=1,
    )
    step_mask = jnp.stack([ahead_mask, behind_mask]).astype(jnp.float32).transpose(2, 0, 1)
    return (step_in, step_mask)


def restarts(keep_ahead, keep_behind, slots):
    ones = jnp.ones((2 * slots, 2, keep_ahead.shape[0]), jnp.float32)
    return ones.at[slots].set(jnp.stack([keep_ahead, keep_behind]))


def shards(
    token_in,
    char_in,
    char_ids,
    char_counts,
    segments,
    token_cot,
    char_cot,
    query_proj,
    key_proj,
    value_proj,
    output_proj,
    query_bias,
    value_bias,
    output_bias,
    first_gain,
    first_shift,
    expand_proj,
    expand_bias,
    shrink_proj,
    shrink_bias,
    char_table,
    gate_input,
    input_bias,
    gate_recur,
    recur_bias,
    token_proj,
    token_bias,
    char_proj,
    char_bias,
    merging_kernel,
    merging_bias,
    token_gain,
    token_shift,
    char_gain,
    char_shift,
):
    masters = (
        query_proj,
        key_proj,
        value_proj,
        output_proj,
        query_bias,
        value_bias,
        output_bias,
        first_gain,
        first_shift,
        expand_proj,
        expand_bias,
        shrink_proj,
        shrink_bias,
        char_table,
        gate_input,
        input_bias,
        gate_recur,
        recur_bias,
        token_proj,
        token_bias,
        char_proj,
        char_bias,
        merging_kernel,
        merging_bias,
        token_gain,
        token_shift,
        char_gain,
        char_shift,
    )
    lowered = [item.astype(jnp.bfloat16) for item in masters]
    weights = (
        lax.all_gather(lowered[0], "shard", axis=0, tiled=True),
        lax.all_gather(lowered[1], "shard", axis=0, tiled=True),
        lax.all_gather(lowered[2], "shard", axis=0, tiled=True),
        lax.all_gather(lowered[3], "shard", axis=0, tiled=True),
        lax.all_gather(lowered[4], "shard", axis=0, tiled=True),
        lax.all_gather(lowered[5], "shard", axis=0, tiled=True),
        lax.all_gather(lowered[6], "shard", axis=0, tiled=True),
        lax.all_gather(lowered[7], "shard", axis=0, tiled=True),
        lax.all_gather(lowered[8], "shard", axis=0, tiled=True),
        lax.all_gather(lowered[9], "shard", axis=0, tiled=True),
        lax.all_gather(lowered[10], "shard", axis=0, tiled=True),
        lax.all_gather(lowered[11], "shard", axis=0, tiled=True),
        lax.all_gather(lowered[12], "shard", axis=0, tiled=True),
        lax.all_gather(lowered[13], "shard", axis=0, tiled=True),
        lax.all_gather(lowered[14], "shard", axis=1, tiled=True),
        lax.all_gather(lowered[15], "shard", axis=1, tiled=True),
        lax.all_gather(lowered[16], "shard", axis=1, tiled=True),
        lax.all_gather(lowered[17], "shard", axis=1, tiled=True),
        lax.all_gather(lowered[18], "shard", axis=0, tiled=True),
        lax.all_gather(lowered[19], "shard", axis=0, tiled=True),
        lax.all_gather(lowered[20], "shard", axis=0, tiled=True),
        lax.all_gather(lowered[21], "shard", axis=0, tiled=True),
        lax.all_gather(lowered[22], "shard", axis=1, tiled=True),
        lax.all_gather(lowered[23], "shard", axis=0, tiled=True),
        lax.all_gather(lowered[24], "shard", axis=0, tiled=True),
        lax.all_gather(lowered[25], "shard", axis=0, tiled=True),
        lax.all_gather(lowered[26], "shard", axis=0, tiled=True),
        lax.all_gather(lowered[27], "shard", axis=0, tiled=True),
    )
    (
        query_low,
        key_low,
        value_low,
        output_low,
        bias_query,
        bias_value,
        bias_output,
        gain_first,
        shift_first,
        expand_low,
        bias_expand,
        shrink_low,
        bias_shrink,
        table_low,
        input_low,
        bias_input,
        recur_low,
        bias_recur,
        project_token,
        bias_token,
        project_char,
        bias_char,
        kernel_low,
        bias_merging,
        gain_token,
        shift_token,
        gain_char,
        shift_char,
    ) = weights
    rows = token_in.shape[0]
    width = token_in.shape[1]
    place = lax.axis_index("shard")
    parts = lax.axis_size("shard")
    length = rows * parts
    scale = HEAD_DIM ** (-0.5)
    seg_rows = lax.dynamic_slice_in_dim(segments, place * rows, rows)
    allowed = seg_rows[:, None] == segments[None, :]
    queries = (matmul(token_in, query_low) + widen(bias_query)).astype(jnp.bfloat16)
    keys = matmul(token_in, key_low).astype(jnp.bfloat16)
    values = (matmul(token_in, value_low) + widen(bias_value)).astype(jnp.bfloat16)
    everyone = lax.all_gather(jnp.concatenate([keys, values], axis=1), "shard", axis=0, tiled=True)
    head_q = queries.reshape(rows, HEADS, HEAD_DIM).transpose(1, 0, 2)
    head_k = everyone[:, :width].reshape(length, HEADS, HEAD_DIM).transpose(1, 0, 2)
    head_v = everyone[:, width:].reshape(length, HEADS, HEAD_DIM).transpose(1, 0, 2)

    def attend(item):
        one_q, one_k, one_v = item
        scores = jnp.where(
            allowed,
            jnp.einsum("rd,ld->rl", one_q, one_k, preferred_element_type=jnp.float32) * scale,
            masked_score,
        )
        top = jnp.max(scores, axis=1, keepdims=True)
        expo = jnp.exp(scores - top)
        total = jnp.sum(expo, axis=1, keepdims=True)
        probs = (expo / total).astype(jnp.bfloat16)
        return (matmul(probs, one_v), (top + jnp.log(total))[:, 0])

    mixed_heads, logsum = lax.map(attend, (head_q, head_k, head_v))
    mixed = mixed_heads.transpose(1, 0, 2).reshape(rows, width).astype(jnp.bfloat16)
    attn = matmul(mixed, output_low) + widen(bias_output)
    first_in = widen(token_in) + attn
    first = layer_norm(first_in, widen(gain_first), widen(shift_first))
    first_low = first.astype(jnp.bfloat16)
    up = matmul(first_low, expand_low) + widen(bias_expand)
    hidden = gelu_exact(up).astype(jnp.bfloat16)
    token_mid = first + matmul(hidden, shrink_low) + widen(bias_shrink)
    mid_low = token_mid.astype(jnp.bfloat16)
    slots = char_ids.shape[1]
    packed = jnp.concatenate([char_ids, char_counts[:, None]], axis=1)
    packed_ext = with_halo(packed, (("shard", 0),), 1)
    ids_ext = packed_ext[:, :slots]
    counts_ext = packed_ext[:, slots]
    vocab = table_low.shape[0]
    onehot = (ids_ext.reshape(-1)[:, None] == jnp.arange(vocab)[None, :]).astype(jnp.bfloat16)
    embedded = matmul(onehot, table_low).astype(jnp.bfloat16)
    inputs = (
        jnp.einsum("nc,dcg->dng", embedded, input_low, preferred_element_type=jnp.float32)
        + widen(bias_input)[:, None, :]
    )
    gate_width = inputs.shape[-1]
    inputs = inputs.reshape(2, rows + 2, slots, gate_width)
    step_in, step_mask = letter_steps(inputs, counts_ext, rows, slots)
    position = place * rows + jnp.arange(rows)
    before = jnp.take(segments, jnp.maximum(position - 1, 0))
    after = jnp.take(segments, jnp.minimum(position + 1, length - 1))
    keep_ahead = ((position > 0) & (before == seg_rows)).astype(jnp.float32)
    keep_behind = ((position < length - 1) & (after == seg_rows)).astype(jnp.float32)
    restart = restarts(keep_ahead, keep_behind, slots)
    hidden_size = gate_width // 3

    def cell(state, item):
        one_in, one_mask, one_restart = item
        start = state * one_restart[..., None]
        recur = (
            jnp.einsum(
                "drh,dhg->drg",
                start.astype(jnp.bfloat16),
                recur_low,
                preferred_element_type=jnp.float32,
            )
            + widen(bias_recur)[:, None, :]
        )
        reset, update, candidate = gates(one_in, recur)
        fresh = (1.0 - update) * candidate + update * start
        mask = one_mask[..., None]
        return (mask * fresh + (1.0 - mask) * start, (start, recur))

    final_state, (starts, recurs) = lax.scan(
        cell, jnp.zeros((2, rows, hidden_size), jnp.float32), (step_in, step_mask, restart)
    )
    pooled_low = jnp.concatenate([final_state[0], final_state[1]], axis=1).astype(jnp.bfloat16)
    tok_side = matmul(mid_low, project_token) + widen(bias_token)
    char_side = matmul(pooled_low, project_char) + widen(bias_char)
    joined = jnp.concatenate([tok_side, char_side], axis=1).astype(jnp.bfloat16)
    joined_ext = with_halo(joined, (("shard", 0),), 1)
    merged = (
        widen(bias_merging)
        + matmul(joined_ext[0:rows], kernel_low[0])
        + matmul(joined_ext[1 : rows + 1], kernel_low[1])
        + matmul(joined_ext[2 : rows + 2], kernel_low[2])
    )
    act = gelu_exact(merged)
    tok_pre = token_mid + act[:, :width]
    char_pre = widen(char_in) + act[:, width:]
    token_out = layer_norm(tok_pre, widen(gain_token), widen(shift_token)).astype(jnp.bfloat16)
    char_out = layer_norm(char_pre, widen(gain_char), widen(shift_char)).astype(jnp.bfloat16)
    (
        query_low,
        key_low,
        value_low,
        output_low,
        bias_query,
        bias_value,
        bias_output,
        gain_first,
        shift_first,
        expand_low,
        bias_expand,
        shrink_low,
        bias_shrink,
        table_low,
        input_low,
        bias_input,
        recur_low,
        bias_recur,
        project_token,
        bias_token,
        project_char,
        bias_char,
        kernel_low,
        bias_merging,
        gain_token,
        shift_token,
        gain_char,
        shift_char,
    ) = weights
    _, token_pull = jax.vjp(layer_norm, tok_pre, widen(gain_token), widen(shift_token))
    tok_pre_grad, token_gain_grad, token_shift_grad = token_pull(widen(token_cot))
    _, char_pull = jax.vjp(layer_norm, char_pre, widen(gain_char), widen(shift_char))
    char_grad, char_gain_grad, char_shift_grad = char_pull(widen(char_cot))
    _, gelu_pull = jax.vjp(gelu_exact, merged)
    merged_grad = gelu_pull(jnp.concatenate([tok_pre_grad, char_grad], axis=1))[0].astype(
        jnp.bfloat16
    )
    merging_bias_grad = jnp.sum(widen(merged_grad), axis=0)
    merging_kernel_grad = jnp.stack(
        [
            jnp.einsum(
                "rc,rg->cg",
                joined_ext[tap : tap + rows],
                merged_grad,
                preferred_element_type=jnp.float32,
            )
            for tap in range(3)
        ]
    )
    merged_ext = with_halo(merged_grad, (("shard", 0),), 1)
    joined_grad = (
        jnp.einsum(
            "rg,cg->rc", merged_ext[2 : rows + 2], kernel_low[0], preferred_element_type=jnp.float32
        )
        + jnp.einsum(
            "rg,cg->rc", merged_ext[1 : rows + 1], kernel_low[1], preferred_element_type=jnp.float32
        )
        + jnp.einsum(
            "rg,cg->rc", merged_ext[0:rows], kernel_low[2], preferred_element_type=jnp.float32
        )
    )
    tok_side_grad = joined_grad[:, :width].astype(jnp.bfloat16)
    char_side_grad = joined_grad[:, width:].astype(jnp.bfloat16)
    token_bias_grad = jnp.sum(widen(tok_side_grad), axis=0)
    token_proj_grad = jnp.einsum(
        "rc,rg->cg", mid_low, tok_side_grad, preferred_element_type=jnp.float32
    )
    char_bias_grad = jnp.sum(widen(char_side_grad), axis=0)
    char_proj_grad = jnp.einsum(
        "rc,rg->cg", pooled_low, char_side_grad, preferred_element_type=jnp.float32
    )
    pooled_grad = jnp.einsum(
        "rg,cg->rc", char_side_grad, project_char, preferred_element_type=jnp.float32
    )
    mid_grad = tok_pre_grad + jnp.einsum(
        "rg,cg->rc", tok_side_grad, project_token, preferred_element_type=jnp.float32
    )
    shrink_out_grad = mid_grad.astype(jnp.bfloat16)
    shrink_bias_grad = jnp.sum(widen(shrink_out_grad), axis=0)
    shrink_proj_grad = jnp.einsum(
        "rf,rc->fc", hidden, shrink_out_grad, preferred_element_type=jnp.float32
    )
    hidden_grad = jnp.einsum(
        "rc,fc->rf", shrink_out_grad, shrink_low, preferred_element_type=jnp.float32
    )
    _, up_pull = jax.vjp(gelu_exact, up)
    up_grad = up_pull(hidden_grad)[0].astype(jnp.bfloat16)
    expand_bias_grad = jnp.sum(widen(up_grad), axis=0)
    expand_proj_grad = jnp.einsum(
        "rc,rf->cf", first_low, up_grad, preferred_element_type=jnp.float32
    )
    first_grad = mid_grad + jnp.einsum(
        "rf,cf->rc", up_grad, expand_low, preferred_element_type=jnp.float32
    )
    early = (
        expand_proj_grad,
        expand_bias_grad,
        shrink_proj_grad,
        shrink_bias_grad,
        token_proj_grad,
        token_bias_grad,
        char_proj_grad,
        char_bias_grad,
        merging_kernel_grad,
        merging_bias_grad,
        token_gain_grad,
        token_shift_grad,
        char_gain_grad,
        char_shift_grad,
    )
    _, first_pull = jax.vjp(layer_norm, first_in, widen(gain_first), widen(shift_first))
    first_in_grad, first_gain_grad, first_shift_grad = first_pull(first_grad)
    attn_grad = first_in_grad.astype(jnp.bfloat16)
    output_bias_grad = jnp.sum(widen(attn_grad), axis=0)
    output_proj_grad = jnp.einsum("rc,rg->cg", mixed, attn_grad, preferred_element_type=jnp.float32)
    mixed_grad = jnp.einsum(
        "rg,cg->rc", attn_grad, output_low, preferred_element_type=jnp.float32
    ).astype(jnp.bfloat16)
    head_grad = mixed_grad.reshape(rows, HEADS, HEAD_DIM).transpose(1, 0, 2)

    def attend_back(item):
        one_q, one_k, one_v, one_d, one_lse = item
        scores = jnp.where(
            allowed,
            jnp.einsum("rd,ld->rl", one_q, one_k, preferred_element_type=jnp.float32) * scale,
            masked_score,
        )
        probs = jnp.exp(scores - one_lse[:, None])
        probs_grad = jnp.einsum("rd,ld->rl", one_d, one_v, preferred_element_type=jnp.float32)
        delta = jnp.sum(probs * probs_grad, axis=1, keepdims=True)
        scores_grad = (probs * (probs_grad - delta)).astype(jnp.bfloat16)
        query_part = matmul(scores_grad, one_k) * scale
        key_part = (
            jnp.einsum("rl,rd->ld", scores_grad, one_q, preferred_element_type=jnp.float32) * scale
        )
        value_part = jnp.einsum(
            "rl,rd->ld", probs.astype(jnp.bfloat16), one_d, preferred_element_type=jnp.float32
        )
        return (query_part, key_part, value_part)

    query_heads, key_heads, value_heads = lax.map(
        attend_back, (head_q, head_k, head_v, head_grad, logsum)
    )
    queries_grad = query_heads.transpose(1, 0, 2).reshape(rows, width).astype(jnp.bfloat16)
    kv_terms = jnp.concatenate(
        [
            key_heads.transpose(1, 0, 2).reshape(length, width),
            value_heads.transpose(1, 0, 2).reshape(length, width),
        ],
        axis=1,
    )
    kv_owned = lax.psum_scatter(kv_terms, "shard", scatter_dimension=0, tiled=True).astype(
        jnp.bfloat16
    )
    keys_grad = kv_owned[:, :width]
    values_grad = kv_owned[:, width:]
    query_bias_grad = jnp.sum(widen(queries_grad), axis=0)
    value_bias_grad = jnp.sum(widen(values_grad), axis=0)
    query_proj_grad = jnp.einsum(
        "rc,rg->cg", token_in, queries_grad, preferred_element_type=jnp.float32
    )
    key_proj_grad = jnp.einsum("rc,rg->cg", token_in, keys_grad, preferred_element_type=jnp.float32)
    value_proj_grad = jnp.einsum(
        "rc,rg->cg", token_in, values_grad, preferred_element_type=jnp.float32
    )
    token_grad = (
        first_in_grad
        + jnp.einsum("rg,cg->rc", queries_grad, query_low, preferred_element_type=jnp.float32)
        + jnp.einsum("rg,cg->rc", keys_grad, key_low, preferred_element_type=jnp.float32)
        + jnp.einsum("rg,cg->rc", values_grad, value_low, preferred_element_type=jnp.float32)
    )

    def cell_back(state_grad, item):
        one_in, one_mask, one_restart, start, recur = item
        reset, update, candidate = gates(one_in, recur)
        mask = one_mask[..., None]
        fresh_grad = mask * state_grad
        start_grad = (1.0 - mask) * state_grad + update * fresh_grad
        update_pre = fresh_grad * (start - candidate) * update * (1.0 - update)
        cand_pre = fresh_grad * (1.0 - update) * (1.0 - candidate * candidate)
        reset_pre = cand_pre * recur[..., 2 * hidden_size :] * reset * (1.0 - reset)
        input_part = jnp.concatenate([reset_pre, update_pre, cand_pre], axis=-1)
        recur_part = jnp.concatenate([reset_pre, update_pre, cand_pre * reset], axis=-1).astype(
            jnp.bfloat16
        )
        start_grad = start_grad + jnp.einsum(
            "drg,dhg->drh", recur_part, recur_low, preferred_element_type=jnp.float32
        )
        return (start_grad * one_restart[..., None], (input_part, recur_part))

    final_grad = jnp.stack([pooled_grad[:, :hidden_size], pooled_grad[:, hidden_size:]])
    _, (step_grads, recur_grads) = lax.scan(
        cell_back, final_grad, (step_in, step_mask, restart, starts, recurs), reverse=True
    )
    gate_recur_grad = jnp.einsum(
        "tdrh,tdrg->dhg",
        starts.astype(jnp.bfloat16),
        recur_grads,
        preferred_element_type=jnp.float32,
    )
    recur_bias_grad = jnp.sum(widen(recur_grads), axis=(0, 2))
    ahead_grad = step_grads[:, 0].transpose(1, 0, 2)
    behind_grad = step_grads[:, 1].transpose(1, 0, 2)
    ahead_ext = jnp.pad(ahead_grad[:, :slots], ((0, 2), (0, 0), (0, 0))) + jnp.pad(
        ahead_grad[:, slots:], ((1, 1), (0, 0), (0, 0))
    )
    behind_ext = jnp.pad(behind_grad[:, :slots][:, ::-1], ((2, 0), (0, 0), (0, 0))) + jnp.pad(
        behind_grad[:, slots:][:, ::-1], ((1, 1), (0, 0), (0, 0))
    )
    rims = jnp.stack([ahead_ext[0], behind_ext[rows + 1]])
    returned = with_halo(rims, (("shard", 0),), 1)
    ahead_own = ahead_ext[1 : rows + 1].at[rows - 1].add(returned[3])
    behind_own = behind_ext[1 : rows + 1].at[0].add(returned[0])
    inputs_grad = jnp.stack([ahead_own, behind_own]).astype(jnp.bfloat16)
    input_bias_grad = jnp.sum(widen(inputs_grad), axis=(1, 2))
    flat_grad = inputs_grad.reshape(2, rows * slots, gate_width)
    own_embedded = embedded.reshape(rows + 2, slots, -1)[1 : rows + 1].reshape(rows * slots, -1)
    gate_input_grad = jnp.einsum(
        "nc,dng->dcg", own_embedded, flat_grad, preferred_element_type=jnp.float32
    )
    embedded_grad = jnp.einsum(
        "dng,dcg->nc", flat_grad, input_low, preferred_element_type=jnp.float32
    )
    own_onehot = widen(
        onehot.reshape(rows + 2, slots, vocab)[1 : rows + 1].reshape(rows * slots, vocab)
    )
    char_table_grad = jnp.einsum("nv,nc->vc", own_onehot, embedded_grad, precision=exact_mode)
    late = (
        query_proj_grad,
        key_proj_grad,
        value_proj_grad,
        output_proj_grad,
        query_bias_grad,
        value_bias_grad,
        output_bias_grad,
        first_gain_grad,
        first_shift_grad,
        char_table_grad,
        gate_input_grad,
        input_bias_grad,
        gate_recur_grad,
        recur_bias_grad,
    )
    owned = (
        lax.psum_scatter(late[0], "shard", scatter_dimension=0, tiled=True),
        lax.psum_scatter(late[1], "shard", scatter_dimension=0, tiled=True),
        lax.psum_scatter(late[2], "shard", scatter_dimension=0, tiled=True),
        lax.psum_scatter(late[3], "shard", scatter_dimension=0, tiled=True),
        lax.psum_scatter(late[4], "shard", scatter_dimension=0, tiled=True),
        lax.psum_scatter(late[5], "shard", scatter_dimension=0, tiled=True),
        lax.psum_scatter(late[6], "shard", scatter_dimension=0, tiled=True),
        lax.psum_scatter(late[7], "shard", scatter_dimension=0, tiled=True),
        lax.psum_scatter(late[8], "shard", scatter_dimension=0, tiled=True),
        lax.psum_scatter(early[0], "shard", scatter_dimension=0, tiled=True),
        lax.psum_scatter(early[1], "shard", scatter_dimension=0, tiled=True),
        lax.psum_scatter(early[2], "shard", scatter_dimension=0, tiled=True),
        lax.psum_scatter(early[3], "shard", scatter_dimension=0, tiled=True),
        lax.psum_scatter(late[9], "shard", scatter_dimension=0, tiled=True),
        lax.psum_scatter(late[10], "shard", scatter_dimension=1, tiled=True),
        lax.psum_scatter(late[11], "shard", scatter_dimension=1, tiled=True),
        lax.psum_scatter(late[12], "shard", scatter_dimension=1, tiled=True),
        lax.psum_scatter(late[13], "shard", scatter_dimension=1, tiled=True),
        lax.psum_scatter(early[4], "shard", scatter_dimension=0, tiled=True),
        lax.psum_scatter(early[5], "shard", scatter_dimension=0, tiled=True),
        lax.psum_scatter(early[6], "shard", scatter_dimension=0, tiled=True),
        lax.psum_scatter(early[7], "shard", scatter_dimension=0, tiled=True),
        lax.psum_scatter(early[8], "shard", scatter_dimension=1, tiled=True),
        lax.psum_scatter(early[9], "shard", scatter_dimension=0, tiled=True),
        lax.psum_scatter(early[10], "shard", scatter_dimension=0, tiled=True),
        lax.psum_scatter(early[11], "shard", scatter_dimension=0, tiled=True),
        lax.psum_scatter(early[12], "shard", scatter_dimension=0, tiled=True),
        lax.psum_scatter(early[13], "shard", scatter_dimension=0, tiled=True),
    )
    final = lax.psum(
        (
            owned[0],
            owned[1],
            owned[2],
            owned[3],
            owned[4],
            owned[5],
            owned[6],
            owned[7],
            owned[8],
            owned[9],
            owned[10],
            owned[11],
            owned[12],
            owned[13],
            owned[14],
            owned[15],
            owned[16],
            owned[17],
            owned[18],
            owned[19],
            owned[20],
            owned[21],
            owned[22],
            owned[23],
            owned[24],
            owned[25],
            owned[26],
            owned[27],
        ),
        "rep",
    )
    return (token_out, char_out, token_grad, char_grad) + tuple(final)


def solution(mesh):
    in_specs = (
        P(("rep", "shard"), None),
        P(("rep", "shard"), None),
        P(("rep", "shard"), None),
        P(("rep", "shard")),
        P("rep"),
        P(("rep", "shard"), None),
        P(("rep", "shard"), None),
        P("shard", None),
        P("shard", None),
        P("shard", None),
        P("shard", None),
        P("shard"),
        P("shard"),
        P("shard"),
        P("shard"),
        P("shard"),
        P("shard", None),
        P("shard"),
        P("shard", None),
        P("shard"),
        P("shard", None),
        P(None, "shard", None),
        P(None, "shard"),
        P(None, "shard", None),
        P(None, "shard"),
        P("shard", None),
        P("shard"),
        P("shard", None),
        P("shard"),
        P(None, "shard", None),
        P("shard"),
        P("shard"),
        P("shard"),
        P("shard"),
        P("shard"),
    )
    out_specs = (
        P(("rep", "shard"), None),
        P(("rep", "shard"), None),
        P(("rep", "shard"), None),
        P(("rep", "shard"), None),
        P("shard", None),
        P("shard", None),
        P("shard", None),
        P("shard", None),
        P("shard"),
        P("shard"),
        P("shard"),
        P("shard"),
        P("shard"),
        P("shard", None),
        P("shard"),
        P("shard", None),
        P("shard"),
        P("shard", None),
        P(None, "shard", None),
        P(None, "shard"),
        P(None, "shard", None),
        P(None, "shard"),
        P("shard", None),
        P("shard"),
        P("shard", None),
        P("shard"),
        P(None, "shard", None),
        P("shard"),
        P("shard"),
        P("shard"),
        P("shard"),
        P("shard"),
    )
    return jax.shard_map(shards, mesh=mesh, in_specs=in_specs, out_specs=out_specs, check_vma=False)
```

profile of v0, /device:TPU:17, one launch (start us, length us, event | category | flops | bytes accessed | tf_op | source)
XLA Modules:
  0.0 2794.6 jit_solution(18263240684463961321)
XLA Ops:
  21.7 12.4 all-gather.31.cloned.1.call-done
  36.1 22.9 all-gather.33.cloned.1.call-done
  95.5 14.0 all_gather.104
  174.5 12.5 add_bitcast_fusion
  187.0 43.0 %copy.296 = f32[2,2570,1152]{2,0,1:T(2,128)} copy(f32[2,2570,1152]{2,1,0:T(8,128)} %add_bitcast_fusion) | data formatting | bytes 47370240 | tf_op jit(solution)/shard_map/add | solution.py:257
  230.0 49.6 %fusion.184 = (f32[1,512,5,1152]{3,0,2,1:T(1,128)}, f32[1,512,5,1152]{3,0,2,1:T(1,128)}, f32[1,512,5,1152]{3,0,2,1:T(1,128)}, f32[1,512,5,1152]{3,0,2,1:T(1,128)}) fusion(f32[2,514,5,1152]{3,0,2,1:T(2,128)} %bitcast.350), kind=kLoop, calls=%fused_computation.379 | loop fusion | bytes 94371840 | tf_op jit(solution)/shard_map/slice | solution.py:57
  279.6 10.6 rev.17
  290.3 9.4 copy.334
  299.7 10.7 rev.16
  310.3 10.6 copy.335
  320.9 10.1 copy.336
  340.4 19.3 maximum_bitcast_fusion.3
  372.1 33.4 %maximum_bitcast_fusion.1 = f32[10,2,512,1152]{3,2,0,1:T(8,128)} fusion(f32[1,512,10,1152]{3,1,2,0:T(8,128)} %maximum_bitcast_fusion.3, f32[1,512,10,1152]{3,1,2,0:T(8,128)} %maximum_bitcast_fusion.2), kind=kLoop, calls=%fused_computation.117 | loop fusion | flops 11796480 | bytes 94371840 | tf_op jit(solution)/shard_map/transpose | solution.py:59
  405.4 36.0 %copy.303 = f32[10,2,512,1152]{3,2,1,0:T(8,128)} copy(f32[10,2,512,1152]{3,2,0,1:T(8,128)} %maximum_bitcast_fusion.1) | data formatting | bytes 94371840
  445.3 15.6 broadcast.470.clone
  460.9 105.4 %while.67 = (s32[]{:T(128)}, f32[2,512,384]{2,1,0:T(8,128)S(1)}, f32[10,2,512,384]{3,2,1,0:T(8,128)}, f32[10,2,512,1152]{3,2,1,0:T(8,128)}, f32[10,2,512]{2,1,0:...) while((s32[]{:T(128)}, f32[2,512,384]{2,1,0:T(8,128)S(1)}, ...), condition=%wide.region_7.9_spmd.clone, body=%wide.region_6.8_spmd.clone.sunk | while | flops 916589824 | bytes 38009492 | solution.py:288
  585.6 66.2 %while.65 = (s32[]{:T(128)}, bf16[12,512,64]{1,2,0:T(8,128)(2,1)}, f32[12,512]{1,0:T(8,128)}, bf16[12,512,64]{2,1,0:T(8,128)(2,1)}, bf16[12,1024,64]{2,1,0:T(8,1...) while((s32[]{:T(128)}, bf16[12,512,64]{1,2,0:T(8,128)(2,1)}, ...), condition=%wide.region_3.4_spmd.clone, body=%wide.region_0.3_spmd.clone.sunk | while | flops 138935808 | bytes 7106673 | solution.py:238
  656.0 21.0 multiply_convert_fusion.2
  704.5 11.0 multiply_multiply_fusion.10
  747.0 10.1 convert_reduce_fusion.2
  769.2 108.9 %while.66 = (s32[]{:T(128)}, bf16[12,512,64]{1,2,0:T(8,128)(2,1)}, f32[12,1024,64]{1,2,0:T(8,128)}, f32[12,1024,64]{1,2,0:T(8,128)}, bf16[12,512,64]{2,1,0:T(8,1...) while((s32[]{:T(128)}, bf16[12,512,64]{1,2,0:T(8,128)(2,1)}, ...), condition=%wide.region_20.22_spmd.clone, body=%wide.region_18.21_spmd.clone.sunk | while | flops 340884992 | bytes 17585280 | solution.py:448
  887.5 15.5 broadcast.470
  912.0 156.2 %while.64 = (s32[]{:T(128)}, f32[2,512,384]{2,1,0:T(8,128)S(1)}, f32[10,2,512,1152]{3,2,1,0:T(8,128)}, bf16[10,2,512,1152]{3,2,1,0:T(8,128)(2,1)}, f32[10,2,512]...) while((s32[]{:T(128)}, f32[2,512,384]{2,1,0:T(8,128)S(1)}, ...), condition=%wide.region_56.58_spmd, body=%wide.region_55.57_spmd.sunk | while | flops 940573696 | bytes 75735192 | solution.py:499
  1068.1 16.5 slice_bitcast_fusion
  1139.2 11.5 add_bitcast_fusion.2
  1170.1 10.2 copy.312
  1180.3 11.4 stack.85
  1194.4 10.2 copy.314
  1204.6 11.6 stack.88
  1229.6 9.6 fusion.82
  1252.5 9.4 convolution_bitcast_fusion.6
  1261.9 19.9 fusion.98
  1318.1 10.0 pad_maximum_fusion
  1328.1 9.9 convert_reduce_fusion
  1348.3 36.8 %reduce-scatter.40.cloned.1.call-done = f32[384,768]{1,0:T(8,128)} async-done(((f32[768,768]{1,0:T(8,128)}), f32[384,768]{1,0:T(8,128)}) %reduce-scatter.40.cloned.1.call-update) | async-done | bytes 1179664 | tf_op jit(solution)/shard_map/reduce_scatter | solution.py:570
  1385.2 36.9 %reduce-scatter.42.cloned.1.call-done = f32[384,768]{1,0:T(8,128)} async-done(((f32[768,768]{1,0:T(8,128)}), f32[384,768]{1,0:T(8,128)}) %reduce-scatter.42.cloned.1.call-update) | async-done | bytes 1179664 | tf_op jit(solution)/shard_map/reduce_scatter | solution.py:572
  1422.1 37.0 %reduce-scatter.36.cloned.1.call-done = f32[2,128,1152]{1,2,0:T(8,128)} async-done(((f32[2,256,1152]{1,2,0:T(8,128)}), f32[2,128,1152]{1,2,0:T(8,128)}) %reduce-scatter.36.cloned.1.call-update) | async-done | bytes 1179664 | tf_op jit(solution)/shard_map/reduce_scatter | solution.py:566
  1459.1 50.5 %reduce-scatter.38.cloned.1.call-done = f32[2,192,1152]{2,1,0:T(8,128)} async-done(((f32[2,384,1152]{2,1,0:T(8,128)}), f32[2,192,1152]{2,1,0:T(8,128)}) %reduce-scatter.38.cloned.1.call-update) | async-done | bytes 1769488 | tf_op jit(solution)/shard_map/reduce_scatter | solution.py:568
  1509.6 37.0 %reduce-scatter.24.cloned.1.call-done = f32[384,768]{0,1:T(8,128)} async-done(((f32[768,768]{0,1:T(8,128)}), f32[384,768]{0,1:T(8,128)}) %reduce-scatter.24.cloned.1.call-update) | async-done | bytes 1179664 | tf_op jit(solution)/shard_map/reduce_scatter | solution.py:553
  1546.6 37.1 %reduce-scatter.26.cloned.1.call-done = f32[384,768]{0,1:T(8,128)} async-done(((f32[768,768]{0,1:T(8,128)}), f32[384,768]{0,1:T(8,128)}) %reduce-scatter.26.cloned.1.call-update) | async-done | bytes 1179664 | tf_op jit(solution)/shard_map/reduce_scatter | solution.py:554
  1583.6 113.5 %reduce-scatter.30.cloned.1.call-done = f32[384,3072]{1,0:T(8,128)} async-done(((f32[768,3072]{1,0:T(8,128)}), f32[384,3072]{1,0:T(8,128)}) %reduce-scatter.30.cloned.1.call-update) | async-done | bytes 4718608 | tf_op jit(solution)/shard_map/reduce_scatter | solution.py:561
  1697.1 112.7 %reduce-scatter.32.cloned.1.call-done = f32[1536,768]{1,0:T(8,128)} async-done(((f32[3072,768]{1,0:T(8,128)}), f32[1536,768]{1,0:T(8,128)}) %reduce-scatter.32.cloned.1.call-update) | async-done | bytes 4718608 | tf_op jit(solution)/shard_map/reduce_scatter | solution.py:563
  1809.9 315.5 %reduce-scatter.44.cloned.1.call-done = f32[3,768,1536]{2,1,0:T(8,128)} async-done(((f32[3,1536,1536]{2,1,0:T(8,128)}), f32[3,768,1536]{2,1,0:T(8,128)}) %reduce-scatter.44.cloned.1.call-update) | async-done | bytes 14155792 | tf_op jit(solution)/shard_map/reduce_scatter | solution.py:574
  2133.7 9.6 reduce-scatter.48.cloned.1.call-done
  2144.5 16.9 reduce-scatter.46.cloned.1.call-done
  2169.9 50.2 %all-reduce.19 = (f32[384]{0:T(512)}, f32[384]{0:T(512)}, f32[384]{0:T(512)}, f32[384]{0:T(512)}, f32[384]{0:T(512)}, /*index=5*/f32[1536]{0:T(1024)}, f32[384]{...) all-reduce(f32[384]{0:T(512)S(1)} %dynamic-slice.22, ...), channel_id=1, replica_groups=mesh['rep'=16,'shard'=2] {'rep'}, use_global_device_ids=true, to_apply=%region_32.34 | all-reduce | flops 9216 | bytes 73728 | tf_op jit(solution)/shard_map/psum | solution.py:581
  2224.7 530.8 %all-reduce.24.cloned.1.call-done = (f32[384,768]{0,1:T(8,128)}, f32[384,768]{0,1:T(8,128)}, f32[384,768]{0,1:T(8,128)}, f32[384,768]{1,0:T(8,128)}, f32[384,307...) async-done(((f32[384,768]{0,1:T(8,128)}, ...) | async-done | bytes 34144272 | tf_op jit(solution)/shard_map/psum | solution.py:581
  2775.7 11.8 copy.414
  (900 shorter events, 881.2 us)
Async XLA Ops:
  7.2 26.9 all-gather.31.cloned.1.call-start
  9.5 49.5 %all-gather.33.cloned.1.call-start = ((), (), s32[]{:S(2)}) async-start(), calls=%async_computation.17 | async-start | bytes 1769472 | tf_op jit(solution)/shard_map/all_gather | solution.py:152
  10.5 164.0 %all-gather.45.cloned.1.call-start = ((), (), s32[]{:S(2)}) async-start(), calls=%async_computation.23 | async-start | bytes 1769472 | tf_op jit(solution)/shard_map/all_gather | solution.py:164
  12.8 428.6 %all-gather.29.cloned.1.call-start = ((), (), s32[]{:S(2)}) async-start(), calls=%async_computation.15 | async-start | bytes 1769472 | tf_op jit(solution)/shard_map/all_gather | solution.py:150
  15.1 430.2 %all-gather.47.cloned.1.call-start = ((), (), s32[]{:S(2)}) async-start(), calls=%async_computation.24 | async-start | bytes 2654208 | tf_op jit(solution)/shard_map/all_gather | solution.py:166
  16.2 550.4 %all-gather.49.cloned.1.call-start = ((), (), s32[]{:S(2)}) async-start(), calls=%async_computation.25 | async-start | bytes 1769472 | tf_op jit(solution)/shard_map/all_gather | solution.py:170
  18.4 551.6 %all-gather.35.cloned.1.call-start = ((), (), s32[]{:S(2)}) async-start(), calls=%async_computation.18 | async-start | bytes 4718592 | tf_op jit(solution)/shard_map/all_gather | solution.py:220
  62.4 589.4 %all-gather.37.cloned.1.call-start = ((), (), s32[]{:S(2)}) async-start(), calls=%async_computation.19 | async-start | bytes 1769472 | tf_op jit(solution)/shard_map/all_gather | solution.py:153
  63.8 592.2 %all-gather.39.cloned.1.call-start = ((), (), s32[]{:S(2)}) async-start(), calls=%async_computation.20 | async-start | bytes 7077888 | tf_op jit(solution)/shard_map/all_gather | solution.py:159
  67.9 609.1 %all-gather.41.cloned.1.call-start = ((), (), s32[]{:S(2)}) async-start(), calls=%async_computation.21 | async-start | bytes 7077888 | tf_op jit(solution)/shard_map/all_gather | solution.py:161
  72.2 612.4 %all-gather.43.cloned.1.call-start = ((), (), s32[]{:S(2)}) async-start(), calls=%async_computation.22 | async-start | bytes 1769472 | tf_op jit(solution)/shard_map/all_gather | solution.py:168
  74.4 618.4 %all-gather.51.cloned.1.call-start = ((), (), s32[]{:S(2)}) async-start(), calls=%async_computation.26 | async-start | bytes 21233664 | tf_op jit(solution)/shard_map/all_gather | solution.py:172
  74.5 92.4 %collective-permute-start = (s32[1,6]{0,1:T(8,128)S(1)}, s32[1,6]{0,1:T(8,128)S(1)}, u32[]{:S(2)}, u32[]{:S(2)}) collective-permute-start(s32[1,6]{0,1:T(8,128)S(1)} %get-tuple-element.1211), channel_id=1, source_target_pairs={{0,1},{2,3},{4,5},{6,7},{8,9},{10,11},{12,13},{14,15},{16,17},{18,... | collective-permute-start | bytes 80 | tf_op jit(solution)/shard_map/ppermute | solution.py:22
  76.7 90.2 %collective-permute-start.1 = (s32[1,6]{0,1:T(8,128)S(1)}, s32[1,6]{0,1:T(8,128)S(1)}, u32[]{:S(2)}, u32[]{:S(2)}) collective-permute-start(s32[1,6]{0,1:T(8,128)S(1)} %get-tuple-element.1212), channel_id=1, source_target_pairs={{1,0},{3,2},{5,4},{7,6},{9,8},{11,10},{13,12},{15,14},{17,16},{19,... | collective-permute-start | bytes 80 | tf_op jit(solution)/shard_map/ppermute | solution.py:23
  86.9 1195.0 %reduce-scatter.20.cloned.1.call-start = ((), (), s32[]{:S(2)}) async-start(), calls=%async_computation.27 | async-start | bytes 9437184 | tf_op jit(solution)/shard_map/reduce_scatter | solution.py:459
  95.5 47.6 %copy-start.105 = (f32[384]{0:T(512)S(1)}, f32[384]{0:T(512)}, u32[]{:S(2)}) copy-start(f32[384]{0:T(512)} %param.70) | copy-start | bytes 4612
  95.5 51.4 %copy-start.97 = (f32[768]{0:T(1024)S(1)}, f32[768]{0:T(1024)}, u32[]{:S(2)}) copy-start(f32[768]{0:T(1024)} %param.81) | copy-start | bytes 9220
  95.5 55.3 %copy-start.106 = (f32[384]{0:T(512)S(1)}, f32[384]{0:T(512)}, u32[]{:S(2)}) copy-start(f32[384]{0:T(512)} %param.82) | copy-start | bytes 4612
  95.5 59.1 %copy-start.107 = (f32[384]{0:T(512)S(1)}, f32[384]{0:T(512)}, u32[]{:S(2)}) copy-start(f32[384]{0:T(512)} %param.84) | copy-start | bytes 4612
  95.5 62.9 %copy-start.108 = (f32[384]{0:T(512)S(1)}, f32[384]{0:T(512)}, u32[]{:S(2)}) copy-start(f32[384]{0:T(512)} %param.83) | copy-start | bytes 4612
  95.5 67.2 %copy-start.109 = (f32[384]{0:T(512)S(1)}, f32[384]{0:T(512)}, u32[]{:S(2)}) copy-start(f32[384]{0:T(512)} %param.85) | copy-start | bytes 4612
  114.3 54.0 %copy-start.60 = (s32[512]{0:T(512)}, s32[512]{0:T(512)S(1)}, u32[]{:S(2)}) copy-start(s32[512]{0:T(512)S(1)} %get-tuple-element.1574) | copy-start | bytes 6148
  585.6 66.2 %copy-start.93 = (f32[768]{0:T(1024)S(1)}, f32[768]{0:T(1024)}, u32[]{:S(2)}) copy-start(f32[768]{0:T(1024)} %reshape.497) | copy-start | bytes 9220
  654.5 106.2 %copy-start.66 = (f32[512]{0:T(512)}, f32[512]{0:T(512)S(1)}, u32[]{:S(2)}) copy-start(f32[512]{0:T(512)S(1)} %broadcast_multiply_fusion.2) | copy-start | bytes 6148
  655.9 104.8 %copy-start.82 = (f32[512]{0:T(512)}, f32[512]{0:T(512)S(1)}, u32[]{:S(2)}) copy-start(f32[512]{0:T(512)S(1)} %fusion.149) | copy-start | bytes 6148
  688.1 10.7 collective-permute-start.2
  691.5 13.0 collective-permute-start.3
  726.6 9.6 collective-permute-start.5
  730.6 9.9 collective-permute-start.4
  884.8 461.9 %reduce-scatter.34.cloned.1.call-start = ((), (), s32[]{:S(2)}) async-start(), calls=%async_computation.34 | async-start | bytes 1572864 | tf_op jit(solution)/shard_map/reduce_scatter | solution.py:565
  1101.7 66.6 %collective-permute-start.6 = (f32[1,5,1152]{2,0,1:T(1,128)S(1)}, f32[1,5,1152]{2,0,1:T(1,128)S(1)}, u32[]{:S(2)}, u32[]{:S(2)}) collective-permute-start(f32[1,5,1152]{2,0,1:T(1,128)S(1)} %pad_add_fusion.1), channel_id=1, source_target_pairs={{1,0},{3,2},{5,4},{7,6},{9,8},{11,10},{13,12},{15,14},{17,16},{19,... | collective-permute-start | bytes 69128 | tf_op jit(solution)/shard_map/ppermute | solution.py:23
  1163.7 28.0 %collective-permute-start.7 = (f32[1,5,1152]{2,0,1:T(1,128)S(1)}, f32[1,5,1152]{2,0,1:T(1,128)S(1)}, u32[]{:S(2)}, u32[]{:S(2)}) collective-permute-start(f32[1,5,1152]{2,0,1:T(1,128)S(1)} %pad_add_fusion), channel_id=1, source_target_pairs={{0,1},{2,3},{4,5},{6,7},{8,9},{10,11},{12,13},{14,15},{16,17},{18,... | collective-permute-start | bytes 69128 | tf_op jit(solution)/shard_map/ppermute | solution.py:22
  1239.3 107.4 %reduce-scatter.22.cloned.1.call-start = ((), (), s32[]{:S(2)}) async-start(), calls=%async_computation.28 | async-start | bytes 3538944 | tf_op jit(solution)/shard_map/reduce_scatter | solution.py:552
  1241.6 106.8 %reduce-scatter.28.cloned.1.call-start = ((), (), s32[]{:S(2)}) async-start(), calls=%async_computation.31 | async-start | bytes 3538944 | tf_op jit(solution)/shard_map/reduce_scatter | solution.py:555
  1245.3 139.9 %reduce-scatter.40.cloned.1.call-start = ((), (), s32[]{:S(2)}) async-start(), calls=%async_computation.37 | async-start | bytes 3538944 | tf_op jit(solution)/shard_map/reduce_scatter | solution.py:570
  1249.1 173.0 %reduce-scatter.42.cloned.1.call-start = ((), (), s32[]{:S(2)}) async-start(), calls=%async_computation.38 | async-start | bytes 3538944 | tf_op jit(solution)/shard_map/reduce_scatter | solution.py:572
  1252.4 206.7 %reduce-scatter.36.cloned.1.call-start = ((), (), s32[]{:S(2)}) async-start(), calls=%async_computation.35 | async-start | bytes 3538944 | tf_op jit(solution)/shard_map/reduce_scatter | solution.py:566
  1261.9 247.7 %reduce-scatter.38.cloned.1.call-start = ((), (), s32[]{:S(2)}) async-start(), calls=%async_computation.36 | async-start | bytes 5308416 | tf_op jit(solution)/shard_map/reduce_scatter | solution.py:568
  1281.9 264.7 %reduce-scatter.24.cloned.1.call-start = ((), (), s32[]{:S(2)}) async-start(), calls=%async_computation.29 | async-start | bytes 3538944 | tf_op jit(solution)/shard_map/reduce_scatter | solution.py:553
  1286.8 296.8 %reduce-scatter.26.cloned.1.call-start = ((), (), s32[]{:S(2)}) async-start(), calls=%async_computation.30 | async-start | bytes 3538944 | tf_op jit(solution)/shard_map/reduce_scatter | solution.py:554
  1289.1 408.1 %reduce-scatter.30.cloned.1.call-start = ((), (), s32[]{:S(2)}) async-start(), calls=%async_computation.32 | async-start | bytes 14155776 | tf_op jit(solution)/shard_map/reduce_scatter | solution.py:561
  1298.2 511.7 %reduce-scatter.32.cloned.1.call-start = ((), (), s32[]{:S(2)}) async-start(), calls=%async_computation.33 | async-start | bytes 14155776 | tf_op jit(solution)/shard_map/reduce_scatter | solution.py:563
  1307.1 818.2 %reduce-scatter.44.cloned.1.call-start = ((), (), s32[]{:S(2)}) async-start(), calls=%async_computation.39 | async-start | bytes 42467328 | tf_op jit(solution)/shard_map/reduce_scatter | solution.py:574
  1328.1 815.2 %reduce-scatter.48.cloned.1.call-start = ((), (), s32[]{:S(2)}) async-start(), calls=%async_computation.41 | async-start | bytes 884736
  1339.1 822.3 %reduce-scatter.46.cloned.1.call-start = ((), (), s32[]{:S(2)}) async-start(), calls=%async_computation.40 | async-start | bytes 884736
  1346.6 1408.9 %all-reduce.24.cloned.1.call-start = ((), (), s32[]{:S(2)}) async-start(), calls=%async_computation.42 | async-start | bytes 68288512 | tf_op jit(solution)/shard_map/psum | solution.py:581
  2143.3 79.1 %copy-start.10 = (f32[512,768]{1,0:T(8,128)S(1)}, f32[512,768]{1,0:T(8,128)}, u32[]{:S(2)}) copy-start(f32[512,768]{1,0:T(8,128)} %copy-done.9) | copy-start | bytes 4718596
  2143.3 79.1 %copy-start.69 = (f32[512]{0:T(512)S(1)}, f32[512]{0:T(512)}, u32[]{:S(2)}) copy-start(f32[512]{0:T(512)} %copy-done.68) | copy-start | bytes 6148
  (123 other events, 1316.4 us)
Sparse Core Ops, SparseCore 0:
  10.2 23.8 all-gather.30
  36.2 22.7 all-gather.32
  61.1 22.8 all-gather.44
  86.0 28.4 all-gather.28
  116.4 29.6 all-gather.46
  148.1 22.9 all-gather.48
  173.1 44.9 all-gather.34
  220.2 22.7 all-gather.36
  245.2 62.6 all-gather.38
  309.3 62.6 all-gather.40
  374.1 22.7 all-gather.42
  398.3 169.3 all-gather.50
  884.9 93.5 reduce-scatter.19
  1239.4 35.1 reduce-scatter.33
  1276.7 34.7 reduce-scatter.21
  1313.6 34.6 reduce-scatter.27
  1350.4 34.7 reduce-scatter.39
  1387.4 34.6 reduce-scatter.41
  1424.3 34.7 reduce-scatter.35
  1461.9 47.6 reduce-scatter.37
  1511.8 34.7 reduce-scatter.23
  1548.9 34.6 reduce-scatter.25
  1586.5 110.5 reduce-scatter.29
  1699.3 110.5 reduce-scatter.31
  1812.2 313.1 reduce-scatter.43
  2128.0 15.2 reduce-scatter.47
  2146.1 15.2 reduce-scatter.45
  2167.8 587.5 all-reduce.23
where the time goes:
time: 2810 us; the launch traced here: 2790 us
  waiting for transfers between devices  1370 us (49%)
  local copies, waits for them, and re-layouts  556 us (20%)
  matrix products  402 us (14%)
  other arithmetic  301 us (11%)
  blocking collectives  124 us (4%)
    psum x1, waiting for transfers between devices, shards(): lax.psum((owned[0], owned[1], owned[2], owned[3], owned[4], owned[5], own...  531 us
    reduce_scatter x1, waiting for transfers between devices, shards(): lax.psum_scatter(early[8], 'shard', scatter_dimension=1, tiled=True)  315 us
    unnamed x322, local copies, waits for them, and re-layouts  120 us
    reduce_scatter x1, waiting for transfers between devices, shards(): lax.psum_scatter(early[0], 'shard', scatter_dimension=0, tiled=True)  113 us
    reduce_scatter x1, waiting for transfers between devices, shards(): lax.psum_scatter(early[2], 'shard', scatter_dimension=0, tiled=True)  113 us
    dot_general x36, matrix products, matmul(): return jnp.dot(left, right, preferred_element_type=jnp.float32)  106 us
    squeeze x20, local copies, waits for them, and re-layouts, shards(): lax.scan(cell, jnp.zeros((2, rows, hidden_size), jnp.float32), (step_in,...  71 us
    slice x2, local copies, waits for them, and re-layouts, letter_steps(): ext_inputs[0, :rows]  59 us
  transfers between devices with their start and end apart: 36, of which 15 were waited for; matrix products, arithmetic and copies ran while one was open for 37% of the time, Pallas kernels for 0%

commit v1 on v0

v1 whole, which is shorter than its diff:
```python
import functools
import jax
import jax.numpy as jnp
from jax import lax
from jax.sharding import PartitionSpec as P
from jax.experimental import pallas as pl
from jax.experimental.pallas import tpu as pltpu

F32 = jnp.float32
BF16 = jnp.bfloat16
VMEM_BYTES = 60 * 1024 * 1024


def dot(left, right):
    return jnp.dot(left, right, preferred_element_type=F32)


def dot_nt(left, right):
    return lax.dot_general(left, right, (((1,), (1,)), ((), ())), preferred_element_type=F32)


def dot_tn(left, right):
    return lax.dot_general(left, right, (((0,), (0,)), ((), ())), preferred_element_type=F32)


def sigmoid(values):
    return 0.5 * jnp.tanh(0.5 * values) + 0.5


def chunks(rows):
    size = min(rows, 256)
    return [slice(start, start + size) for start in range(0, rows, size)]


def gru_specs(slots, rows, chars, gate_width, at):
    hid = gate_width // 3
    whole = lambda *shape: pl.BlockSpec(shape, lambda i: (0,) * len(shape))
    letters = lambda place: pl.BlockSpec((1, rows, chars), lambda i: (place(at(i)), 0, 0))
    last = slots - 1
    return [
        letters(lambda t: jnp.minimum(t, last)),
        letters(lambda t: jnp.maximum(last - t, 0)),
        letters(lambda t: jnp.maximum(t - slots, 0)),
        letters(lambda t: jnp.minimum(2 * slots - 1 - t, last)),
        whole(2, chars, gate_width),
        whole(2, hid, gate_width),
        whole(2, 1, gate_width),
        whole(2, 1, gate_width),
        whole(3, rows, 1),
        whole(2, rows, 1),
    ]


def gru_gates(letter, start_low, wi, wr, bi, br, hid):
    both = 2 * hid
    mixed = dot(letter, wi[:, :both]) + dot(start_low, wr[:, :both]) + (bi[:, :both] + br[:, :both])
    reset = sigmoid(mixed[:, :hid])
    update = sigmoid(mixed[:, hid:])
    carried = dot(start_low, wr[:, both:]) + br[:, both:]
    candidate = jnp.tanh(dot(letter, wi[:, both:]) + bi[:, both:] + reset * carried)
    return reset, update, candidate, carried


def gru_forward_kernel(slots, a0, a1, b0, b1, wi, wr, bi, br, counts, keep, starts, pooled, state):
    step = pl.program_id(0)
    rows, hid = state.shape[1], state.shape[2]

    @pl.when(step == 0)
    def _():
        state[...] = jnp.zeros_like(state)

    @pl.when(step == slots)
    def _():
        for way in range(2):
            state[way] = state[way] * keep[way]

    first = step < slots
    place = jnp.where(first, step, step - slots)
    for part in chunks(rows):
        for way, (near, own) in enumerate(((a0, b0), (a1, b1))):
            letter = jnp.where(first, near[0, part], own[0, part])
            start = state[way, part]
            starts[0, way, part] = start
            _, update, candidate, _ = gate_values = gru_gates(
                letter, start.astype(BF16), wi[way], wr[way], bi[way], br[way], hid
            )
            fresh = candidate + update * (start - candidate)
            slot = place if way == 0 else slots - 1 - place
            count = jnp.where(first, counts[way, part], counts[2, part])
            state[way, part] = jnp.where(slot < count, fresh, start)

    @pl.when(step == 2 * slots - 1)
    def _():
        for way in range(2):
            pooled[:, way * hid : (way + 1) * hid] = state[way].astype(BF16)


def gru_forward(letters, wi, wr, bi, br, counts, keep):
    near0, near1, own = letters
    slots, rows, chars = own.shape
    gate_width = wi.shape[-1]
    hid = gate_width // 3
    flops = 2 * 2 * slots * 2 * rows * (chars + hid) * gate_width
    return pl.pallas_call(
        functools.partial(gru_forward_kernel, slots),
        grid=(2 * slots,),
        in_specs=gru_specs(slots, rows, chars, gate_width, lambda i: i),
        out_specs=[
            pl.BlockSpec((1, 2, rows, hid), lambda i: (i, 0, 0, 0)),
            pl.BlockSpec((rows, 2 * hid), lambda i: (0, 0)),
        ],
        out_shape=[
            jax.ShapeDtypeStruct((2 * slots, 2, rows, hid), F32),
            jax.ShapeDtypeStruct((rows, 2 * hid), BF16),
        ],
        scratch_shapes=[pltpu.VMEM((2, rows, hid), F32)],
        compiler_params=pltpu.CompilerParams(vmem_limit_bytes=VMEM_BYTES),
        cost_estimate=pl.CostEstimate(
            flops=flops,
            bytes_accessed=2 * slots * 2 * rows * (hid * 4 + chars * 2),
            transcendentals=2 * slots * 2 * rows * gate_width,
        ),
        name="gru_forward",
    )(near0, near1, own, own, wi, wr, bi, br, counts, keep)


def gru_backward_kernel(
    slots, a0, a1, b0, b1, wi, wr, bi, br, counts, keep, starts, final, wi_t, wr_t,
    letter_grad, wi_grad, wr_grad, bi_grad, br_grad, state,
):
    back = pl.program_id(0)
    step = 2 * slots - 1 - back
    rows, hid = state.shape[1], state.shape[2]
    both = 2 * hid

    @pl.when(back == 0)
    def _():
        for way in range(2):
            state[way] = final[:, way * hid : (way + 1) * hid]
        wi_grad[...] = jnp.zeros_like(wi_grad)
        wr_grad[...] = jnp.zeros_like(wr_grad)
        bi_grad[...] = jnp.zeros_like(bi_grad)
        br_grad[...] = jnp.zeros_like(br_grad)

    first = step < slots
    place = jnp.where(first, step, step - slots)
    for part in chunks(rows):
        for way, (near, own) in enumerate(((a0, b0), (a1, b1))):
            letter = jnp.where(first, near[0, part], own[0, part])
            start = starts[0, way, part]
            start_low = start.astype(BF16)
            reset, update, candidate, carried = gru_gates(
                letter, start_low, wi[way], wr[way], bi[way], br[way], hid
            )
            slot = place if way == 0 else slots - 1 - place
            count = jnp.where(first, counts[way, part], counts[2, part])
            grad = state[way, part]
            fresh = jnp.where(slot < count, grad, 0.0)
            kept = grad - fresh
            scaled = fresh * (1.0 - update)
            cand_pre = scaled * (1.0 - candidate * candidate)
            update_pre = scaled * update * (start - candidate)
            cand_reset = cand_pre * reset
            reset_pre = cand_reset * carried * (1.0 - reset)
            shared = jnp.concatenate([reset_pre.astype(BF16), update_pre.astype(BF16)], axis=1)
            cand_in = cand_pre.astype(BF16)
            cand_rec = cand_reset.astype(BF16)
            state[way, part] = (
                kept
                + update * fresh
                + dot(shared, wr_t[way, :both])
                + dot(cand_rec, wr_t[way, both:])
            )
            letter_grad[0, way, part] = (
                dot(shared, wi_t[way, :both]) + dot(cand_in, wi_t[way, both:])
            ).astype(letter_grad.dtype)
            wi_grad[way, :, :both] += dot_tn(letter, shared)
            wi_grad[way, :, both:] += dot_tn(letter, cand_in)
            wr_grad[way, :, :both] += dot_tn(start_low, shared)
            wr_grad[way, :, both:] += dot_tn(start_low, cand_rec)
            total = jnp.sum(shared.astype(F32), axis=0, keepdims=True)
            bi_grad[way, :, :both] += total
            br_grad[way, :, :both] += total
            bi_grad[way, :, both:] += jnp.sum(cand_in.astype(F32), axis=0, keepdims=True)
            br_grad[way, :, both:] += jnp.sum(cand_rec.astype(F32), axis=0, keepdims=True)

    @pl.when(step == slots)
    def _():
        for way in range(2):
            state[way] = state[way] * keep[way]


def gru_backward(letters, wi, wr, bi, br, counts, keep, starts, final):
    near0, near1, own = letters
    slots, rows, chars = own.shape
    gate_width = wi.shape[-1]
    hid = gate_width // 3
    at = lambda i: 2 * slots - 1 - i
    flops = 3 * 2 * 2 * slots * 2 * rows * (chars + hid) * gate_width
    whole = lambda *shape: pl.BlockSpec(shape, lambda i: (0,) * len(shape))
    return pl.pallas_call(
        functools.partial(gru_backward_kernel, slots),
        grid=(2 * slots,),
        in_specs=gru_specs(slots, rows, chars, gate_width, at)
        + [
            pl.BlockSpec((1, 2, rows, hid), lambda i: (at(i), 0, 0, 0)),
            whole(rows, 2 * hid),
            whole(2, gate_width, chars),
            whole(2, gate_width, hid),
        ],
        out_specs=[
            pl.BlockSpec((1, 2, rows, chars), lambda i: (at(i), 0, 0, 0)),
            whole(2, chars, gate_width),
            whole(2, hid, gate_width),
            whole(2, 1, gate_width),
            whole(2, 1, gate_width),
        ],
        out_shape=[
            jax.ShapeDtypeStruct((2 * slots, 2, rows, chars), BF16),
            jax.ShapeDtypeStruct((2, chars, gate_width), F32),
            jax.ShapeDtypeStruct((2, hid, gate_width), F32),
            jax.ShapeDtypeStruct((2, 1, gate_width), F32),
            jax.ShapeDtypeStruct((2, 1, gate_width), F32),
        ],
        scratch_shapes=[pltpu.VMEM((2, rows, hid), F32)],
        compiler_params=pltpu.CompilerParams(vmem_limit_bytes=VMEM_BYTES),
        cost_estimate=pl.CostEstimate(
            flops=flops,
            bytes_accessed=2 * slots * 2 * rows * (hid * 4 + chars * 4),
            transcendentals=2 * slots * 2 * rows * gate_width,
        ),
        name="gru_backward",
    )(
        near0, near1, own, own, wi, wr, bi, br, counts, keep, starts, final,
        wi.transpose(0, 2, 1), wr.transpose(0, 2, 1),
    )


def head_masks(width, dtype, axis=1, other=1):
    lane = lax.broadcasted_iota(jnp.int32, (1, width) if axis == 1 else (width, 1), axis)
    low = (lane < width // 2).astype(dtype)
    return low, (1 - low).astype(dtype)


def attend_kernel(scale, q, k, v, seg_q, seg_k, out, logsum):
    pair = q.shape[1]
    half = pair // 2
    allowed = seg_k[...] == seg_q[...]
    lane = lax.broadcasted_iota(jnp.int32, (1, pair), 1)
    keys = k[...]
    values = v[...].T
    for head in range(2):
        mine = (lane < half) if head == 0 else (lane >= half)
        query = jnp.where(mine, q[...] * scale, 0).astype(BF16)
        scores = jnp.where(allowed, dot_nt(keys, query), -1e9)
        top = jnp.max(scores, axis=0, keepdims=True)
        expo = jnp.exp(scores - top)
        total = jnp.sum(expo, axis=0, keepdims=True)
        probs = (expo * (1.0 / total)).astype(BF16)
        logsum[0, head : head + 1, :] = top + jnp.log(total)
        mixed = dot(values[head * half : (head + 1) * half], probs)
        out[:, head * half : (head + 1) * half] = mixed.T.astype(BF16)


def attend(q, k, v, seg_q, seg_k, head_dim):
    rows, width = q.shape
    length = k.shape[0]
    pair = 2 * head_dim
    pairs = width // pair
    return pl.pallas_call(
        functools.partial(attend_kernel, head_dim ** -0.5),
        grid=(pairs,),
        in_specs=[
            pl.BlockSpec((rows, pair), lambda i: (0, i)),
            pl.BlockSpec((length, pair), lambda i: (0, i)),
            pl.BlockSpec((length, pair), lambda i: (0, i)),
            pl.BlockSpec((1, rows), lambda i: (0, 0)),
            pl.BlockSpec((length, 1), lambda i: (0, 0)),
        ],
        out_specs=[
            pl.BlockSpec((rows, pair), lambda i: (0, i)),
            pl.BlockSpec((1, 2, rows), lambda i: (i, 0, 0)),
        ],
        out_shape=[
            jax.ShapeDtypeStruct((rows, width), BF16),
            jax.ShapeDtypeStruct((pairs, 2, rows), F32),
        ],
        compiler_params=pltpu.CompilerParams(vmem_limit_bytes=VMEM_BYTES),
        cost_estimate=pl.CostEstimate(
            flops=16 * rows * length * width,
            bytes_accessed=4 * (rows + length) * width,
            transcendentals=rows * length * 2 * pairs,
        ),
        name="attend",
    )(q, k, v, seg_q, seg_k)


def attend_back_kernel(scale, q, k, v, seg_q, seg_k, grad, logsum, dq, dk, dv):
    pair = q.shape[1]
    half = pair // 2
    allowed = seg_k[...] == seg_q[...]
    lane = lax.broadcasted_iota(jnp.int32, (1, pair), 1)
    keys = k[...]
    values = v[...]
    keys_t = keys.T
    key_total = None
    value_total = None
    for head in range(2):
        mine = (lane < half) if head == 0 else (lane >= half)
        query = jnp.where(mine, q[...] * scale, 0).astype(BF16)
        out_grad = jnp.where(mine, grad[...], 0).astype(BF16)
        scores = jnp.where(allowed, dot_nt(keys, query), -1e9)
        probs = jnp.exp(scores - logsum[0, head : head + 1, :])
        probs_grad = dot_nt(values, out_grad)
        delta = jnp.sum(probs * probs_grad, axis=0, keepdims=True)
        scores_grad = (probs * (probs_grad - delta)).astype(BF16)
        key_part = dot(scores_grad, query)
        value_part = dot(probs.astype(BF16), out_grad)
        key_total = key_part if head == 0 else key_total + key_part
        value_total = value_part if head == 0 else value_total + value_part
        query_part = dot(keys_t[head * half : (head + 1) * half], scores_grad)
        dq[:, head * half : (head + 1) * half] = (query_part.T * scale).astype(BF16)
    dk[...] = key_total.astype(dk.dtype)
    dv[...] = value_total.astype(dv.dtype)


def attend_back(q, k, v, seg_q, seg_k, grad, logsum, head_dim):
    rows, width = q.shape
    length = k.shape[0]
    pair = 2 * head_dim
    pairs = width // pair
    return pl.pallas_call(
        functools.partial(attend_back_kernel, head_dim ** -0.5),
        grid=(pairs,),
        in_specs=[
            pl.BlockSpec((rows, pair), lambda i: (0, i)),
            pl.BlockSpec((length, pair), lambda i: (0, i)),
            pl.BlockSpec((length, pair), lambda i: (0, i)),
            pl.BlockSpec((1, rows), lambda i: (0, 0)),
            pl.BlockSpec((length, 1), lambda i: (0, 0)),
            pl.BlockSpec((rows, pair), lambda i: (0, i)),
            pl.BlockSpec((1, 2, rows), lambda i: (i, 0, 0)),
        ],
        out_specs=[
            pl.BlockSpec((rows, pair), lambda i: (0, i)),
            pl.BlockSpec((length, pair), lambda i: (0, i)),
            pl.BlockSpec((length, pair), lambda i: (0, i)),
        ],
        out_shape=[
            jax.ShapeDtypeStruct((rows, width), BF16),
            jax.ShapeDtypeStruct((length, width), BF16),
            jax.ShapeDtypeStruct((length, width), BF16),
        ],
        compiler_params=pltpu.CompilerParams(vmem_limit_bytes=VMEM_BYTES),
        cost_estimate=pl.CostEstimate(
            flops=40 * rows * length * width,
            bytes_accessed=6 * (rows + length) * width,
            transcendentals=rows * length * 2 * pairs,
        ),
        name="attend_back",
    )(q, k, v, seg_q, seg_k, grad, logsum)


HEAD_DIM = 64
PACK = 384
norm_eps = 1e-05


def layer_norm(values, gain, shift):
    centre = jnp.mean(values, axis=-1, keepdims=True)
    centred = values - centre
    spread = jnp.mean(centred * centred, axis=-1, keepdims=True)
    return centred * lax.rsqrt(spread + norm_eps) * gain + shift


def gelu_exact(values):
    return jax.nn.gelu(values, approximate=False)


def widen(values):
    return values.astype(F32)


def back_product(grad, weight):
    return jnp.einsum("rg,cg->rc", grad, weight, preferred_element_type=F32)


def flip(value, bit):
    count = lax.axis_size("rep")
    return lax.ppermute(value, "rep", [(i, i ^ bit) for i in range(count)])


def shift_shard(value, hop):
    count = lax.axis_size("shard")
    return lax.ppermute(value, "shard", [(i, (i - hop) % count) for i in range(count)])


def neighbour_rows(first, last):
    count, place = lax.axis_size("shard"), lax.axis_index("shard")
    if count == 2:
        got = lax.ppermute(jnp.where(place == 0, last, first), "shard", [(0, 1), (1, 0)])
        nothing = jnp.zeros_like(got)
        return jnp.where(place == 0, nothing, got), jnp.where(place == 0, got, nothing)
    up = [(i, i + 1) for i in range(count - 1)]
    down = [(i + 1, i) for i in range(count - 1)]
    return lax.ppermute(last, "shard", up), lax.ppermute(first, "shard", down)


def with_halo(value):
    before, after = neighbour_rows(value[:1], value[-1:])
    return jnp.concatenate([before, value, after], axis=0)


def gather_wide(master, dim):
    reps, rep = lax.axis_size("rep"), lax.axis_index("rep")
    rows = master.shape[dim]
    if rows % (8 * reps) == 0 or lax.axis_size("shard") != 2 and rows % reps == 0:
        piece = lax.dynamic_slice_in_dim(master, rep * (rows // reps), rows // reps, dim)
        return lax.all_gather(piece.astype(BF16), ("shard", "rep"), axis=dim, tiled=True)
    return lax.all_gather(master.astype(BF16), "shard", axis=dim, tiled=True)


def gather_small(value):
    if lax.axis_size("shard") != 2:
        return lax.all_gather(value, "shard")
    place = lax.axis_index("shard")
    other = lax.ppermute(value, "shard", [(0, 1), (1, 0)])
    return jnp.stack([jnp.where(place == 0, value, other), jnp.where(place == 0, other, value)])


def both_cores(*values):
    widths = [value.shape[1] for value in values]
    other = flip(jnp.concatenate(values, axis=1), 1)
    result, at = [], 0
    for value, width in zip(values, widths):
        result.append((value, other[:, at : at + width]))
        at += width
    return result


def core_half(value, which):
    half = value.shape[1] // 2
    return lax.dynamic_slice_in_dim(value, which * half, half, 1)


def pair_product(left, right):
    total = None
    for one, two in zip(left, right):
        part = jnp.einsum("rc,rg->cg", one, two, preferred_element_type=F32)
        total = part if total is None else total + part
    return total


def columns(pair, place, parts):
    size = pair[0].shape[1] // parts
    return [lax.dynamic_slice_in_dim(item, place * size, size, 1) for item in pair]


def packed(blocks, width):
    rows = []
    for block in blocks:
        lanes = block.shape[1]
        if lanes % width == 0:
            rows += [block[:, at : at + width] for at in range(0, lanes, width)]
        else:
            rows.append(block.reshape(-1, width))
    return jnp.concatenate(rows, axis=0) if len(rows) > 1 else rows[0]


def unpacked(rows, shapes, width):
    blocks, at = [], 0
    for depth, lanes in shapes:
        if lanes % width == 0:
            parts = []
            for _ in range(lanes // width):
                parts.append(rows[at : at + depth])
                at += depth
            blocks.append(jnp.concatenate(parts, axis=1) if len(parts) > 1 else parts[0])
        else:
            size = depth * lanes // width
            blocks.append(rows[at : at + size].reshape(depth, lanes))
            at += size
    return blocks


def reduce_group(build):
    parts, place = lax.axis_size("shard"), lax.axis_index("shard")
    rep = lax.axis_index("rep")
    sent = [
        shift_shard(build((place + hop) % parts).astype(BF16), hop * -1 % parts)
        for hop in range(1, parts)
    ]
    total = build(place)
    for item in sent:
        total = total + widen(item)
    bits = [1 << k for k in range(1, (lax.axis_size("rep") - 1).bit_length())]
    for bit in bits:
        half = total.shape[0] // 2
        side = (rep // bit) % 2
        away = lax.dynamic_slice_in_dim(total, (1 - side) * half, half, 0).astype(BF16)
        mine = lax.dynamic_slice_in_dim(total, side * half, half, 0)
        total = widen(mine) + widen(flip(away, bit))
    total = total.astype(BF16)
    for bit in bits[::-1]:
        other = flip(total, bit)
        side = (rep // bit) % 2
        total = jnp.concatenate(
            [jnp.where(side == 0, total, other), jnp.where(side == 0, other, total)], axis=0
        )
    other = flip(total, 1)
    core = rep % 2
    return jnp.where(core == 0, total, other), jnp.where(core == 0, other, total)


def shards(
    token_in,
    char_in,
    char_ids,
    char_counts,
    segments,
    token_cot,
    char_cot,
    query_proj,
    key_proj,
    value_proj,
    output_proj,
    query_bias,
    value_bias,
    output_bias,
    first_gain,
    first_shift,
    expand_proj,
    expand_bias,
    shrink_proj,
    shrink_bias,
    char_table,
    gate_input,
    input_bias,
    gate_recur,
    recur_bias,
    token_proj,
    token_bias,
    char_proj,
    char_bias,
    merging_kernel,
    merging_bias,
    token_gain,
    token_shift,
    char_gain,
    char_shift,
):
    rows, width = token_in.shape
    place, parts = lax.axis_index("shard"), lax.axis_size("shard")
    rep = lax.axis_index("rep")
    core = rep % 2
    slots = char_ids.shape[1]
    chars = char_table.shape[1]
    vocab = char_table.shape[0] * parts
    gate_width = gate_input.shape[-1]
    hid = gate_width // 3
    ff = expand_proj.shape[1]

    vectors = (
        query_bias, value_bias, output_bias, first_gain, first_shift, expand_bias, shrink_bias,
        input_bias, recur_bias, token_bias, char_bias, merging_bias, token_gain, token_shift,
        char_gain, char_shift,
    )
    flat = jnp.concatenate([item.reshape(-1) for item in vectors]).astype(BF16)
    pad = -flat.shape[0] % (8 * chars)
    small = jnp.concatenate(
        [char_table.astype(BF16), jnp.pad(flat, (0, pad)).reshape(-1, chars)], axis=0
    )
    small = gather_small(small)
    table_low = small[:, : char_table.shape[0]].reshape(vocab, chars)
    tail = widen(small[:, char_table.shape[0] :].reshape(parts, -1))
    wide, at = [], 0
    for item in vectors:
        size = item.size
        block = tail[:, at : at + size].reshape((parts,) + item.shape)
        at += size
        if item.ndim == 2:
            wide.append(block.transpose(1, 0, 2).reshape(item.shape[0], 1, -1))
        else:
            wide.append(block.reshape(-1))
    (
        bias_query, bias_value, bias_output, gain_first, shift_first, bias_expand, bias_shrink,
        bias_input, bias_recur, bias_token, bias_char, bias_merging, gain_token, shift_token,
        gain_char, shift_char,
    ) = wide

    qkv_low = gather_wide(jnp.stack([query_proj, key_proj, value_proj]), 1)
    query_low, key_low, value_low = qkv_low[0], qkv_low[1], qkv_low[2]
    input_low = gather_wide(gate_input, 1)
    recur_low = gather_wide(gate_recur, 1)
    side_low = gather_wide(jnp.stack([output_proj, token_proj, char_proj]), 1)
    output_low, project_token, project_char = side_low[0], side_low[1], side_low[2]
    expand_low = gather_wide(expand_proj, 0)
    shrink_low = gather_wide(shrink_proj, 0)
    kernel_low = gather_wide(merging_kernel, 1)

    queries = (dot(token_in, query_low) + bias_query).astype(BF16)
    keys = dot(token_in, key_low).astype(BF16)
    values = (dot(token_in, value_low) + bias_value).astype(BF16)
    keys_values = jnp.concatenate([keys, values], axis=1)
    blocks = [keys_values] + [shift_shard(keys_values, hop) for hop in range(1, parts)]
    everyone = jnp.concatenate(blocks, axis=0)
    seg_blocks = [
        lax.dynamic_slice_in_dim(segments, ((place + hop) % parts) * rows, rows)
        for hop in range(parts)
    ]
    seg_rows = seg_blocks[0]
    seg_q = seg_rows[None, :]
    seg_k = jnp.concatenate(seg_blocks)[:, None]
    all_keys, all_values = everyone[:, :width], everyone[:, width:]
    mixed, logsum = attend(queries, all_keys, all_values, seg_q, seg_k, HEAD_DIM)

    packed_ids = jnp.concatenate([char_ids, char_counts[:, None]], axis=1)
    ids_ext = with_halo(packed_ids)
    counts_ext = ids_ext[:, slots]
    onehot = (
        ids_ext[:, :slots].T.reshape(-1)[:, None] == jnp.arange(vocab, dtype=jnp.int32)[None, :]
    ).astype(BF16)
    embedded = dot(onehot, table_low).astype(BF16).reshape(slots, rows + 2, chars)
    letters = (embedded[:, :rows], embedded[:, 2:], embedded[:, 1 : rows + 1])
    counts = jnp.stack([counts_ext[:rows], counts_ext[2:], counts_ext[1 : rows + 1]])[:, :, None]
    length = segments.shape[0]
    position = place * rows + jnp.arange(rows)
    before = jnp.take(segments, jnp.maximum(position - 1, 0))
    after = jnp.take(segments, jnp.minimum(position + 1, length - 1))
    keep = jnp.stack(
        [
            ((position > 0) & (before == seg_rows)).astype(F32),
            ((position < length - 1) & (after == seg_rows)).astype(F32),
        ]
    )[:, :, None]
    starts, pooled_low = gru_forward(
        letters, input_low, recur_low, bias_input, bias_recur, counts, keep
    )

    first_in = widen(token_in) + (dot(mixed, output_low) + bias_output)
    first = layer_norm(first_in, gain_first, shift_first)
    first_low = first.astype(BF16)
    up = dot(first_low, expand_low) + bias_expand
    hidden = gelu_exact(up).astype(BF16)
    token_mid = first + dot(hidden, shrink_low) + bias_shrink
    mid_low = token_mid.astype(BF16)

    tok_side = dot(mid_low, project_token) + bias_token
    char_side = dot(pooled_low, project_char) + bias_char
    joined = jnp.concatenate([tok_side, char_side], axis=1).astype(BF16)
    joined_ext = with_halo(joined)
    merged = (
        bias_merging
        + dot(joined_ext[0:rows], kernel_low[0])
        + dot(joined_ext[1 : rows + 1], kernel_low[1])
        + dot(joined_ext[2 : rows + 2], kernel_low[2])
    )
    act = gelu_exact(merged)
    tok_pre = token_mid + act[:, :width]
    char_pre = widen(char_in) + act[:, width:]
    token_out = layer_norm(tok_pre, gain_token, shift_token).astype(BF16)
    char_out = layer_norm(char_pre, gain_char, shift_char).astype(BF16)

    _, token_pull = jax.vjp(layer_norm, tok_pre, gain_token, shift_token)
    tok_pre_grad, token_gain_grad, token_shift_grad = token_pull(widen(token_cot))
    _, char_pull = jax.vjp(layer_norm, char_pre, gain_char, shift_char)
    char_grad, char_gain_grad, char_shift_grad = char_pull(widen(char_cot))
    _, gelu_pull = jax.vjp(gelu_exact, merged)
    merged_grad = gelu_pull(jnp.concatenate([tok_pre_grad, char_grad], axis=1))[0].astype(BF16)
    merging_bias_grad = jnp.sum(widen(merged_grad), axis=0)
    joined_pair, merged_pair = both_cores(
        joined_ext, jnp.pad(core_half(merged_grad, 1 - core), ((0, 2), (0, 0)))
    )
    merged_pair = (core_half(merged_grad, core), merged_pair[1][:rows])

    def merging_terms(target):
        sources = columns(joined_pair, target, parts)
        return jnp.concatenate(
            [
                pair_product([item[tap : tap + rows] for item in sources], merged_pair)
                for tap in range(3)
            ],
            axis=0,
        )

    merging_sum = reduce_group(merging_terms)
    merged_ext = with_halo(merged_grad)
    joined_grad = (
        back_product(merged_ext[2 : rows + 2], kernel_low[0])
        + back_product(merged_ext[1 : rows + 1], kernel_low[1])
        + back_product(merged_ext[0:rows], kernel_low[2])
    )
    tok_side_grad = joined_grad[:, :width].astype(BF16)
    char_side_grad = joined_grad[:, width:].astype(BF16)
    token_bias_grad = jnp.sum(widen(tok_side_grad), axis=0)
    char_bias_grad = jnp.sum(widen(char_side_grad), axis=0)
    pooled_grad = back_product(char_side_grad, project_char)
    mid_grad = tok_pre_grad + back_product(tok_side_grad, project_token)

    shrink_out_grad = mid_grad.astype(BF16)
    shrink_bias_grad = jnp.sum(widen(shrink_out_grad), axis=0)
    hidden_grad = back_product(shrink_out_grad, shrink_low)
    _, up_pull = jax.vjp(gelu_exact, up)
    up_grad = up_pull(hidden_grad)[0].astype(BF16)
    expand_bias_grad = jnp.sum(widen(up_grad), axis=0)
    first_grad = mid_grad + back_product(up_grad, expand_low)
    halves = (shrink_out_grad, up_grad, tok_side_grad, char_side_grad)
    pairs = both_cores(
        hidden, first_low, mid_low, pooled_low, *[core_half(item, 1 - core) for item in halves]
    )
    mine = [(core_half(item, core), pair[1]) for item, pair in zip(halves, pairs[4:])]

    def middle_terms(target):
        return packed(
            [
                pair_product(columns(pairs[0], target, parts), mine[0]),
                pair_product(mine[1], columns(pairs[1], target, parts)),
                pair_product(columns(pairs[2], target, parts), mine[2]),
                pair_product(columns(pairs[3], target, parts), mine[3]),
            ],
            PACK,
        )

    middle_sum = reduce_group(middle_terms)

    _, first_pull = jax.vjp(layer_norm, first_in, gain_first, shift_first)
    first_in_grad, first_gain_grad, first_shift_grad = first_pull(first_grad)
    attn_grad = first_in_grad.astype(BF16)
    output_bias_grad = jnp.sum(widen(attn_grad), axis=0)
    mixed_grad = back_product(attn_grad, output_low).astype(BF16)
    queries_grad, key_terms, value_terms = attend_back(
        queries, all_keys, all_values, seg_q, seg_k, mixed_grad, logsum, HEAD_DIM
    )
    terms = jnp.concatenate([key_terms, value_terms], axis=1)
    owned = widen(terms[:rows])
    for hop in range(1, parts):
        owned = owned + widen(shift_shard(terms[hop * rows : (hop + 1) * rows], -hop % parts))
    owned = owned.astype(BF16)

    letter_grad, input_grad, recur_grad, bias_input_grad, bias_recur_grad = gru_backward(
        letters, input_low, recur_low, bias_input, bias_recur, counts, keep, starts, pooled_grad
    )
    ahead, behind = widen(letter_grad[:, 0]), widen(letter_grad[:, 1])
    embedded_grad = (
        jnp.pad(ahead[:slots], ((0, 0), (0, 2), (0, 0)))
        + jnp.pad(behind[:slots][::-1], ((0, 0), (2, 0), (0, 0)))
        + jnp.pad(ahead[slots:] + behind[slots:][::-1], ((0, 0), (1, 1), (0, 0)))
    )
    table_grad = dot_tn(onehot, embedded_grad.astype(BF16).reshape(-1, chars))

    keys_grad, values_grad = owned[:, :width], owned[:, width:]
    query_bias_grad = jnp.sum(widen(queries_grad), axis=0)
    value_bias_grad = jnp.sum(widen(values_grad), axis=0)
    token_grad = (
        first_in_grad
        + back_product(queries_grad, query_low)
        + back_product(keys_grad, key_low)
        + back_product(values_grad, value_low)
    )

    late = (queries_grad, keys_grad, values_grad, attn_grad)
    late_pairs = both_cores(token_in, mixed, *[core_half(item, 1 - core) for item in late])
    late_mine = [(core_half(item, core), pair[1]) for item, pair in zip(late, late_pairs[2:])]
    gru_terms = jnp.concatenate([input_grad, recur_grad], axis=1)
    gru_away = lax.dynamic_index_in_dim(gru_terms, 1 - core, 0, keepdims=False).astype(BF16)
    gru_own = lax.dynamic_index_in_dim(gru_terms, core, 0, keepdims=False) + widen(flip(gru_away, 1))
    table_terms = table_grad.reshape(parts, 2, -1, chars)
    table_away = lax.dynamic_index_in_dim(table_terms, 1 - core, 1, keepdims=False).astype(BF16)
    table_own = lax.dynamic_index_in_dim(table_terms, core, 1, keepdims=False) + widen(
        flip(table_away, 1)
    )
    chars_part, hid_part = chars // parts, hid // parts

    def late_terms(target):
        table_part = lax.dynamic_index_in_dim(table_own, target, 0, keepdims=False)
        return packed(
            [
                pair_product(columns(late_pairs[0], target, parts), late_mine[0]),
                pair_product(columns(late_pairs[0], target, parts), late_mine[1]),
                pair_product(columns(late_pairs[0], target, parts), late_mine[2]),
                pair_product(columns(late_pairs[1], target, parts), late_mine[3]),
                lax.dynamic_slice_in_dim(gru_own, target * chars_part, chars_part, 0),
                lax.dynamic_slice_in_dim(gru_own, chars + target * hid_part, hid_part, 0),
                jnp.pad(table_part, ((0, 0), (0, PACK - chars))),
            ],
            PACK,
        )

    late_sum = reduce_group(late_terms)

    vector_grads = (
        query_bias_grad, value_bias_grad, output_bias_grad, first_gain_grad, first_shift_grad,
        expand_bias_grad, shrink_bias_grad, bias_input_grad[:, 0], bias_recur_grad[:, 0],
        token_bias_grad, char_bias_grad, merging_bias_grad, token_gain_grad, token_shift_grad,
        char_gain_grad, char_shift_grad,
    )
    flat_grad = jnp.concatenate([item.reshape(-1) for item in vector_grads])
    flat_grad = jnp.pad(flat_grad, (0, -flat_grad.shape[0] % 1024)).reshape(-1, 128)
    flat_grad = lax.psum(flat_grad, ("rep", "shard")).reshape(-1)
    vector_out, at = [], 0
    for item in vector_grads:
        full = flat_grad[at : at + item.size].reshape(item.shape)
        at += item.size
        size = item.shape[-1] // parts
        vector_out.append(lax.dynamic_slice_in_dim(full, place * size, size, item.ndim - 1))
    (
        query_bias_out, value_bias_out, output_bias_out, first_gain_out, first_shift_out,
        expand_bias_out, shrink_bias_out, input_bias_out, recur_bias_out, token_bias_out,
        char_bias_out, merging_bias_out, token_gain_out, token_shift_out, char_gain_out,
        char_shift_out,
    ) = vector_out

    part, joint = width // parts, 2 * width // parts
    merging_out = jnp.concatenate(
        [widen(half).reshape(3, joint, width) for half in merging_sum], axis=2
    )
    middle = [
        unpacked(half, [(ff // parts, PACK), (ff // 2, part), (part, PACK), (part, PACK)], PACK)
        for half in middle_sum
    ]
    shrink_out = jnp.concatenate([widen(half[0]) for half in middle], axis=1)
    expand_out = jnp.concatenate([widen(half[1]) for half in middle], axis=0).T
    token_proj_out = jnp.concatenate([widen(half[2]) for half in middle], axis=1)
    char_proj_out = jnp.concatenate([widen(half[3]) for half in middle], axis=1)
    tail_rows = vocab // parts // 2
    late_blocks = [
        unpacked(
            half,
            [(part, PACK)] * 4
            + [(chars_part, gate_width), (hid_part, gate_width), (tail_rows, PACK)],
            PACK,
        )
        for half in late_sum
    ]
    query_out, key_out, value_out, output_out = [
        jnp.concatenate([widen(half[k]) for half in late_blocks], axis=1) for k in range(4)
    ]
    input_out = jnp.stack([widen(half[4]) for half in late_blocks])
    recur_out = jnp.stack([widen(half[5]) for half in late_blocks])
    table_out = jnp.concatenate([widen(half[6][:, :chars]) for half in late_blocks], axis=0)
    return (
        token_out, char_out, token_grad, char_grad,
        query_out, key_out, value_out, output_out,
        query_bias_out, value_bias_out, output_bias_out, first_gain_out, first_shift_out,
        expand_out, expand_bias_out, shrink_out, shrink_bias_out, table_out,
        input_out, input_bias_out, recur_out, recur_bias_out,
        token_proj_out, token_bias_out, char_proj_out, char_bias_out,
        merging_out, merging_bias_out, token_gain_out, token_shift_out, char_gain_out,
        char_shift_out,
    )


def solution(mesh):
    rows = P(("rep", "shard"), None)
    split, vector = P("shard", None), P("shard")
    in_specs = (
        rows, rows, rows, P(("rep", "shard")), P("rep"), rows, rows,
        split, split, split, split, vector, vector, vector, vector, vector,
        split, vector, split, vector, split,
        P(None, "shard", None), P(None, "shard"), P(None, "shard", None), P(None, "shard"),
        split, vector, split, vector, P(None, "shard", None), vector,
        vector, vector, vector, vector,
    )
    out_specs = (rows,) * 4 + in_specs[7:]
    return jax.shard_map(shards, mesh=mesh, in_specs=in_specs, out_specs=out_specs, check_vma=False)
```

time: 2810 us -> 1280 us (0.46)
  waiting for transfers between devices: 1370 us -> 650 us
  local copies, waits for them, and re-layouts: 556 us -> 126 us
  matrix products: 402 us -> 176 us
  other arithmetic: 301 us -> 110 us
  Pallas kernels: 0 us -> 150 us
  blocking collectives: 124 us -> 0 us
    reduce_scatter x13 -> x0, waiting for transfers between devices: 779 us -> none  [the longest x1 315 us: shards(): lax.psum_scatter(early[8], 'shard', scatter_dimension=1, tiled=True)]
    psum x1, waiting for transfers between devices: 531 us -> 112 us  [shards(): flat_grad = lax.psum(flat_grad, ('rep', 'shard')).reshape(-1)]
    all_gather x12 -> x7, waiting for transfers between devices: 35.4 us -> 303 us  [the longest x6 303 us: gather_wide(): lax.all_gather(piece.astype(BF16), ('shard', 'rep'), axis=dim, tiled=True)]
    ppermute x8 -> x35, waiting for transfers between devices: 0.02 us -> 235 us  [the longest x26 121 us: flip(): return lax.ppermute(value, 'rep', [(i, i ^ bit) for i in range(count)])]
    dot_general x143 -> x68, matrix products: 402 us -> 176 us  [the longest x44 74.6 us: pair_product(): part = jnp.einsum('rc,rg->cg', one, two, preferred_element_type=F32)]
    pallas_call x0 -> x4, Pallas kernels: none -> 150 us  [the longest x1 79.8 us: gru_backward(): pl.pallas_call(functools.partial(gru_backward_kernel, slots), grid=(2 * s...]
    another operation x34 -> x21, other arithmetic: 97.1 us -> 2.73 us  [the longest x1 1.32 us: shards(): recur_out = jnp.stack([widen(half[5]) for half in late_blocks])]
    another operation x12 -> x6, local copies, waits for them, and re-layouts: 77.4 us -> 1.04 us
  transfers between devices with their start and end apart: 36 -> 43, of which waited for: 15 -> 21; matrix products, arithmetic and copies ran while one was open for 37% -> 27% of each run, Pallas kernels for 0% -> 12%
where the time goes in v1:
time: 1280 us
  waiting for transfers between devices  650 us (51%)
  matrix products  176 us (14%)
  Pallas kernels  150 us (12%)
  local copies, waits for them, and re-layouts  126 us (10%)
  other arithmetic  110 us (9%)
  starting transfers between devices  46.6 us (4%)
  between operations  17.3 us (1%)
    all_gather x6, waiting for transfers between devices, gather_wide(): lax.all_gather(piece.astype(BF16), ('shard', 'rep'), axis=dim, tiled=True)  303 us
    ppermute x26, waiting for transfers between devices, flip(): return lax.ppermute(value, 'rep', [(i, i ^ bit) for i in range(count)])  121 us
    psum x1, waiting for transfers between devices, shards(): flat_grad = lax.psum(flat_grad, ('rep', 'shard')).reshape(-1)  112 us
    ppermute x5, waiting for transfers between devices, shift_shard(): lax.ppermute(value, 'shard', [(i, (i - hop) % count) for i in range(count)])  109 us
    pallas_call x1, Pallas kernels, gru_backward(): pl.pallas_call(functools.partial(gru_backward_kernel, slots), grid=(2 * s...  79.8 us
    dot_general x44, matrix products, pair_product(): part = jnp.einsum('rc,rg->cg', one, two, preferred_element_type=F32)  74.6 us
    dot_general x12, matrix products, dot(): return jnp.dot(left, right, preferred_element_type=F32)  60 us
    unnamed x361, local copies, waits for them, and re-layouts  45 us
  transfers between devices with their start and end apart: 43, of which 21 were waited for; matrix products, arithmetic and copies ran while one was open for 27% of the time, Pallas kernels for 12%

profile of v1, /device:TPU:17, one launch (start us, length us, event | category | flops | bytes accessed | tf_op | source)
XLA Modules:
  0.0 1276.8 jit_solution(17822219992378872114)
XLA Ops:
  7.3 3.9 copy.133
  35.8 4.5 collective-permute-done.2
  51.8 6.5 copy.115
  58.3 46.3 %all-gather.16.cloned.1.call-done = bf16[2,256,1152]{2,0,1:T(2,128)(2,1)} async-done(((bf16[2,8,1152]{2,0,1:T(2,128)(2,1)}), bf16[2,256,1152]{2,0,1:T(2,128)(2,1)}) %all-gather.16.cloned.1.call-update) | async-done | bytes 1179664 | tf_op jit(solution)/shard_map/all_gather | solution.py:419
  110.1 57.3 %all-gather.8.cloned.1.call-done = bf16[3,768,768]{2,1,0:T(8,128)(2,1)} async-done(((bf16[3,24,768]{2,1,0:T(8,128)(2,1)}), bf16[3,768,768]{2,1,0:T(8,128)(2,1)}) %all-gather.8.cloned.1.call-update) | async-done | bytes 3538960 | tf_op jit(solution)/shard_map/all_gather | solution.py:419
  174.8 28.6 %gru_forward.1 = (f32[10,2,512,384]{3,2,1,0:T(8,128)}, bf16[512,768]{1,0:T(8,128)(2,1)}) custom-call(bf16[5,512,256]{2,1,0:T(8,128)(2,1)} %get-tuple-element.256.a0, bf16[5,512,256]{2,1,0:T(8,128)(2,1)} %get-tuple-element.255.a1, bf16[5,512,256]{2,1,0:T(8,128)(2,1)} %get-tuple-element.254.b0.b1, bf16[5,512,256]{2,1,0:T(8,128)(2,1)} %get-tuple-element.254.b0.b1, ...), custom_call_target="tpu_custom_call" | custom-call | flops 15099494400 | bytes 20971520 | tf_op jit(solution)/shard_map/gru_forward/pallas_call | solution.py:104
  206.3 25.7 %all-gather.10.cloned.1.call-done = bf16[3,768,768]{2,1,0:T(8,128)(2,1)} async-done(((bf16[3,24,768]{2,1,0:T(8,128)(2,1)}), bf16[3,768,768]{2,1,0:T(8,128)(2,1)}) %all-gather.10.cloned.1.call-update) | async-done | bytes 3538960 | tf_op jit(solution)/shard_map/all_gather | solution.py:419
  238.2 16.6 %attend.1 = (bf16[512,768]{1,0:T(8,128)(2,1)}, f32[6,2,512]{2,1,0:T(2,128)}) custom-call(bf16[512,768]{1,0:T(8,128)(2,1)} %fusion.65.q, bf16[1024,768]{1,0:T(8,128)(2,1)} %get-tuple-element.209.k, bf16[1024,768]{1,0:T(8,128)(2,1)} %get-tuple-element.208.v, s32[1,512]{1,0:T(1,128)} %bitcast.228, s32[1024,1]{1,0:T(8,128)} %copy.104.seg_k), custom_call_target="tpu_custom_call" | custom-call | flops 6442450944 | bytes 4718592 | tf_op jit(solution)/shard_map/attend/pallas_call | solution.py:270
  260.8 38.1 %all-gather.12.cloned.1.call-done = bf16[768,3072]{1,0:T(8,128)(2,1)} async-done(((bf16[24,3072]{1,0:T(8,128)(2,1)}), bf16[768,3072]{1,0:T(8,128)(2,1)}) %all-gather.12.cloned.1.call-update) | async-done | bytes 4718608 | tf_op jit(solution)/shard_map/all_gather | solution.py:419
  298.8 19.3 %constant_dynamic-update-slice_fusion.10 = (bf16[512,8064]{1,0:T(8,128)(2,1)}, bf16[512,3072]{1,0:T(8,128)(2,1)}, f32[512,3072]{1,0:T(8,128)}, f32[512,3072]{1,0:T(8,128)}) fusion(f32[3072]{0:T(1024)S(1)} %add.623, bf16[512,768]{1,0:T(8,128)(2,1)} %fusion.68, bf16[768,3072]{1,0:T(8,128)(2,1)} %all-gather.12.cloned.1.call-done), kind=kOutput, calls=%fused_computation.443 | convolution fusion | flops 2519728128 | bytes 24391680 | tf_op jit(solution)/shard_map/dot_general | solution.py:15
  319.3 44.7 %all-gather.14.cloned.1.call-done = bf16[3072,768]{1,0:T(8,128)(2,1)} async-done(((bf16[96,768]{1,0:T(8,128)(2,1)}), bf16[3072,768]{1,0:T(8,128)(2,1)}) %all-gather.14.cloned.1.call-update) | async-done | bytes 4718608 | tf_op jit(solution)/shard_map/all_gather | solution.py:419
  364.0 7.4 constant_dynamic-update-slice_fusion.8
  377.9 91.0 %all-gather.20.cloned.1.call-done = bf16[3,1536,1536]{2,1,0:T(8,128)(2,1)} async-done(((bf16[3,48,1536]{2,1,0:T(8,128)(2,1)}), bf16[3,1536,1536]{2,1,0:T(8,128)(2,1)}) %all-gather.20.cloned.1.call-update) | async-done | bytes 14155792 | tf_op jit(solution)/shard_map/all_gather | solution.py:419
  468.9 5.4 fusion.16
  478.5 8.9 multiply_multiply_fusion.10
  512.0 3.3 fusion.79.final
  515.3 79.8 %gru_backward.1 = (bf16[10,2,512,256]{3,2,1,0:T(8,128)(2,1)}, f32[2,256,1152]{2,1,0:T(8,128)}, f32[2,384,1152]{2,1,0:T(8,128)}, f32[2,1,1152]{2,1,0:T(1,128)}, f32[2,1,1152]{2,1,0:T(1,128)}) custom-call(bf16[5,512,256]{2,1,0:T(8,128)(2,1)} %get-tuple-element.256.a0, bf16[5,512,256]{2,1,0:T(8,128)(2,1)} %get-tuple-element.255.a1, ...), custom_call_target="tpu_custom_call" | custom-call | flops 45298483200 | bytes 26214400 | tf_op jit(solution)/shard_map/gru_backward/pallas_call | solution.py:201
  595.1 4.7 slice_convert_fusion
  599.8 5.4 fusion.80
  606.1 10.1 convert_reduce_fusion
  616.2 3.6 multiply_reduce_fusion
  622.4 25.1 %attend_back.1 = (bf16[512,768]{1,0:T(8,128)(2,1)}, bf16[1024,768]{1,0:T(8,128)(2,1)}, bf16[1024,768]{1,0:T(8,128)(2,1)}) custom-call(bf16[512,768]{1,0:T(8,128)(2,1)} %fusion.65.q, bf16[1024,768]{1,0:T(8,128)(2,1)} %get-tuple-element.209.k, bf16[1024,768]{1,0:T(8,128)(2,1)} %get-tuple-element.208.v, s32[1,512]{1,0:T(1,128)} %bitcast.229, ...), custom_call_target="tpu_custom_call" | custom-call | flops 16106127360 | bytes 7077888 | tf_op jit(solution)/shard_map/attend_back/pallas_call | solution.py:332
  676.7 3.6 rev.6
  680.3 3.9 add_convert_fusion.3
  685.5 5.2 fusion.1
  709.7 3.3 fusion.77
  725.7 3.3 add_add_fusion.3
  729.0 112.0 %all-reduce.9.cloned.1.call-done = f32[144,128]{1,0:T(8,128)} async-done(((f32[144,128]{1,0:T(8,128)}), f32[144,128]{1,0:T(8,128)}) %all-reduce.9.cloned.1.call-update) | async-done | bytes 73744 | tf_op jit(solution)/shard_map/psum | solution.py:799
  891.5 42.8 %collective-permute-done.27 = bf16[2304,768]{1,0:T(8,128)(2,1)S(1)} collective-permute-done((bf16[2304,768]{1,0:T(8,128)(2,1)S(1)}, bf16[2304,768]{1,0:T(8,128)(2,1)S(1)}, u32[]{:S(2)}, u32[]{:S(2)}) %collective-permute-start.27) | collective-permute-done | bytes 3538976 | tf_op jit(solution)/shard_map/ppermute | solution.py:395
  937.0 42.6 %collective-permute-done.9 = bf16[2752,384]{1,0:T(8,128)(2,1)S(1)} collective-permute-done((bf16[2752,384]{1,0:T(8,128)(2,1)}, bf16[2752,384]{1,0:T(8,128)(2,1)S(1)}, u32[]{:S(2)}, u32[]{:S(2)}) %collective-permute-start.9) | collective-permute-done | bytes 2113568 | tf_op jit(solution)/shard_map/ppermute | solution.py:395
  993.5 11.2 pad_maximum_fusion.4
  1011.9 3.9 convolution_add_fusion.2
  1016.0 4.4 collective-permute-start.12
  1022.6 17.8 %collective-permute-done.12 = bf16[344,384]{1,0:T(8,128)(2,1)S(1)} collective-permute-done((bf16[344,384]{1,0:T(8,128)(2,1)S(1)}, bf16[344,384]{1,0:T(8,128)(2,1)S(1)}, u32[]{:S(2)}, u32[]{:S(2)}) %collective-permute-start.12) | collective-permute-done | bytes 264224 | tf_op jit(solution)/shard_map/ppermute | solution.py:390
  1044.3 23.2 %collective-permute-done.18 = bf16[3840,384]{1,0:T(8,128)(2,1)} collective-permute-done((bf16[3840,384]{1,0:T(8,128)(2,1)S(1)}, bf16[3840,384]{1,0:T(8,128)(2,1)}, u32[]{:S(2)}, u32[]{:S(2)}) %collective-permute-start.18) | collective-permute-done | bytes 2949152 | tf_op jit(solution)/shard_map/ppermute | solution.py:395
  1067.5 5.6 maximum_add_fusion.1
  1076.7 4.4 collective-permute-start.31
  1084.6 14.9 %collective-permute-done.31 = bf16[288,768]{1,0:T(8,128)(2,1)S(1)} collective-permute-done((bf16[288,768]{1,0:T(8,128)(2,1)S(1)}, bf16[288,768]{1,0:T(8,128)(2,1)S(1)}, u32[]{:S(2)}, u32[]{:S(2)}) %collective-permute-start.31) | collective-permute-done | bytes 442400 | tf_op jit(solution)/shard_map/ppermute | solution.py:390
  1109.0 13.9 %collective-permute-done.32 = bf16[576,768]{1,0:T(8,128)(2,1)S(1)} collective-permute-done((bf16[576,768]{1,0:T(8,128)(2,1)S(1)}, bf16[576,768]{1,0:T(8,128)(2,1)S(1)}, u32[]{:S(2)}, u32[]{:S(2)}) %collective-permute-start.32) | collective-permute-done | bytes 884768 | tf_op jit(solution)/shard_map/ppermute | solution.py:390
  1124.6 14.1 %collective-permute-done.20 = bf16[960,384]{1,0:T(8,128)(2,1)S(1)} collective-permute-done((bf16[960,384]{1,0:T(8,128)(2,1)S(1)}, bf16[960,384]{1,0:T(8,128)(2,1)S(1)}, u32[]{:S(2)}, u32[]{:S(2)}) %collective-permute-start.20) | collective-permute-done | bytes 737312 | tf_op jit(solution)/shard_map/ppermute | solution.py:390
  1139.4 14.5 %collective-permute-done.21 = bf16[480,384]{1,0:T(8,128)(2,1)S(1)} collective-permute-done((bf16[480,384]{1,0:T(8,128)(2,1)S(1)}, bf16[480,384]{1,0:T(8,128)(2,1)S(1)}, u32[]{:S(2)}, u32[]{:S(2)}) %collective-permute-start.21) | collective-permute-done | bytes 368672 | tf_op jit(solution)/shard_map/ppermute | solution.py:390
  1154.2 3.2 collective-permute-start.22
  1171.6 4.1 collective-permute-start.23
  1177.6 14.6 %collective-permute-done.23 = bf16[960,384]{1,0:T(8,128)(2,1)S(1)} collective-permute-done((bf16[960,384]{1,0:T(8,128)(2,1)S(1)}, bf16[960,384]{1,0:T(8,128)(2,1)S(1)}, u32[]{:S(2)}, u32[]{:S(2)}) %collective-permute-start.23) | collective-permute-done | bytes 737312 | tf_op jit(solution)/shard_map/ppermute | solution.py:390
  1198.3 27.1 %collective-permute-done.24 = bf16[1920,384]{1,0:T(8,128)(2,1)S(1)} collective-permute-done((bf16[1920,384]{1,0:T(8,128)(2,1)S(1)}, bf16[1920,384]{1,0:T(8,128)(2,1)S(1)}, u32[]{:S(2)}, u32[]{:S(2)}) %collective-permute-start.24) | collective-permute-done | bytes 1474592 | tf_op jit(solution)/shard_map/ppermute | solution.py:390
  1237.0 9.3 maximum_convert_fusion
  1246.3 8.0 broadcast_select_fusion.3
  1259.0 6.0 copy.123
  (732 shorter events, 306.8 us)
Async XLA Ops:
  7.2 41.7 %all-gather.18.cloned.1.call-start = ((), (), s32[]{:S(2)}) async-start(), calls=%async_computation.5 | async-start | bytes 2654208 | tf_op jit(solution)/shard_map/all_gather | solution.py:420
  11.2 93.4 %all-gather.16.cloned.1.call-start = ((), (), s32[]{:S(2)}) async-start(), calls=%async_computation.4 | async-start | bytes 1216512 | tf_op jit(solution)/shard_map/all_gather | solution.py:419
  12.0 155.4 %all-gather.8.cloned.1.call-start = ((), (), s32[]{:S(2)}) async-start(), calls=%async_computation | async-start | bytes 3649536 | tf_op jit(solution)/shard_map/all_gather | solution.py:419
  13.6 218.4 %all-gather.10.cloned.1.call-start = ((), (), s32[]{:S(2)}) async-start(), calls=%async_computation.1 | async-start | bytes 3649536 | tf_op jit(solution)/shard_map/all_gather | solution.py:419
  15.6 283.2 %all-gather.12.cloned.1.call-start = ((), (), s32[]{:S(2)}) async-start(), calls=%async_computation.2 | async-start | bytes 4866048 | tf_op jit(solution)/shard_map/all_gather | solution.py:419
  17.3 346.7 %all-gather.14.cloned.1.call-start = ((), (), s32[]{:S(2)}) async-start(), calls=%async_computation.3 | async-start | bytes 4866048 | tf_op jit(solution)/shard_map/all_gather | solution.py:419
  19.0 449.9 %all-gather.20.cloned.1.call-start = ((), (), s32[]{:S(2)}) async-start(), calls=%async_computation.6 | async-start | bytes 14598144 | tf_op jit(solution)/shard_map/all_gather | solution.py:419
  21.2 819.8 %all-reduce.9.cloned.1.call-start = ((), (), s32[]{:S(2)}) async-start(), calls=%async_computation.7 | async-start | bytes 147456 | tf_op jit(solution)/shard_map/psum | solution.py:799
  25.5 16.2 %collective-permute-start = (bf16[552,256]{1,0:T(8,128)(2,1)S(1)}, bf16[552,256]{1,0:T(8,128)(2,1)S(1)}, u32[]{:S(2)}, u32[]{:S(2)}) collective-permute-start(bf16[552,256]{1,0:T(8,128)(2,1)S(1)} %pad_maximum_fusion.28), channel_id=1, source_target_pairs={{0,1},{1,0},{2,3},{3,2},{4,5},{5,4},{6,7},{7,6},{8,9},{9,8},{10,11... | collective-permute-start | bytes 847880 | tf_op jit(solution)/shard_map/ppermute | solution.py:427
  26.9 13.4 %collective-permute-start.2 = (s32[1,6]{0,1:T(8,128)S(1)}, s32[1,6]{0,1:T(8,128)S(1)}, u32[]{:S(2)}, u32[]{:S(2)}) collective-permute-start(s32[1,6]{0,1:T(8,128)S(1)} %fusion.247), channel_id=1, source_target_pairs={{0,1},{1,0},{2,3},{3,2},{4,5},{5,4},{6,7},{7,6},{8,9},{9,8},{10,11... | collective-permute-start | bytes 80 | tf_op jit(solution)/shard_map/ppermute | solution.py:401
  173.6 60.7 %collective-permute-start.1 = (bf16[512,1536]{1,0:T(8,128)(2,1)}, bf16[512,1536]{1,0:T(8,128)(2,1)}, u32[]{:S(2)}, u32[]{:S(2)}) collective-permute-start(bf16[512,1536]{1,0:T(8,128)(2,1)} %pad_maximum_fusion.21), channel_id=1, source_target_pairs={{0,1},{1,0},{2,3},{3,2},{4,5},{5,4},{6,7},{7,6},{8,9},{9,8},{10,11... | collective-permute-start | bytes 4718600 | tf_op jit(solution)/shard_map/ppermute | solution.py:395
  206.3 28.0 %copy-start.58 = (bf16[512,768]{1,0:T(8,128)(2,1)S(1)}, bf16[512,768]{1,0:T(8,128)(2,1)}, u32[]{:S(2)}) copy-start(bf16[512,768]{1,0:T(8,128)(2,1)} %copy-done.57) | copy-start | bytes 2359300
  234.3 244.2 %copy-start.28 = (bf16[512,768]{1,0:T(8,128)(2,1)}, bf16[512,768]{1,0:T(8,128)(2,1)S(1)}, u32[]{:S(2)}) copy-start(bf16[512,768]{1,0:T(8,128)(2,1)S(1)} %add_convert_fusion.9) | copy-start | bytes 2359300
  259.5 58.6 %copy-start.100 = (f32[512]{0:T(512)}, f32[512]{0:T(512)S(1)}, u32[]{:S(2)}) copy-start(f32[512]{0:T(512)S(1)} %multiply_reduce_fusion.4) | copy-start | bytes 6148
  373.8 2.5 collective-permute-start.3
  498.6 6.9 collective-permute-start.4
  502.3 342.9 %collective-permute-start.26 = (bf16[514,2304]{1,0:T(8,128)(2,1)}, bf16[514,2304]{1,0:T(8,128)(2,1)}, u32[]{:S(2)}, u32[]{:S(2)}) collective-permute-start(bf16[514,2304]{1,0:T(8,128)(2,1)} %fusion.35), channel_id=1, source_target_pairs={{0,2},{2,0},{4,6},{6,4},{8,10},{10,8},{12,14},{14,12},{16,18},{18,... | collective-permute-start | bytes 7105544 | tf_op jit(solution)/shard_map/ppermute | solution.py:390
  620.7 32.8 %copy-start.48 = (bf16[512,768]{1,0:T(8,128)(2,1)}, bf16[512,768]{1,0:T(8,128)(2,1)S(1)}, u32[]{:S(2)}) copy-start(bf16[512,768]{1,0:T(8,128)(2,1)S(1)} %get-tuple-element.180) | copy-start | bytes 2359300
  622.4 27.5 %copy-start.17 = (bf16[512,768]{1,0:T(8,128)(2,1)S(1)}, bf16[512,768]{1,0:T(8,128)(2,1)}, u32[]{:S(2)}) copy-start(bf16[512,768]{1,0:T(8,128)(2,1)} %param.37) | copy-start | bytes 2359300
  661.7 55.7 %collective-permute-start.5 = (bf16[512,1536]{1,0:T(8,128)(2,1)}, bf16[512,1536]{1,0:T(8,128)(2,1)}, u32[]{:S(2)}, u32[]{:S(2)}) collective-permute-start(bf16[512,1536]{1,0:T(8,128)(2,1)} %slice.726), channel_id=1, source_target_pairs={{0,1},{1,0},{2,3},{3,2},{4,5},{5,4},{6,7},{7,6},{8,9},{9,8},{10,11... | collective-permute-start | bytes 4718600 | tf_op jit(solution)/shard_map/ppermute | solution.py:395
  666.8 47.6 %collective-permute-start.7 = (bf16[640,1152]{1,0:T(8,128)(2,1)}, bf16[640,1152]{1,0:T(8,128)(2,1)}, u32[]{:S(2)}, u32[]{:S(2)}) collective-permute-start(bf16[640,1152]{1,0:T(8,128)(2,1)} %fusion.57), channel_id=1, source_target_pairs={{0,2},{2,0},{4,6},{6,4},{8,10},{10,8},{12,14},{14,12},{16,18},{18,... | collective-permute-start | bytes 4423688 | tf_op jit(solution)/shard_map/ppermute | solution.py:390
  692.4 20.5 %collective-permute-start.8 = (bf16[2,256,256]{2,1,0:T(8,128)(2,1)}, bf16[2,256,256]{2,1,0:T(8,128)(2,1)S(1)}, u32[]{:S(2)}, u32[]{:S(2)}) collective-permute-start(bf16[2,256,256]{2,1,0:T(8,128)(2,1)} %fusion.197), channel_id=1, source_target_pairs={{0,2},{2,0},{4,6},{6,4},{8,10},{10,8},{12,14},{14,12},{16,18},{18,... | collective-permute-start | bytes 786440 | tf_op jit(solution)/shard_map/ppermute | solution.py:390
  698.7 283.3 %collective-permute-start.17 = (bf16[512,8064]{1,0:T(8,128)(2,1)}, bf16[512,8064]{1,0:T(8,128)(2,1)}, u32[]{:S(2)}, u32[]{:S(2)}) collective-permute-start(bf16[512,8064]{1,0:T(8,128)(2,1)} %dynamic-slice_dynamic-update-slice_fusion.1), channel_id=1, source_target_pairs={{0,2},{2,0},{4,6},{6,4},{8,10},{10,8},{12,14},{14,12},{16,18},{18,... | collective-permute-start | bytes 24772616 | tf_op jit(solution)/shard_map/ppermute | solution.py:390
  722.2 146.1 %collective-permute-start.6 = (bf16[512,3072]{1,0:T(8,128)(2,1)}, bf16[512,3072]{1,0:T(8,128)(2,1)}, u32[]{:S(2)}, u32[]{:S(2)}) collective-permute-start(bf16[512,3072]{1,0:T(8,128)(2,1)} %dynamic-slice_dynamic-update-slice_fusion.4), channel_id=1, source_target_pairs={{0,2},{2,0},{4,6},{6,4},{8,10},{10,8},{12,14},{14,12},{16,18},{18,... | collective-permute-start | bytes 9437192 | tf_op jit(solution)/shard_map/ppermute | solution.py:390
  857.3 77.0 %collective-permute-start.27 = (bf16[2304,768]{1,0:T(8,128)(2,1)S(1)}, bf16[2304,768]{1,0:T(8,128)(2,1)S(1)}, u32[]{:S(2)}, u32[]{:S(2)}) collective-permute-start(bf16[2304,768]{1,0:T(8,128)(2,1)S(1)} %pad_maximum_fusion), channel_id=1, source_target_pairs={{0,1},{1,0},{2,3},{3,2},{4,5},{5,4},{6,7},{7,6},{8,9},{9,8},{10,11... | collective-permute-start | bytes 10616840 | tf_op jit(solution)/shard_map/ppermute | solution.py:395
  884.2 95.4 %collective-permute-start.9 = (bf16[2752,384]{1,0:T(8,128)(2,1)}, bf16[2752,384]{1,0:T(8,128)(2,1)S(1)}, u32[]{:S(2)}, u32[]{:S(2)}) collective-permute-start(bf16[2752,384]{1,0:T(8,128)(2,1)} %pad_dynamic-update-slice_fusion.1), channel_id=1, source_target_pairs={{0,1},{1,0},{2,3},{3,2},{4,5},{5,4},{6,7},{7,6},{8,9},{9,8},{10,11... | collective-permute-start | bytes 6340616 | tf_op jit(solution)/shard_map/ppermute | solution.py:395
  935.6 45.8 %collective-permute-start.28 = (bf16[1152,768]{1,0:T(8,128)(2,1)S(1)}, bf16[1152,768]{1,0:T(8,128)(2,1)S(1)}, u32[]{:S(2)}, u32[]{:S(2)}) collective-permute-start(bf16[1152,768]{1,0:T(8,128)(2,1)S(1)} %dynamic-slice_convert_fusion), channel_id=1, source_target_pairs={{0,4},{2,6},{4,0},{6,2},{8,12},{10,14},{12,8},{14,10},{16,20},{18,... | collective-permute-start | bytes 5308424 | tf_op jit(solution)/shard_map/ppermute | solution.py:390
  980.1 25.0 %collective-permute-start.10 = (bf16[1376,384]{1,0:T(8,128)(2,1)S(1)}, bf16[1376,384]{1,0:T(8,128)(2,1)S(1)}, u32[]{:S(2)}, u32[]{:S(2)}) collective-permute-start(bf16[1376,384]{1,0:T(8,128)(2,1)S(1)} %dynamic-slice_convert_fusion.3), channel_id=1, source_target_pairs={{0,4},{2,6},{4,0},{6,2},{8,12},{10,14},{12,8},{14,10},{16,20},{18,... | collective-permute-start | bytes 3170312 | tf_op jit(solution)/shard_map/ppermute | solution.py:390
  981.9 38.6 %collective-permute-start.29 = (bf16[576,768]{1,0:T(8,128)(2,1)S(1)}, bf16[576,768]{1,0:T(8,128)(2,1)S(1)}, u32[]{:S(2)}, u32[]{:S(2)}) collective-permute-start(bf16[576,768]{1,0:T(8,128)(2,1)S(1)} %dynamic-slice_convert_fusion.4), channel_id=1, source_target_pairs={{0,8},{2,10},{4,12},{6,14},{8,0},{10,2},{12,4},{14,6},{16,24},{18,... | collective-permute-start | bytes 2654216 | tf_op jit(solution)/shard_map/ppermute | solution.py:390
  1004.7 62.8 %collective-permute-start.18 = (bf16[3840,384]{1,0:T(8,128)(2,1)S(1)}, bf16[3840,384]{1,0:T(8,128)(2,1)}, u32[]{:S(2)}, u32[]{:S(2)}) collective-permute-start(bf16[3840,384]{1,0:T(8,128)(2,1)S(1)} %pad_maximum_fusion.4), channel_id=1, source_target_pairs={{0,1},{1,0},{2,3},{3,2},{4,5},{5,4},{6,7},{7,6},{8,9},{9,8},{10,11... | collective-permute-start | bytes 8847368 | tf_op jit(solution)/shard_map/ppermute | solution.py:395
  1005.4 10.4 collective-permute-start.11
  1016.0 24.4 %collective-permute-start.12 = (bf16[344,384]{1,0:T(8,128)(2,1)S(1)}, bf16[344,384]{1,0:T(8,128)(2,1)S(1)}, u32[]{:S(2)}, u32[]{:S(2)}) collective-permute-start(bf16[344,384]{1,0:T(8,128)(2,1)S(1)} %dynamic-slice_convert_fusion.12), channel_id=1, source_target_pairs={{0,16},{2,18},{4,20},{6,22},{8,24},{10,26},{12,28},{14,30},{16,0},... | collective-permute-start | bytes 792584 | tf_op jit(solution)/shard_map/ppermute | solution.py:390
  1022.6 52.9 %collective-permute-start.30 = (bf16[288,768]{1,0:T(8,128)(2,1)}, bf16[288,768]{1,0:T(8,128)(2,1)}, u32[]{:S(2)}, u32[]{:S(2)}) collective-permute-start(bf16[288,768]{1,0:T(8,128)(2,1)} %dynamic-slice_convert_fusion.7), channel_id=1, source_target_pairs={{0,16},{2,18},{4,20},{6,22},{8,24},{10,26},{12,28},{14,30},{16,0},... | collective-permute-start | bytes 1327112 | tf_op jit(solution)/shard_map/ppermute | solution.py:390
  1041.2 39.9 %collective-permute-start.13 = (bf16[344,384]{1,0:T(8,128)(2,1)}, bf16[344,384]{1,0:T(8,128)(2,1)}, u32[]{:S(2)}, u32[]{:S(2)}) collective-permute-start(bf16[344,384]{1,0:T(8,128)(2,1)} %add_convert_fusion.18), channel_id=1, source_target_pairs={{0,16},{2,18},{4,20},{6,22},{8,24},{10,26},{12,28},{14,30},{16,0},... | collective-permute-start | bytes 792584 | tf_op jit(solution)/shard_map/ppermute | solution.py:390
  1075.2 30.1 %collective-permute-start.19 = (bf16[1920,384]{1,0:T(8,128)(2,1)S(1)}, bf16[1920,384]{1,0:T(8,128)(2,1)S(1)}, u32[]{:S(2)}, u32[]{:S(2)}) collective-permute-start(bf16[1920,384]{1,0:T(8,128)(2,1)S(1)} %dynamic-slice_convert_fusion.1), channel_id=1, source_target_pairs={{0,4},{2,6},{4,0},{6,2},{8,12},{10,14},{12,8},{14,10},{16,20},{18,... | collective-permute-start | bytes 4423688 | tf_op jit(solution)/shard_map/ppermute | solution.py:390
  1076.7 22.8 %collective-permute-start.31 = (bf16[288,768]{1,0:T(8,128)(2,1)S(1)}, bf16[288,768]{1,0:T(8,128)(2,1)S(1)}, u32[]{:S(2)}, u32[]{:S(2)}) collective-permute-start(bf16[288,768]{1,0:T(8,128)(2,1)S(1)} %add_convert_fusion.14), channel_id=1, source_target_pairs={{0,16},{2,18},{4,20},{6,22},{8,24},{10,26},{12,28},{14,30},{16,0},... | collective-permute-start | bytes 1327112 | tf_op jit(solution)/shard_map/ppermute | solution.py:390
  1082.2 20.4 %collective-permute-start.14 = (bf16[688,384]{1,0:T(8,128)(2,1)S(1)}, bf16[688,384]{1,0:T(8,128)(2,1)S(1)}, u32[]{:S(2)}, u32[]{:S(2)}) collective-permute-start(bf16[688,384]{1,0:T(8,128)(2,1)S(1)} %pad_maximum_fusion.26), channel_id=1, source_target_pairs={{0,8},{2,10},{4,12},{6,14},{8,0},{10,2},{12,4},{14,6},{16,24},{18,... | collective-permute-start | bytes 1585160 | tf_op jit(solution)/shard_map/ppermute | solution.py:390
  1099.6 23.3 %collective-permute-start.32 = (bf16[576,768]{1,0:T(8,128)(2,1)S(1)}, bf16[576,768]{1,0:T(8,128)(2,1)S(1)}, u32[]{:S(2)}, u32[]{:S(2)}) collective-permute-start(bf16[576,768]{1,0:T(8,128)(2,1)S(1)} %pad_maximum_fusion.24), channel_id=1, source_target_pairs={{0,8},{2,10},{4,12},{6,14},{8,0},{10,2},{12,4},{14,6},{16,24},{18,... | collective-permute-start | bytes 2654216 | tf_op jit(solution)/shard_map/ppermute | solution.py:390
  1105.8 32.9 %collective-permute-start.20 = (bf16[960,384]{1,0:T(8,128)(2,1)S(1)}, bf16[960,384]{1,0:T(8,128)(2,1)S(1)}, u32[]{:S(2)}, u32[]{:S(2)}) collective-permute-start(bf16[960,384]{1,0:T(8,128)(2,1)S(1)} %dynamic-slice_convert_fusion.5), channel_id=1, source_target_pairs={{0,8},{2,10},{4,12},{6,14},{8,0},{10,2},{12,4},{14,6},{16,24},{18,... | collective-permute-start | bytes 2211848 | tf_op jit(solution)/shard_map/ppermute | solution.py:390
  1108.0 31.0 %collective-permute-start.15 = (bf16[1376,384]{1,0:T(8,128)(2,1)S(1)}, bf16[1376,384]{1,0:T(8,128)(2,1)S(1)}, u32[]{:S(2)}, u32[]{:S(2)}) collective-permute-start(bf16[1376,384]{1,0:T(8,128)(2,1)S(1)} %pad_maximum_fusion.23), channel_id=1, source_target_pairs={{0,4},{2,6},{4,0},{6,2},{8,12},{10,14},{12,8},{14,10},{16,20},{18,... | collective-permute-start | bytes 3170312 | tf_op jit(solution)/shard_map/ppermute | solution.py:390
  1123.4 52.3 %collective-permute-start.33 = (bf16[1152,768]{1,0:T(8,128)(2,1)S(1)}, bf16[1152,768]{1,0:T(8,128)(2,1)S(1)}, u32[]{:S(2)}, u32[]{:S(2)}) collective-permute-start(bf16[1152,768]{1,0:T(8,128)(2,1)S(1)} %pad_maximum_fusion.7), channel_id=1, source_target_pairs={{0,4},{2,6},{4,0},{6,2},{8,12},{10,14},{12,8},{14,10},{16,20},{18,... | collective-permute-start | bytes 5308424 | tf_op jit(solution)/shard_map/ppermute | solution.py:390
  1138.9 15.0 %collective-permute-start.21 = (bf16[480,384]{1,0:T(8,128)(2,1)S(1)}, bf16[480,384]{1,0:T(8,128)(2,1)S(1)}, u32[]{:S(2)}, u32[]{:S(2)}) collective-permute-start(bf16[480,384]{1,0:T(8,128)(2,1)S(1)} %dynamic-slice_convert_fusion.10), channel_id=1, source_target_pairs={{0,16},{2,18},{4,20},{6,22},{8,24},{10,26},{12,28},{14,30},{16,0},... | collective-permute-start | bytes 1105928 | tf_op jit(solution)/shard_map/ppermute | solution.py:390
  1154.2 17.2 %collective-permute-start.22 = (bf16[480,384]{1,0:T(8,128)(2,1)S(1)}, bf16[480,384]{1,0:T(8,128)(2,1)S(1)}, u32[]{:S(2)}, u32[]{:S(2)}) collective-permute-start(bf16[480,384]{1,0:T(8,128)(2,1)S(1)} %add_convert_fusion.15), channel_id=1, source_target_pairs={{0,16},{2,18},{4,20},{6,22},{8,24},{10,26},{12,28},{14,30},{16,0},... | collective-permute-start | bytes 1105928 | tf_op jit(solution)/shard_map/ppermute | solution.py:390
  1157.6 36.3 %collective-permute-start.16 = (bf16[2752,384]{1,0:T(8,128)(2,1)S(1)}, bf16[2752,384]{1,0:T(8,128)(2,1)S(1)}, u32[]{:S(2)}, u32[]{:S(2)}) collective-permute-start(bf16[2752,384]{1,0:T(8,128)(2,1)S(1)} %pad_maximum_fusion.6), channel_id=1, source_target_pairs={{0,2},{2,0},{4,6},{6,4},{8,10},{10,8},{12,14},{14,12},{16,18},{18,... | collective-permute-start | bytes 6340616 | tf_op jit(solution)/shard_map/ppermute | solution.py:390
  1171.6 20.6 %collective-permute-start.23 = (bf16[960,384]{1,0:T(8,128)(2,1)S(1)}, bf16[960,384]{1,0:T(8,128)(2,1)S(1)}, u32[]{:S(2)}, u32[]{:S(2)}) collective-permute-start(bf16[960,384]{1,0:T(8,128)(2,1)S(1)} %pad_maximum_fusion.25), channel_id=1, source_target_pairs={{0,8},{2,10},{4,12},{6,14},{8,0},{10,2},{12,4},{14,6},{16,24},{18,... | collective-permute-start | bytes 2211848 | tf_op jit(solution)/shard_map/ppermute | solution.py:390
  1176.7 57.7 %collective-permute-start.34 = (bf16[2304,768]{1,0:T(8,128)(2,1)S(1)}, bf16[2304,768]{1,0:T(8,128)(2,1)S(1)}, u32[]{:S(2)}, u32[]{:S(2)}) collective-permute-start(bf16[2304,768]{1,0:T(8,128)(2,1)S(1)} %pad_maximum_fusion.1), channel_id=1, source_target_pairs={{0,2},{2,0},{4,6},{6,4},{8,10},{10,8},{12,14},{14,12},{16,18},{18,... | collective-permute-start | bytes 10616840 | tf_op jit(solution)/shard_map/ppermute | solution.py:390
  1192.6 32.8 %collective-permute-start.24 = (bf16[1920,384]{1,0:T(8,128)(2,1)S(1)}, bf16[1920,384]{1,0:T(8,128)(2,1)S(1)}, u32[]{:S(2)}, u32[]{:S(2)}) collective-permute-start(bf16[1920,384]{1,0:T(8,128)(2,1)S(1)} %pad_maximum_fusion.22), channel_id=1, source_target_pairs={{0,4},{2,6},{4,0},{6,2},{8,12},{10,14},{12,8},{14,10},{16,20},{18,... | collective-permute-start | bytes 4423688 | tf_op jit(solution)/shard_map/ppermute | solution.py:390
  1228.0 18.3 %collective-permute-start.25 = (bf16[3840,384]{1,0:T(8,128)(2,1)}, bf16[3840,384]{1,0:T(8,128)(2,1)}, u32[]{:S(2)}, u32[]{:S(2)}) collective-permute-start(bf16[3840,384]{1,0:T(8,128)(2,1)} %pad_maximum_fusion.5), channel_id=1, source_target_pairs={{0,2},{2,0},{4,6},{6,4},{8,10},{10,8},{12,14},{14,12},{16,18},{18,... | collective-permute-start | bytes 8847368 | tf_op jit(solution)/shard_map/ppermute | solution.py:390
  (147 other events, 779.9 us)
Sparse Core Ops, SparseCore 0:
  11.3 36.6 all-gather.17
  51.5 53.0 all-gather.15
  108.1 59.1 all-gather.7
  170.8 61.2 all-gather.9
  235.4 63.4 all-gather.11
  301.6 62.3 all-gather.13
  367.5 101.3 all-gather.19
  723.3 117.6 all-reduce.8

commit v2 on v1

v2 whole, which is shorter than its diff:
```python
import functools
import jax
import jax.numpy as jnp
from jax import lax
from jax.sharding import PartitionSpec as P
from jax.experimental import pallas as pl
from jax.experimental.pallas import tpu as pltpu

F32 = jnp.float32
BF16 = jnp.bfloat16
VMEM_BYTES = 60 * 1024 * 1024
LIGHT = pl.CostEstimate(flops=1024, bytes_accessed=1024, transcendentals=0)


def dot(left, right):
    return jnp.dot(left, right, preferred_element_type=F32)


def dot_nt(left, right):
    return lax.dot_general(left, right, (((1,), (1,)), ((), ())), preferred_element_type=F32)


def dot_tn(left, right):
    return lax.dot_general(left, right, (((0,), (0,)), ((), ())), preferred_element_type=F32)


def sigmoid(values):
    return 0.5 * jnp.tanh(0.5 * values) + 0.5


def chunks(rows):
    size = min(rows, 256)
    return [slice(start, start + size) for start in range(0, rows, size)]


def gru_specs(slots, rows, chars, gate_width, at):
    hid = gate_width // 3
    whole = lambda *shape: pl.BlockSpec(shape, lambda i: (0,) * len(shape))
    letters = lambda place: pl.BlockSpec((1, rows, chars), lambda i: (place(at(i)), 0, 0))
    last = slots - 1
    return [
        letters(lambda t: jnp.minimum(t, last)),
        letters(lambda t: jnp.maximum(last - t, 0)),
        letters(lambda t: jnp.maximum(t - slots, 0)),
        letters(lambda t: jnp.minimum(2 * slots - 1 - t, last)),
        whole(2, chars, gate_width),
        whole(2, hid, gate_width),
        whole(2, 1, gate_width),
        whole(2, 1, gate_width),
        whole(3, rows, 1),
        whole(2, rows, 1),
    ]


def gru_gates(letter, start_low, wi, wr, bi, br, hid):
    both = 2 * hid
    mixed = dot(letter, wi[:, :both]) + dot(start_low, wr[:, :both]) + (bi[:, :both] + br[:, :both])
    reset = sigmoid(mixed[:, :hid])
    update = sigmoid(mixed[:, hid:])
    carried = dot(start_low, wr[:, both:]) + br[:, both:]
    candidate = jnp.tanh(dot(letter, wi[:, both:]) + bi[:, both:] + reset * carried)
    return reset, update, candidate, carried


def gru_forward_kernel(slots, a0, a1, b0, b1, wi, wr, bi, br, counts, keep, starts, pooled, state):
    step = pl.program_id(0)
    rows, hid = state.shape[1], state.shape[2]

    @pl.when(step == 0)
    def _():
        state[...] = jnp.zeros_like(state)

    @pl.when(step == slots)
    def _():
        for way in range(2):
            state[way] = state[way] * keep[way]

    first = step < slots
    place = jnp.where(first, step, step - slots)
    for part in chunks(rows):
        for way, (near, own) in enumerate(((a0, b0), (a1, b1))):
            letter = jnp.where(first, near[0, part], own[0, part])
            start = state[way, part]
            starts[0, way, part] = start
            _, update, candidate, _ = gate_values = gru_gates(
                letter, start.astype(BF16), wi[way], wr[way], bi[way], br[way], hid
            )
            fresh = candidate + update * (start - candidate)
            slot = place if way == 0 else slots - 1 - place
            count = jnp.where(first, counts[way, part], counts[2, part])
            state[way, part] = jnp.where(slot < count, fresh, start)

    @pl.when(step == 2 * slots - 1)
    def _():
        for way in range(2):
            pooled[:, way * hid : (way + 1) * hid] = state[way].astype(BF16)


def gru_forward(letters, wi, wr, bi, br, counts, keep):
    near0, near1, own = letters
    slots, rows, chars = own.shape
    gate_width = wi.shape[-1]
    hid = gate_width // 3
    return pl.pallas_call(
        functools.partial(gru_forward_kernel, slots),
        grid=(2 * slots,),
        in_specs=gru_specs(slots, rows, chars, gate_width, lambda i: i),
        out_specs=[
            pl.BlockSpec((1, 2, rows, hid), lambda i: (i, 0, 0, 0)),
            pl.BlockSpec((rows, 2 * hid), lambda i: (0, 0)),
        ],
        out_shape=[
            jax.ShapeDtypeStruct((2 * slots, 2, rows, hid), F32),
            jax.ShapeDtypeStruct((rows, 2 * hid), BF16),
        ],
        scratch_shapes=[pltpu.VMEM((2, rows, hid), F32)],
        compiler_params=pltpu.CompilerParams(vmem_limit_bytes=VMEM_BYTES),
        cost_estimate=LIGHT,
        name="gru_forward",
    )(near0, near1, own, own, wi, wr, bi, br, counts, keep)


def gru_backward_kernel(slots, last, x0, x1, wi, wr, bi, br, counts, keep, starts, final, *refs):
    sums, refs = (None, refs) if last else (refs[:4], refs[4:])
    letter_grads, (start_grad, wi_grad, wr_grad, bi_grad, br_grad) = refs[:2], refs[2:]
    back = pl.program_id(0)
    place = slots - 1 - back
    rows, hid = final.shape[1], final.shape[2]
    both = 2 * hid

    @pl.when(back == 0)
    def _():
        start_grad[...] = final[...]
        for k, total in enumerate((wi_grad, wr_grad, bi_grad, br_grad)):
            total[...] = jnp.zeros_like(total) if last else sums[k][...]

    for part in chunks(rows):
        for way, letters in enumerate((x0, x1)):
            letter = letters[0, part]
            start = starts[0, way, part]
            start_low = start.astype(BF16)
            reset, update, candidate, carried = gru_gates(
                letter, start_low, wi[way], wr[way], bi[way], br[way], hid
            )
            slot = place if way == 0 else slots - 1 - place
            grad = start_grad[way, part]
            fresh = jnp.where(slot < counts[way, part], grad, 0.0)
            kept = grad - fresh
            scaled = fresh * (1.0 - update)
            cand_pre = scaled * (1.0 - candidate * candidate)
            update_pre = scaled * update * (start - candidate)
            cand_reset = cand_pre * reset
            reset_pre = cand_reset * carried * (1.0 - reset)
            shared = jnp.concatenate([reset_pre.astype(BF16), update_pre.astype(BF16)], axis=1)
            cand_in = cand_pre.astype(BF16)
            cand_rec = cand_reset.astype(BF16)
            start_grad[way, part] = (
                kept
                + update * fresh
                + dot_nt(shared, wr[way, :, :both])
                + dot_nt(cand_rec, wr[way, :, both:])
            )
            letter_grads[way][0, part] = (
                dot_nt(shared, wi[way, :, :both]) + dot_nt(cand_in, wi[way, :, both:])
            ).astype(BF16)
            wi_grad[way, :, :both] += dot_tn(letter, shared)
            wi_grad[way, :, both:] += dot_tn(letter, cand_in)
            wr_grad[way, :, :both] += dot_tn(start_low, shared)
            wr_grad[way, :, both:] += dot_tn(start_low, cand_rec)
            total = jnp.sum(shared.astype(F32), axis=0, keepdims=True)
            bi_grad[way, :, :both] += total
            br_grad[way, :, :both] += total
            bi_grad[way, :, both:] += jnp.sum(cand_in.astype(F32), axis=0, keepdims=True)
            br_grad[way, :, both:] += jnp.sum(cand_rec.astype(F32), axis=0, keepdims=True)

    if last:

        @pl.when(back == slots - 1)
        def _():
            for way in range(2):
                start_grad[way] = start_grad[way] * keep[way]


def gru_backward(last, near0, near1, wi, wr, bi, br, counts, keep, starts, final, sums=()):
    slots, rows, chars = near0.shape
    gate_width = wi.shape[-1]
    hid = gate_width // 3
    offset = slots if last else 0
    whole = lambda *shape: pl.BlockSpec(shape, lambda i: (0,) * len(shape))
    return pl.pallas_call(
        functools.partial(gru_backward_kernel, slots, last),
        grid=(slots,),
        in_specs=[
            pl.BlockSpec((1, rows, chars), lambda i: (slots - 1 - i, 0, 0)),
            pl.BlockSpec((1, rows, chars), lambda i: (i, 0, 0)),
            whole(2, chars, gate_width),
            whole(2, hid, gate_width),
            whole(2, 1, gate_width),
            whole(2, 1, gate_width),
            whole(2, rows, 1),
            whole(2, rows, 1),
            pl.BlockSpec((1, 2, rows, hid), lambda i: (offset + slots - 1 - i, 0, 0, 0)),
            whole(2, rows, hid),
        ]
        + [whole(*item.shape) for item in sums],
        out_specs=[
            pl.BlockSpec((1, rows, chars), lambda i: (slots - 1 - i, 0, 0)),
            pl.BlockSpec((1, rows, chars), lambda i: (i, 0, 0)),
            whole(2, rows, hid),
            whole(2, chars, gate_width),
            whole(2, hid, gate_width),
            whole(2, 1, gate_width),
            whole(2, 1, gate_width),
        ],
        out_shape=[
            jax.ShapeDtypeStruct((slots, rows, chars), BF16),
            jax.ShapeDtypeStruct((slots, rows, chars), BF16),
            jax.ShapeDtypeStruct((2, rows, hid), F32),
            jax.ShapeDtypeStruct((2, chars, gate_width), F32),
            jax.ShapeDtypeStruct((2, hid, gate_width), F32),
            jax.ShapeDtypeStruct((2, 1, gate_width), F32),
            jax.ShapeDtypeStruct((2, 1, gate_width), F32),
        ],
        compiler_params=pltpu.CompilerParams(vmem_limit_bytes=VMEM_BYTES),
        cost_estimate=LIGHT,
        name="gru_backward",
    )(near0, near1, wi, wr, bi, br, counts, keep, starts, final, *sums)


def half_spec(item, place):
    if item.ndim == 3:
        return pl.BlockSpec((1,) + item.shape[1:], lambda i, w: (place(i, w)[0], place(i, w)[1], 0))
    rows, lanes = item.shape
    return pl.BlockSpec((rows, lanes // 2), lambda i, w: (place(i, w)[1], place(i, w)[0]))


def flat2(ref):
    return ref.at[0] if len(ref.shape) == 3 else ref


def pack_kernel(width, where, *refs):
    out, at = refs[-1], 0
    for ref in refs[:-1]:
        item = flat2(ref)
        rows, lanes = item.shape
        for lane in range(0, lanes, width):
            out[at : at + rows, :] = item[:, lane : lane + width].astype(BF16)
            at += rows


def pack_halves(core, masters, width):
    total = sum(item.size for item in masters) // 2 // width
    where = jnp.stack([core, core])
    return pl.pallas_call(
        functools.partial(pack_kernel, width),
        grid_spec=pltpu.PrefetchScalarGridSpec(
            num_scalar_prefetch=1,
            grid=(1,),
            in_specs=[half_spec(item, lambda i, w: (w[0], 0)) for item in masters],
            out_specs=pl.BlockSpec((total, width), lambda i, w: (0, 0)),
        ),
        out_shape=jax.ShapeDtypeStruct((total, width), BF16),
        compiler_params=pltpu.CompilerParams(vmem_limit_bytes=VMEM_BYTES),
        cost_estimate=LIGHT,
        name="pack_halves",
    )(where, *masters)


def table_kernel(ids, near0, near1, own0, own1, out):
    @pl.when(pl.program_id(0) == 0)
    def _():
        out[...] = jnp.zeros_like(out)

    own = (own0[0].astype(F32) + own1[0].astype(F32)).astype(BF16)
    rows, vocab = own.shape[0], out.shape[0]
    letters = lax.broadcasted_iota(jnp.int32, (rows, vocab), 1)
    total = None
    for which, grad in enumerate((near0[0], near1[0], own)):
        chosen = jnp.where(ids[which, 0] == letters, 1.0, 0.0).astype(BF16)
        part = dot_tn(chosen, grad)
        total = part if total is None else total + part
    out[...] += total


def table_terms_of(ids, near0, near1, own0, own1, vocab):
    slots, rows, chars = near0.shape
    one = pl.BlockSpec((1, rows, chars), lambda i: (i, 0, 0))
    return pl.pallas_call(
        table_kernel,
        grid=(slots,),
        in_specs=[pl.BlockSpec((3, 1, rows, 1), lambda i: (0, i, 0, 0)), one, one, one, one],
        out_specs=pl.BlockSpec((vocab, chars), lambda i: (0, 0)),
        out_shape=jax.ShapeDtypeStruct((vocab, chars), F32),
        compiler_params=pltpu.CompilerParams(vmem_limit_bytes=VMEM_BYTES),
        cost_estimate=LIGHT,
        name="table_terms",
    )(ids, near0, near1, own0, own1)


def block_terms_kernel(table, a0, b0, a1, b1, out):
    out[...] = (dot_tn(a0[...], b0[...]) + dot_tn(a1[...], b1[...])).astype(out.dtype)


def block_terms(left, right, table, width, dtype):
    rows, count = left[0].shape[0], table.shape[1]
    one = pl.BlockSpec((rows, width), lambda i, t: (0, t[0, i]))
    if right[0].ndim == 3:
        across = right[0].shape[2] // width
        two = pl.BlockSpec(
            (None, rows, width), lambda i, t: (t[1, i] // across, 0, t[1, i] % across)
        )
    else:
        two = pl.BlockSpec((rows, width), lambda i, t: (0, t[1, i]))
    return pl.pallas_call(
        block_terms_kernel,
        grid_spec=pltpu.PrefetchScalarGridSpec(
            num_scalar_prefetch=1,
            grid=(count,),
            in_specs=[one, two, one, two],
            out_specs=pl.BlockSpec((width, width), lambda i, t: (i, 0)),
        ),
        out_shape=jax.ShapeDtypeStruct((count * width, width), dtype),
        compiler_params=pltpu.CompilerParams(vmem_limit_bytes=VMEM_BYTES),
        cost_estimate=LIGHT,
        name="block_terms",
    )(table, left[0], right[0], left[1], right[1])


def unpack_kernel(shapes, where, mine, other, *outs):
    width = mine.shape[1]
    for turn, source in ((0, mine), (1, other)):

        @pl.when(pl.program_id(0) == turn)
        def _(source=source):
            at = 0
            for (rows, lanes, kind), out in zip(shapes, outs):
                if kind == "turned":
                    out[...] = source[at : at + rows, :].astype(F32).T
                    at += rows
                    continue
                target = out.at[0] if kind == "stacked" else out
                for lane in range(0, lanes, width):
                    some = min(width, lanes - lane)
                    target[:, lane : lane + some] = source[at : at + rows, :some].astype(F32)
                    at += rows


def unpack_halves(core, mine, other, shapes):
    where = jnp.stack([core, core])
    half = lambda i, w: jnp.where(i == 0, w[0], 1 - w[0])
    specs, outs = [], []
    for rows, lanes, kind in shapes:
        if kind == "lanes":
            specs.append(pl.BlockSpec((rows, lanes), lambda i, w: (0, half(i, w))))
            outs.append((rows, 2 * lanes))
        elif kind == "stacked":
            specs.append(pl.BlockSpec((1, rows, lanes), lambda i, w: (half(i, w), 0, 0)))
            outs.append((2, rows, lanes))
        elif kind == "rows":
            specs.append(pl.BlockSpec((rows, lanes), lambda i, w: (half(i, w), 0)))
            outs.append((2 * rows, lanes))
        else:
            specs.append(pl.BlockSpec((lanes, rows), lambda i, w: (0, half(i, w))))
            outs.append((lanes, 2 * rows))
    whole = pl.BlockSpec(mine.shape, lambda i, w: (0, 0))
    return pl.pallas_call(
        functools.partial(unpack_kernel, shapes),
        grid_spec=pltpu.PrefetchScalarGridSpec(
            num_scalar_prefetch=1, grid=(2,), in_specs=[whole, whole], out_specs=specs
        ),
        out_shape=[jax.ShapeDtypeStruct(item, F32) for item in outs],
        compiler_params=pltpu.CompilerParams(vmem_limit_bytes=VMEM_BYTES),
        cost_estimate=LIGHT,
        name="unpack_halves",
    )(where, mine, other)


def rows_kernel(width, *refs):
    out, at = refs[-1], 0
    for ref in refs[:-1]:
        rows, lanes = ref.shape
        for lane in range(0, lanes, width):
            out[at : at + rows, :] = ref[:, lane : lane + width].astype(out.dtype)
            at += rows


def pack_rows(blocks, width, dtype):
    blocks = [item if item.shape[1] % width == 0 else item.reshape(-1, width) for item in blocks]
    total = sum(item.size for item in blocks) // width
    return pl.pallas_call(
        functools.partial(rows_kernel, width),
        out_shape=jax.ShapeDtypeStruct((total, width), dtype),
        compiler_params=pltpu.CompilerParams(vmem_limit_bytes=VMEM_BYTES),
        cost_estimate=LIGHT,
        name="pack_rows",
    )(*blocks)


def gru_terms_kernel(width, where, *refs):
    out = refs[-1]
    sums, table, vectors = refs[:-3], refs[-3], refs[-2]
    parts = out.shape[0]
    out[...] = jnp.zeros_like(out)
    for part in range(parts):
        at = 0
        for item in sums:
            rows = item.shape[1] // parts
            rest = slice(part * rows, (part + 1) * rows)
            for lane in range(0, item.shape[2], width):
                out[part, at : at + rows, :] = item[0, rest, lane : lane + width].astype(out.dtype)
                at += rows
        rows, lanes = table.shape[2], table.shape[3]
        out[part, at : at + rows, :lanes] = table[part, 0].astype(out.dtype)
        at += rows
        rows = vectors.shape[2]
        out[part, at : at + rows, :] = vectors[part, 0].astype(out.dtype)


def pack_gru_terms(which, sums, table, vectors, depth, width, dtype):
    parts = table.shape[0]
    where = jnp.stack([which, which])
    chosen = lambda item: pl.BlockSpec((1,) + item.shape[1:], lambda i, w: (w[0], 0, 0))
    second = lambda item: pl.BlockSpec(
        (parts, 1) + item.shape[2:], lambda i, w: (0, w[0], 0, 0)
    )
    return pl.pallas_call(
        functools.partial(gru_terms_kernel, width),
        grid_spec=pltpu.PrefetchScalarGridSpec(
            num_scalar_prefetch=1,
            grid=(1,),
            in_specs=[chosen(item) for item in sums] + [second(table), second(vectors)],
            out_specs=pl.BlockSpec((parts, depth, width), lambda i, w: (0, 0, 0)),
        ),
        out_shape=jax.ShapeDtypeStruct((parts, depth, width), dtype),
        compiler_params=pltpu.CompilerParams(vmem_limit_bytes=VMEM_BYTES),
        cost_estimate=LIGHT,
        name="pack_gru_terms",
    )(where, *sums, table, vectors)


def join_kernel(width, count, where, *refs):
    step = pl.program_id(0)
    masters, (mine, peer), outs = refs[:count], refs[count : count + 2], refs[count + 2 :]

    @pl.when(step < 2)
    def _():
        for master, out in zip(masters, outs):
            out[...] = master[...].astype(BF16)

    for turn, source in ((2, mine), (3, peer)):

        @pl.when(step == turn)
        def _(source=source):
            at = 0
            for out in outs:
                item = flat2(out)
                rows, lanes = item.shape
                for lane in range(0, lanes, width):
                    item[:, lane : lane + width] = source[at : at + rows, :]
                    at += rows


def join_halves(place, core, masters, mine, peer, width):
    where = jnp.stack([place, core])

    def source(i, w):
        return (jnp.minimum(i, 1), 0)

    def target(i, w):
        half = jnp.where(i < 2, i, jnp.where(i == 2, w[1], 1 - w[1]))
        return (half, jnp.where(i < 2, w[0], 1 - w[0]))

    def wide(item):
        return item.shape[:-2] + (2 * item.shape[-2], item.shape[-1])

    rows = pl.BlockSpec(mine.shape, lambda i, w: (0, 0))
    return pl.pallas_call(
        functools.partial(join_kernel, width, len(masters)),
        grid_spec=pltpu.PrefetchScalarGridSpec(
            num_scalar_prefetch=1,
            grid=(4,),
            in_specs=[half_spec(item, source) for item in masters] + [rows, rows],
            out_specs=[half_spec(item, target) for item in masters],
        ),
        out_shape=[jax.ShapeDtypeStruct(wide(item), BF16) for item in masters],
        compiler_params=pltpu.CompilerParams(vmem_limit_bytes=VMEM_BYTES),
        cost_estimate=LIGHT,
        name="join_halves",
    )(where, *masters, mine, peer)


def attend_kernel(scale, q, k, v, seg_q, seg_k, out, logsum):
    pair = q.shape[1]
    half = pair // 2
    allowed = seg_k[...] == seg_q[...]
    lane = lax.broadcasted_iota(jnp.int32, (1, pair), 1)
    keys = k[...]
    values = v[...].T
    for head in range(2):
        mine = (lane < half) if head == 0 else (lane >= half)
        query = jnp.where(mine, q[...] * scale, 0).astype(BF16)
        scores = jnp.where(allowed, dot_nt(keys, query), -1e9)
        top = jnp.max(scores, axis=0, keepdims=True)
        expo = jnp.exp(scores - top)
        total = jnp.sum(expo, axis=0, keepdims=True)
        probs = (expo * (1.0 / total)).astype(BF16)
        logsum[0, head : head + 1, :] = top + jnp.log(total)
        mixed = dot(values[head * half : (head + 1) * half], probs)
        out[:, head * half : (head + 1) * half] = mixed.T.astype(BF16)


def attend(q, k, v, seg_q, seg_k, head_dim):
    rows, width = q.shape
    length = k.shape[0]
    pair = 2 * head_dim
    pairs = width // pair
    return pl.pallas_call(
        functools.partial(attend_kernel, head_dim ** -0.5),
        grid=(pairs,),
        in_specs=[
            pl.BlockSpec((rows, pair), lambda i: (0, i)),
            pl.BlockSpec((length, pair), lambda i: (0, i)),
            pl.BlockSpec((length, pair), lambda i: (0, i)),
            pl.BlockSpec((1, rows), lambda i: (0, 0)),
            pl.BlockSpec((length, 1), lambda i: (0, 0)),
        ],
        out_specs=[
            pl.BlockSpec((rows, pair), lambda i: (0, i)),
            pl.BlockSpec((1, 2, rows), lambda i: (i, 0, 0)),
        ],
        out_shape=[
            jax.ShapeDtypeStruct((rows, width), BF16),
            jax.ShapeDtypeStruct((pairs, 2, rows), F32),
        ],
        compiler_params=pltpu.CompilerParams(vmem_limit_bytes=VMEM_BYTES),
        cost_estimate=LIGHT,
        name="attend",
    )(q, k, v, seg_q, seg_k)


def attend_back_kernel(scale, q, k, v, seg_q, seg_k, grad, logsum, dq, *terms):
    pair = q.shape[1]
    half = pair // 2
    allowed = seg_k[...] == seg_q[...]
    lane = lax.broadcasted_iota(jnp.int32, (1, pair), 1)
    keys = k[...]
    values = v[...]
    keys_t = keys.T
    key_total = None
    value_total = None
    for head in range(2):
        mine = (lane < half) if head == 0 else (lane >= half)
        query = jnp.where(mine, q[...] * scale, 0).astype(BF16)
        out_grad = jnp.where(mine, grad[...], 0).astype(BF16)
        scores = jnp.where(allowed, dot_nt(keys, query), -1e9)
        probs = jnp.exp(scores - logsum[0, head : head + 1, :])
        probs_grad = dot_nt(values, out_grad)
        delta = jnp.sum(probs * probs_grad, axis=0, keepdims=True)
        scores_grad = (probs * (probs_grad - delta)).astype(BF16)
        key_part = dot(scores_grad, query)
        value_part = dot(probs.astype(BF16), out_grad)
        key_total = key_part if head == 0 else key_total + key_part
        value_total = value_part if head == 0 else value_total + value_part
        query_part = dot(keys_t[head * half : (head + 1) * half], scores_grad)
        dq[:, head * half : (head + 1) * half] = (query_part.T * scale).astype(BF16)
    for part, out in enumerate(terms):
        rows = slice(part * out.shape[1], (part + 1) * out.shape[1])
        out[0] = key_total[rows].astype(BF16)
        out[1] = value_total[rows].astype(BF16)


def attend_back(q, k, v, seg_q, seg_k, grad, logsum, head_dim):
    rows, width = q.shape
    length = k.shape[0]
    pair = 2 * head_dim
    pairs = width // pair
    return pl.pallas_call(
        functools.partial(attend_back_kernel, head_dim ** -0.5),
        grid=(pairs,),
        in_specs=[
            pl.BlockSpec((rows, pair), lambda i: (0, i)),
            pl.BlockSpec((length, pair), lambda i: (0, i)),
            pl.BlockSpec((length, pair), lambda i: (0, i)),
            pl.BlockSpec((1, rows), lambda i: (0, 0)),
            pl.BlockSpec((length, 1), lambda i: (0, 0)),
            pl.BlockSpec((rows, pair), lambda i: (0, i)),
            pl.BlockSpec((1, 2, rows), lambda i: (i, 0, 0)),
        ],
        out_specs=[
            pl.BlockSpec((rows, pair), lambda i: (0, i)),
        ]
        + [pl.BlockSpec((2, rows, pair), lambda i: (0, 0, i))] * (length // rows),
        out_shape=[jax.ShapeDtypeStruct((rows, width), BF16)]
        + [jax.ShapeDtypeStruct((2, rows, width), BF16)] * (length // rows),
        compiler_params=pltpu.CompilerParams(vmem_limit_bytes=VMEM_BYTES),
        cost_estimate=LIGHT,
        name="attend_back",
    )(q, k, v, seg_q, seg_k, grad, logsum)


HEAD_DIM = 64
PACK = 384
TAIL = "adbcdacdbcdabcdbdb"
norm_eps = 1e-05


def layer_norm(values, gain, shift):
    centre = jnp.mean(values, axis=-1, keepdims=True)
    centred = values - centre
    spread = jnp.mean(centred * centred, axis=-1, keepdims=True)
    return centred * lax.rsqrt(spread + norm_eps) * gain + shift


ERFC = (
    -1.26551223, 1.00002368, 0.37409196, 0.09678418, -0.18628806, 0.27886807, -1.13520398,
    1.48851587, -0.82215223, 0.17087277,
)


def normal_share(values):
    size = jnp.abs(values) * (0.5 ** 0.5)
    place = 1.0 / (1.0 + 0.5 * size)
    power = ERFC[-1]
    for term in ERFC[-2::-1]:
        power = power * place + term
    tail = 0.5 * place * jnp.exp(power - size * size)
    return jnp.where(values < 0, tail, 1.0 - tail)


def gelu_exact(values):
    return values * normal_share(values)


def gelu_slope(values):
    return normal_share(values) + values * jnp.exp(-0.5 * values * values) * 0.3989422804014327


def widen(values):
    return values.astype(F32)


def back_product(grad, weight):
    return jnp.einsum("rg,cg->rc", grad, weight, preferred_element_type=F32)


def rep_size():
    return 2 * lax.axis_size("pair")


def rep_index():
    return 2 * lax.axis_index("pair") + lax.axis_index("core")


def flip(value, bit):
    if bit == 1:
        return lax.ppermute(value, "core", [(0, 1), (1, 0)])
    count = lax.axis_size("pair")
    return lax.ppermute(value, "pair", [(i, i ^ (bit // 2)) for i in range(count)])


def shift_shard(value, hop):
    count = lax.axis_size("shard")
    return lax.ppermute(value, "shard", [(i, (i - hop) % count) for i in range(count)])


def neighbour_rows(first, last):
    count, place = lax.axis_size("shard"), lax.axis_index("shard")
    if count == 2:
        got = lax.ppermute(jnp.where(place == 0, last, first), "shard", [(0, 1), (1, 0)])
        nothing = jnp.zeros_like(got)
        return jnp.where(place == 0, nothing, got), jnp.where(place == 0, got, nothing)
    up = [(i, i + 1) for i in range(count - 1)]
    down = [(i + 1, i) for i in range(count - 1)]
    return lax.ppermute(last, "shard", up), lax.ppermute(first, "shard", down)


def with_halo(value):
    before, after = neighbour_rows(value[:1], value[-1:])
    return jnp.concatenate([before, value, after], axis=0)


def small_pieces(masters):
    fits = all(item.shape[-2] % (8 * rep_size()) == 0 for item in masters)
    return fits and lax.axis_size("shard") == 2


def own_piece(master):
    rows = master.shape[-2] // rep_size()
    return lax.dynamic_slice_in_dim(master, rep_index() * rows, rows, master.ndim - 2).astype(BF16)


def in_order(piece, other):
    first = lax.axis_index("shard") == 0
    return jnp.stack([jnp.where(first, piece, other), jnp.where(first, other, piece)])


def gather_shard(master):
    return lax.all_gather(master.astype(BF16), "shard", axis=master.ndim - 2, tiled=True)


class Fetch:
    def __init__(self, masters, spread=False):
        self.masters = masters
        self.alone = lax.axis_size("shard") != 2
        self.spread = spread and rep_size() > 2
        self.core = rep_index() % 2
        self.side = rep_index() // 2 % 2
        if self.alone:
            self.state = [gather_shard(item) for item in masters]
            return
        self.state = pack_halves(self.core, masters, PACK)
        if self.spread:
            half = self.state.shape[0] // 2
            self.state = lax.dynamic_slice_in_dim(self.state, self.side * half, half, 0)

    def cross(self):
        if not self.alone:
            self.state = shift_shard(self.state, 1)

    def share(self):
        if not self.alone and self.spread:
            self.state = (self.state, flip(self.state, 2))

    def swap(self):
        if self.alone:
            return
        if self.spread:
            mine, other = self.state
            self.state = jnp.concatenate(
                [
                    jnp.where(self.side == 0, mine, other),
                    jnp.where(self.side == 0, other, mine),
                ],
                axis=0,
            )
        self.state = (self.state, flip(self.state, 1))

    def whole(self):
        if self.alone:
            return self.state
        place = lax.axis_index("shard")
        return join_halves(place, self.core, self.masters, *self.state, PACK)


def land(fetches, *values):
    states, values = lax.optimization_barrier(([item.state for item in fetches], values))
    for item, state in zip(fetches, states):
        item.state = state
    return values


def gather_small(value):
    if lax.axis_size("shard") != 2:
        return lax.all_gather(value, "shard")
    place = lax.axis_index("shard")
    other = lax.ppermute(value, "shard", [(0, 1), (1, 0)])
    return jnp.stack([jnp.where(place == 0, value, other), jnp.where(place == 0, other, value)])


def both_cores(*values):
    widths = [value.shape[1] for value in values]
    other = flip(jnp.concatenate(values, axis=1), 1)
    result, at = [], 0
    for value, width in zip(values, widths):
        result.append((value, other[:, at : at + width]))
        at += width
    return result


def core_half(value, which):
    half = value.shape[1] // 2
    return lax.dynamic_slice_in_dim(value, which * half, half, 1)


def pair_product(left, right):
    total = None
    for one, two in zip(left, right):
        part = jnp.einsum("rc,rg->cg", one, two, preferred_element_type=F32)
        total = part if total is None else total + part
    return total


def columns(pair, place, parts):
    size = pair[0].shape[1] // parts
    return [lax.dynamic_slice_in_dim(item, place * size, size, 1) for item in pair]


def weights_of(pair, shapes):
    core, width = lax.axis_index("core"), pair[0].shape[1]
    if all(lanes % width == 0 or kind == "rows" for _, lanes, kind in shapes):
        return unpack_halves(core, *pair, shapes)
    low, high = [jnp.where(core == k, pair[0], pair[1]) for k in range(2)]
    blocks, at = [], 0
    for rows, lanes, kind in shapes:
        if kind == "rows":
            halves = [half[at : at + rows, :lanes] for half in (low, high)]
            at += rows
        elif lanes % width:
            size = rows * lanes // width
            halves = [half[at : at + size].reshape(rows, lanes) for half in (low, high)]
            at += size
        else:
            count = lanes // width
            halves = [
                jnp.concatenate(
                    [half[at + k * rows : at + (k + 1) * rows] for k in range(count)], axis=1
                )
                for half in (low, high)
            ]
            at += count * rows
        halves = [widen(half) for half in halves]
        if kind == "stacked":
            blocks.append(jnp.stack(halves))
        elif kind == "turned":
            blocks.append(jnp.concatenate(halves, axis=0).T)
        else:
            blocks.append(jnp.concatenate(halves, axis=1 if kind == "lanes" else 0))
    return blocks


class Flow:
    def __init__(self, sent, value):
        self.value, self.away = value, sent
        bits = [1 << k for k in range(1, (rep_size() - 1).bit_length())]
        self.stages = [("shard", 0)] + [("halve", bit) for bit in bits]
        self.stages += [("double", bit) for bit in bits[::-1]] + [("core", 1)]
        if len(bits) > 1:
            self.stages[2:-2] = [("scatter", 0), ("gather", 0)]

    def launch(self):
        kind, bit = self.stages[0]
        if kind == "shard":
            parts = lax.axis_size("shard")
            self.got = [shift_shard(item, -hop % parts) for hop, item in enumerate(self.away, 1)]
        elif kind in ("scatter", "gather"):
            self.got = [flip(item, 4 * hop) for hop, item in enumerate(self.away, 1)]
        else:
            self.got = [flip(item, bit) for item in self.away]

    @staticmethod
    def by_place(items):
        whole, z = jnp.stack(items), rep_index() // 4
        return [
            lax.dynamic_index_in_dim(whole, jnp.bitwise_xor(z, p), 0, keepdims=False)
            for p in range(len(items))
        ]

    def combine(self):
        kind, bit = self.stages.pop(0)
        side = (rep_index() // max(bit, 1)) % 2
        if kind in ("shard", "halve", "scatter"):
            total = widen(self.value)
            for item in self.got:
                total = total + widen(item)
            self.value = total.astype(BF16)
        elif kind == "core":
            self.value = (self.value, self.got[0])
        elif kind == "gather":
            self.value = jnp.concatenate(self.by_place([self.value] + self.got), axis=0)
        else:
            low = jnp.where(side == 0, self.value, self.got[0])
            high = jnp.where(side == 0, self.got[0], self.value)
            self.value = jnp.concatenate([low, high], axis=0)
        if not self.stages:
            return
        kind, bit = self.stages[0]
        if kind in ("scatter", "gather"):
            count = rep_size() // 4
            self.away = [self.value] * (count - 1)
            if kind == "scatter":
                rows = self.value.shape[0] // count
                self.value, *self.away = self.by_place(
                    [self.value[k * rows : (k + 1) * rows] for k in range(count)]
                )
        elif kind == "halve":
            half = self.value.shape[0] // 2
            side = (rep_index() // bit) % 2
            self.away = [lax.dynamic_slice_in_dim(self.value, (1 - side) * half, half, 0)]
            self.value = lax.dynamic_slice_in_dim(self.value, side * half, half, 0)
        else:
            self.away = [self.value]


def turn(token, landing, starting, *values):
    landing = [flow for flow in landing if flow.stages]
    got, values, token = lax.optimization_barrier(([flow.got for flow in landing], values, token))
    for flow, item in zip(landing, got):
        flow.got = item
        flow.combine()
    going = [flow for flow in landing if flow.stages] + list(starting)
    away, values, token = lax.optimization_barrier(([flow.away for flow in going], values, token))
    for flow, item in zip(going, away):
        flow.away = item
        flow.launch()
    return token, values


def shards(
    token_in,
    char_in,
    char_ids,
    char_counts,
    segments,
    token_cot,
    char_cot,
    query_proj,
    key_proj,
    value_proj,
    output_proj,
    query_bias,
    value_bias,
    output_bias,
    first_gain,
    first_shift,
    expand_proj,
    expand_bias,
    shrink_proj,
    shrink_bias,
    char_table,
    gate_input,
    input_bias,
    gate_recur,
    recur_bias,
    token_proj,
    token_bias,
    char_proj,
    char_bias,
    merging_kernel,
    merging_bias,
    token_gain,
    token_shift,
    char_gain,
    char_shift,
):
    rows, width = token_in.shape
    place, parts = lax.axis_index("shard"), lax.axis_size("shard")
    rep = rep_index()
    core = rep % 2
    slots = char_ids.shape[1]
    chars = char_table.shape[1]
    vocab = char_table.shape[0] * parts
    gate_width = gate_input.shape[-1]
    hid = gate_width // 3
    ff = expand_proj.shape[1]

    first_fetch = Fetch([query_proj, key_proj, value_proj])
    gate_input, gate_recur, merging_kernel, flat_first = land(
        [first_fetch], gate_input, gate_recur, merging_kernel, query_bias
    )
    first_fetch.cross()
    spread = small_pieces([merging_kernel])
    kernel_piece = own_piece(merging_kernel) if spread else jnp.zeros((8, 128), BF16)
    gate_fetch = Fetch([gate_input, gate_recur])

    vectors = (
        flat_first, value_bias, output_bias, first_gain, first_shift, expand_bias, shrink_bias,
        input_bias, recur_bias, token_bias, char_bias, merging_bias, token_gain, token_shift,
        char_gain, char_shift,
    )
    flat = jnp.concatenate([item.reshape(-1) for item in vectors]).astype(BF16)
    pad = -flat.shape[0] % (8 * chars)
    small = jnp.concatenate(
        [char_table.astype(BF16), jnp.pad(flat, (0, pad)).reshape(-1, chars)], axis=0
    )
    packed_ids = jnp.concatenate([char_ids, char_counts[:, None]], axis=1)
    small, packed_ids, kernel_piece = land([first_fetch, gate_fetch], small, packed_ids, kernel_piece)
    gate_fetch.cross()
    first_fetch.swap()
    kernel_other = shift_shard(kernel_piece, 1) if spread else kernel_piece
    small = gather_small(small)
    ids_ext = with_halo(packed_ids)
    query_low, key_low, value_low = first_fetch.whole()
    table_low = small[:, : char_table.shape[0]].reshape(vocab, chars)
    tail = widen(small[:, char_table.shape[0] :].reshape(parts, -1))
    wide, at = [], 0
    for item in vectors:
        size = item.size
        block = tail[:, at : at + size].reshape((parts,) + item.shape)
        at += size
        if item.ndim == 2:
            wide.append(block.transpose(1, 0, 2).reshape(item.shape[0], 1, -1))
        else:
            wide.append(block.reshape(-1))
    (
        bias_query, bias_value, bias_output, gain_first, shift_first, bias_expand, bias_shrink,
        bias_input, bias_recur, bias_token, bias_char, bias_merging, gain_token, shift_token,
        gain_char, shift_char,
    ) = wide

    counts_ext = ids_ext[:, slots]
    onehot = (
        ids_ext[:, :slots].T.reshape(-1)[:, None] == jnp.arange(vocab, dtype=jnp.int32)[None, :]
    ).astype(BF16)
    letters_of = [ids_ext[at : at + rows, :slots].T for at in (0, 2, 1)]
    id_columns = jnp.stack(letters_of)[..., None]
    counts = jnp.stack([counts_ext[:rows], counts_ext[2:], counts_ext[1 : rows + 1]])[:, :, None]
    length = segments.shape[0]
    seg_blocks = [
        lax.dynamic_slice_in_dim(segments, ((place + hop) % parts) * rows, rows)
        for hop in range(parts)
    ]
    seg_rows = seg_blocks[0]
    seg_q = seg_rows[None, :]
    seg_k = jnp.concatenate(seg_blocks)[:, None]
    start = place * rows
    near = jnp.stack([segments[:1], segments[-1:]])
    before = lax.dynamic_slice_in_dim(jnp.concatenate([near[0], segments]), start, rows)
    after_rows = lax.dynamic_slice_in_dim(jnp.concatenate([segments[1:], near[1]]), start, rows)
    position = start + jnp.arange(rows)
    keep = jnp.stack(
        [
            ((position > 0) & (before == seg_rows)).astype(F32),
            ((position < length - 1) & (after_rows == seg_rows)).astype(F32),
        ]
    )[:, :, None]

    keys = dot(token_in, key_low).astype(BF16)
    values = (dot(token_in, value_low) + bias_value).astype(BF16)
    keys_values = jnp.concatenate([keys, values], axis=1)
    keys_values, query_low, onehot, output_proj, expand_proj, shrink_proj, token_proj, char_proj = land(
        [], keys_values, query_low, onehot, output_proj, expand_proj, shrink_proj, token_proj, char_proj
    )
    blocks = [keys_values] + [shift_shard(keys_values, hop) for hop in range(1, parts)]
    queries = (dot(token_in, query_low) + bias_query).astype(BF16)
    up_fetch = Fetch([output_proj, expand_proj], True)
    down_fetch = Fetch([shrink_proj, token_proj, char_proj], True)
    kernel_other, queries = land([gate_fetch, up_fetch, down_fetch], kernel_other, queries)
    gate_fetch.swap()
    if spread:
        kernel_low = jnp.moveaxis(in_order(kernel_piece, kernel_other), 0, 1)
        kernel_low = lax.all_gather(kernel_low, ("pair", "core"), axis=2, tiled=True)
        kernel_low = kernel_low.reshape(merging_kernel.shape[0], 2 * width, 2 * width)
    else:
        kernel_low = gather_shard(merging_kernel)
    embedded = dot(onehot, table_low).astype(BF16).reshape(slots, rows + 2, chars)
    letters = (embedded[:, :rows], embedded[:, 2:], embedded[:, 1 : rows + 1])
    input_low, recur_low = gate_fetch.whole()
    up_fetch.cross()
    starts, pooled_low = gru_forward(
        letters, input_low, recur_low, bias_input, bias_recur, counts, keep
    )
    pooled_low, blocks = land([up_fetch], pooled_low, blocks)
    up_fetch.share()
    down_fetch.cross()
    everyone = jnp.concatenate(blocks, axis=0)
    all_keys, all_values = everyone[:, :width], everyone[:, width:]
    mixed, logsum = attend(queries, all_keys, all_values, seg_q, seg_k, HEAD_DIM)
    (mixed,) = land([up_fetch, down_fetch], mixed)
    up_fetch.swap()
    down_fetch.share()

    output_low, expand_low = up_fetch.whole()
    first_in = widen(token_in) + (dot(mixed, output_low) + bias_output)
    first = layer_norm(first_in, gain_first, shift_first)
    first_low = first.astype(BF16)
    up = dot(first_low, expand_low) + bias_expand
    hidden = gelu_exact(up).astype(BF16)
    (hidden,) = land([down_fetch], hidden)
    down_fetch.swap()
    shrink_low, project_token, project_char = down_fetch.whole()
    token_mid = first + dot(hidden, shrink_low) + bias_shrink
    mid_low = token_mid.astype(BF16)

    tok_side = dot(mid_low, project_token) + bias_token
    char_side = dot(pooled_low, project_char) + bias_char
    joined = jnp.concatenate([tok_side, char_side], axis=1).astype(BF16)
    joined_ext = with_halo(joined)
    merged = (
        bias_merging
        + dot(joined_ext[0:rows], kernel_low[0])
        + dot(joined_ext[1 : rows + 1], kernel_low[1])
        + dot(joined_ext[2 : rows + 2], kernel_low[2])
    )
    act = gelu_exact(merged)
    tok_pre = token_mid + act[:, :width]
    char_pre = widen(char_in) + act[:, width:]
    token_out = layer_norm(tok_pre, gain_token, shift_token).astype(BF16)
    char_out = layer_norm(char_pre, gain_char, shift_char).astype(BF16)

    _, token_pull = jax.vjp(layer_norm, tok_pre, gain_token, shift_token)
    tok_pre_grad, token_gain_grad, token_shift_grad = token_pull(widen(token_cot))
    _, char_pull = jax.vjp(layer_norm, char_pre, gain_char, shift_char)
    char_grad, char_gain_grad, char_shift_grad = char_pull(widen(char_cot))
    act_grad = jnp.concatenate([tok_pre_grad, char_grad], axis=1)
    merged_grad = (act_grad * gelu_slope(merged)).astype(BF16)
    merging_bias_grad = jnp.sum(widen(merged_grad), axis=0)
    exchange = flip(
        jnp.concatenate(
            [joined_ext, jnp.pad(core_half(merged_grad, 1 - core), ((0, 2), (0, 0)))], axis=1
        ),
        1,
    )
    merged_ext = with_halo(merged_grad)
    centre = back_product(merged_grad, kernel_low[1])
    exchange, merged_ext, centre = lax.optimization_barrier((exchange, merged_ext, centre))
    joined_pair = (joined_ext, exchange[:, : 2 * width])
    merged_pair = (core_half(merged_grad, core), exchange[:rows, 2 * width :])
    others = [(place + hop) % parts for hop in range(1, parts)]

    def merging_terms(target):
        sources = columns(joined_pair, target, parts)
        return jnp.concatenate(
            [
                pair_product([item[tap : tap + rows] for item in sources], merged_pair)
                for tap in range(3)
            ],
            axis=0,
        )

    token = jnp.zeros((8, 128), F32)
    merging_flow = Flow([merging_terms(j).astype(BF16) for j in others], merging_terms(place))
    token, (centre, merged_ext) = turn(token, [], [merging_flow], centre, merged_ext)
    joined_grad = (
        back_product(merged_ext[2 : rows + 2], kernel_low[0])
        + centre
        + back_product(merged_ext[0:rows], kernel_low[2])
    )
    tok_side_grad = joined_grad[:, :width].astype(BF16)
    char_side_grad = joined_grad[:, width:].astype(BF16)
    token_bias_grad = jnp.sum(widen(tok_side_grad), axis=0)
    char_bias_grad = jnp.sum(widen(char_side_grad), axis=0)
    pooled_grad = back_product(char_side_grad, project_char)
    mid_grad = tok_pre_grad + back_product(tok_side_grad, project_token)

    shrink_out_grad = mid_grad.astype(BF16)
    shrink_bias_grad = jnp.sum(widen(shrink_out_grad), axis=0)
    hidden_grad = back_product(shrink_out_grad, shrink_low)
    up_grad = (hidden_grad * gelu_slope(up)).astype(BF16)
    expand_bias_grad = jnp.sum(widen(up_grad), axis=0)
    middle_own = jnp.concatenate(
        [
            hidden, first_low, mid_low, pooled_low, shrink_out_grad, up_grad, tok_side_grad,
            char_side_grad,
        ],
        axis=1,
    )
    middle_pair = (middle_own, flip(middle_own, 1))
    first_grad = mid_grad + back_product(up_grad, expand_low)
    _, first_pull = jax.vjp(layer_norm, first_in, gain_first, shift_first)
    first_in_grad, first_gain_grad, first_shift_grad = first_pull(first_grad)
    attn_grad = first_in_grad.astype(BF16)
    output_bias_grad = jnp.sum(widen(attn_grad), axis=0)
    mixed_grad = back_product(attn_grad, output_low).astype(BF16)
    mixed_grad, middle_pair = lax.optimization_barrier((mixed_grad, middle_pair))

    def middle_terms(target, dtype):
        if width // parts == PACK:
            deep = ff // 2 // PACK
            at_first = 2 * deep
            at_mid, at_pooled, at_out, at_up = [at_first + 2 * k for k in range(1, 5)]
            at_tok, at_char = at_up + 2 * deep, at_up + 2 * deep + 2
            left = [target * deep + k for k in range(deep)]
            left += [at_up + core * deep + k for k in range(deep)]
            left += [at_mid + target, at_pooled + target]
            right = [at_out + core] * deep + [at_first + target] * deep
            right += [at_tok + core, at_char + core]
            table = jnp.stack([jnp.stack(left), jnp.stack(right)])
            return block_terms(middle_pair, middle_pair, table, PACK, dtype)
        ends = [ff + width * k for k in range(5)] + [2 * ff + width * k for k in range(4, 7)]
        hiddens, firsts, mids, pools, outs, ups, toks, sides = [
            [item[:, lo:hi] for item in middle_pair] for lo, hi in zip([0] + ends[:-1], ends)
        ]
        outs, ups, toks, sides = [
            [core_half(item, core) for item in pair] for pair in (outs, ups, toks, sides)
        ]
        return pack_rows(
            [
                pair_product(columns(hiddens, target, parts), outs),
                pair_product(ups, columns(firsts, target, parts)),
                pair_product(columns(mids, target, parts), toks),
                pair_product(columns(pools, target, parts), sides),
            ],
            PACK,
            dtype,
        )

    middle_flow = Flow([middle_terms(j, BF16) for j in others], None)
    final = jnp.stack([pooled_grad[:, :hid], pooled_grad[:, hid:]])
    token, (mixed_grad, final) = turn(token, [], [middle_flow], mixed_grad, final)

    queries_grad, *terms = attend_back(
        queries, all_keys, all_values, seg_q, seg_k, mixed_grad, logsum, HEAD_DIM
    )
    token, (final, queries_grad, terms, middle_flow.value) = turn(
        token, [merging_flow], [], final, queries_grad, terms, middle_terms(place, BF16)
    )
    away_terms = [shift_shard(terms[hop], -hop % parts) for hop in range(1, parts)]
    late_own = jnp.concatenate([token_in, mixed, queries_grad, attn_grad], axis=1)
    late_other = flip(late_own, 1)

    own_counts = jnp.stack([counts[2], counts[2]])
    own_grads = gru_backward(
        True, letters[2], letters[2], input_low, recur_low, bias_input, bias_recur, own_counts,
        keep, starts, final,
    )
    token, (own_grads, away_terms, late_other) = turn(
        token, [merging_flow], [], own_grads, away_terms, late_other
    )
    owned = widen(terms[0])
    for item in away_terms:
        owned = owned + widen(item)
    owned = owned.astype(BF16)
    keys_grad, values_grad = owned[0], owned[1]
    owned_other = flip(owned, 1)
    late_pair = (late_own, late_other)

    def late_terms(targets):
        if width // parts == PACK:
            left = jnp.stack([item for j in targets for item in (j, 2 + j)])
            right = jnp.stack([4 + core, 6 + core] * len(targets))
            first = block_terms(late_pair, late_pair, jnp.stack([left, right]), PACK, BF16)
            first, owned_other_now = lax.optimization_barrier((first, owned_other))
            owned_pair = (owned, owned_other_now)
            left = jnp.stack([item for j in targets for item in (j, j)])
            right = jnp.stack([core, 2 + core] * len(targets))
            second = block_terms(late_pair, owned_pair, jnp.stack([left, right]), PACK, BF16)
            deep = 2 * PACK
            return [
                jnp.concatenate([item[k * deep : (k + 1) * deep] for item in (first, second)], axis=0)
                for k in range(len(targets))
            ]
        inputs, mixes, query_part, attn_part = [
            [item[:, k * width : (k + 1) * width] for item in late_pair] for k in range(4)
        ]
        key_part, value_part = [
            [item[k] for item in (owned, owned_other)] for k in range(2)
        ]
        products = (
            (inputs, query_part), (mixes, attn_part), (inputs, key_part), (inputs, value_part)
        )
        return [
            pack_rows(
                [
                    pair_product(columns(one, j, parts), [core_half(item, core) for item in two])
                    for one, two in products
                ],
                PACK,
                BF16,
            )
            for j in targets
        ]

    *late_sent, late_own_terms = late_terms(others + [place])
    late_flow = Flow(late_sent, late_own_terms)
    token, (own_grads,) = turn(token, [], [late_flow], own_grads)

    near_grads = gru_backward(
        False, letters[0], letters[1], input_low, recur_low, bias_input, bias_recur, counts[:2],
        keep, starts, own_grads[2], own_grads[3:],
    )
    token, (own_grads, near_grads) = turn(
        token, [late_flow, merging_flow, middle_flow], [], own_grads, near_grads
    )

    table_grad = table_terms_of(id_columns, *near_grads[:2], *own_grads[:2], vocab)
    query_bias_grad = jnp.sum(widen(queries_grad), axis=0)
    value_bias_grad = jnp.sum(widen(values_grad), axis=0)
    bias_input_grad, bias_recur_grad = near_grads[5:]
    vector_grads = (
        query_bias_grad, value_bias_grad, output_bias_grad, first_gain_grad, first_shift_grad,
        expand_bias_grad, shrink_bias_grad, bias_input_grad[:, 0], bias_recur_grad[:, 0],
        token_bias_grad, char_bias_grad, merging_bias_grad, token_gain_grad, token_shift_grad,
        char_gain_grad, char_shift_grad,
    )
    vector_terms = jnp.concatenate(
        [
            jnp.moveaxis(item.reshape(item.shape[:-1] + (parts, -1)), -2, 0).reshape(parts, -1)
            for item in vector_grads
        ],
        axis=1,
    ).reshape(parts, 2, -1, PACK)
    chars_part, hid_part = chars // parts, hid // parts
    part, joint = width // parts, 2 * width // parts
    tail_rows = vocab // parts // 2
    gru_shapes = [
        (chars_part, gate_width), (hid_part, gate_width), (tail_rows, PACK),
        (vector_terms.shape[2], PACK),
    ]
    depth = sum(deep * lanes for deep, lanes in gru_shapes) // PACK
    depth += -depth % (4 * rep_size())
    table_terms = table_grad.reshape(parts, 2, tail_rows, chars)
    gru_sums = near_grads[3:5]
    gru_away = pack_gru_terms(
        1 - core, gru_sums, table_terms, vector_terms, depth, PACK, BF16
    )
    token, (gru_sums, table_terms, vector_terms, gru_away) = turn(
        token, [late_flow], [], gru_sums, table_terms, vector_terms, gru_away
    )
    gru_away = flip(gru_away, 1)
    gru_own = pack_gru_terms(core, gru_sums, table_terms, vector_terms, depth, PACK, F32)
    token, (gru_own, gru_away) = turn(token, [], [], gru_own, gru_away)
    gru_total = gru_own + widen(gru_away)
    gru_flow = Flow(
        [lax.dynamic_index_in_dim(gru_total, j, 0, keepdims=False).astype(BF16) for j in others],
        lax.dynamic_index_in_dim(gru_total, place, 0, keepdims=False),
    )
    token, (queries_grad, keys_grad, values_grad) = turn(
        token, [], [gru_flow], queries_grad, keys_grad, values_grad
    )
    token_grad = (
        first_in_grad
        + back_product(queries_grad, query_low)
        + back_product(keys_grad, key_low)
        + back_product(values_grad, value_low)
    )
    flows = dict(a=merging_flow, b=middle_flow, c=late_flow, d=gru_flow)
    shapes = dict(
        a=[(3 * joint, width, "lanes")],
        b=[
            (ff // parts, PACK, "lanes"), (ff // 2, part, "turned"), (part, PACK, "lanes"),
            (part, PACK, "lanes"),
        ],
        c=[(part, PACK, "lanes")] * 4,
        d=[
            (chars_part, gate_width, "stacked"), (hid_part, gate_width, "stacked"),
            (tail_rows, chars, "rows"), (vector_terms.shape[2], PACK, "stacked"),
        ],
    )
    for name in TAIL + "abcd" * 16:
        token, _ = turn(token, [flows[name]], [])
    owned_shards = {name: weights_of(flow.value, shapes[name]) for name, flow in flows.items()}
    (merging_out,) = owned_shards["a"]
    merging_out = merging_out.reshape(3, joint, 2 * width)
    shrink_out, expand_out, token_proj_out, char_proj_out = owned_shards["b"]
    query_out, output_out, key_out, value_out = owned_shards["c"]
    input_out, recur_out, table_out, flat_out = owned_shards["d"]
    flat_out = flat_out.reshape(-1)
    vector_out, at = [], 0
    for item in vectors:
        vector_out.append(flat_out[at : at + item.size].reshape(item.shape))
        at += item.size
    (
        query_bias_out, value_bias_out, output_bias_out, first_gain_out, first_shift_out,
        expand_bias_out, shrink_bias_out, input_bias_out, recur_bias_out, token_bias_out,
        char_bias_out, merging_bias_out, token_gain_out, token_shift_out, char_gain_out,
        char_shift_out,
    ) = vector_out
    return (
        token_out, char_out, token_grad, char_grad,
        query_out, key_out, value_out, output_out,
        query_bias_out, value_bias_out, output_bias_out, first_gain_out, first_shift_out,
        expand_out, expand_bias_out, shrink_out, shrink_bias_out, table_out,
        input_out, input_bias_out, recur_out, recur_bias_out,
        token_proj_out, token_bias_out, char_proj_out, char_bias_out,
        merging_out, merging_bias_out, token_gain_out, token_shift_out, char_gain_out,
        char_shift_out,
    )


def solution(mesh):
    sizes = (mesh.shape["rep"] // 2, 2, mesh.shape["shard"])
    mesh = jax.sharding.Mesh(mesh.devices.reshape(sizes), ("pair", "core", "shard"))
    rows = P(("pair", "core", "shard"), None)
    split, vector = P("shard", None), P("shard")
    in_specs = (
        rows, rows, rows, P(("pair", "core", "shard")), P(("pair", "core")), rows, rows,
        split, split, split, split, vector, vector, vector, vector, vector,
        split, vector, split, vector, split,
        P(None, "shard", None), P(None, "shard"), P(None, "shard", None), P(None, "shard"),
        split, vector, split, vector, P(None, "shard", None), vector,
        vector, vector, vector, vector,
    )
    out_specs = (rows,) * 4 + in_specs[7:]
    return jax.shard_map(shards, mesh=mesh, in_specs=in_specs, out_specs=out_specs, check_vma=False)
```

time: 1280 us -> 834 us (0.65)
  waiting for transfers between devices: 650 us -> 178 us
  Pallas kernels: 150 us -> 277 us
  matrix products: 176 us -> 107 us
  local copies, waits for them, and re-layouts: 126 us -> 83.2 us
  starting transfers between devices: 46.6 us -> 82 us
  other arithmetic: 110 us -> 77.9 us
    all_gather x7 -> x1, waiting for transfers between devices: 303 us -> 0.02 us  [shards(): lax.all_gather(kernel_low, ('pair', 'core'), axis=2, tiled=True)]
    pallas_call x1 -> x21, Pallas kernels: 79.8 us -> 207 us  [the longest x2 85.5 us: gru_backward(): pl.pallas_call(functools.partial(gru_backward_kernel, slots, last), grid=...]
    psum x1 -> x0, waiting for transfers between devices: 112 us -> none  [shards(): flat_grad = lax.psum(flat_grad, ('rep', 'shard')).reshape(-1)]
    ppermute x5 -> x11, waiting for transfers between devices: 109 us -> 16.7 us  [shift_shard(): lax.ppermute(value, 'shard', [(i, (i - hop) % count) for i in range(count)])]
    dot_general x44 -> x12, matrix products: 74.6 us -> 24.4 us  [pair_product(): part = jnp.einsum('rc,rg->cg', one, two, preferred_element_type=F32)]
    ppermute x26 -> x47, waiting for transfers between devices: 121 us -> 160 us  [the longest x34 159 us: flip(): lax.ppermute(value, 'pair', [(i, i ^ bit // 2) for i in range(count)])]
    ppermute x26 -> x47, starting transfers between devices: 38.7 us -> 68.7 us  [the longest x34 36 us: flip(): lax.ppermute(value, 'pair', [(i, i ^ bit // 2) for i in range(count)])]
    concatenate x21 -> x15, other arithmetic: 37.8 us -> 9.03 us  [the longest x1 2.45 us: shards(): jnp.concatenate([joined_ext, jnp.pad(core_half(merged_grad, 1 - core), ((...]
  transfers between devices with their start and end apart: 43 -> 63, of which waited for: 21 -> 25; matrix products, arithmetic and copies ran while one was open for 27% -> 20% of each run, Pallas kernels for 12% -> 31%
where the time goes in v2:
time: 834 us; the launch traced here: 822 us
  Pallas kernels  277 us (33%)
  waiting for transfers between devices  178 us (21%)
  matrix products  107 us (13%)
  local copies, waits for them, and re-layouts  83.2 us (10%)
  starting transfers between devices  82 us (10%)
  other arithmetic  77.9 us (9%)
  between operations  17.1 us (2%)
    ppermute x34, waiting for transfers between devices, flip(): lax.ppermute(value, 'pair', [(i, i ^ bit // 2) for i in range(count)])  159 us
    pallas_call x2, Pallas kernels, gru_backward(): pl.pallas_call(functools.partial(gru_backward_kernel, slots, last), grid=...  85.5 us
    dot_general x12, matrix products, dot(): return jnp.dot(left, right, preferred_element_type=F32)  45.7 us
    dot_general x11, matrix products, back_product(): return jnp.einsum('rg,cg->rc', grad, weight, preferred_element_type=F32)  37.1 us
    pallas_call x4, Pallas kernels, block_terms(): pl.pallas_call(block_terms_kernel, grid_spec=pltpu.PrefetchScalarGridSpec...  36.7 us
    ppermute x34, starting transfers between devices, flip(): lax.ppermute(value, 'pair', [(i, i ^ bit // 2) for i in range(count)])  36 us
    ppermute x13, starting transfers between devices, flip(): return lax.ppermute(value, 'core', [(0, 1), (1, 0)])  32.8 us
    pallas_call x1, Pallas kernels, gru_forward(): pl.pallas_call(functools.partial(gru_forward_kernel, slots), grid=(2 * sl...  28.3 us
  transfers between devices with their start and end apart: 63, of which 25 were waited for; matrix products, arithmetic and copies ran while one was open for 20% of the time, Pallas kernels for 31%

profile of v2, /device:TPU:17, one launch (start us, length us, event | category | flops | bytes accessed | tf_op | source)
XLA Modules:
  0.0 822.4 jit_solution(10310153633295113870)
XLA Ops:
  21.3 10.6 %collective-permute-done.refs_3_ = bf16[1152,384]{1,0:T(8,128)(2,1)S(1)} collective-permute-done((bf16[1152,384]{1,0:T(8,128)(2,1)}, bf16[1152,384]{1,0:T(8,128)(2,1)S(1)}, u32[]{:S(2)}, u32[]{:S(2)}) %collective-permute-start) | collective-permute-done | bytes 884768 | tf_op jit(solution)/shard_map/ppermute | solution.py:663
  41.9 5.3 join_halves.4
  82.2 5.1 convolution_convert_fusion
  91.7 5.2 join_halves.5
  96.9 28.3 %gru_forward.1 = (f32[10,2,512,384]{3,2,1,0:T(8,128)}, bf16[512,768]{1,0:T(8,128)(2,1)}) custom-call(bf16[5,512,256]{2,1,0:T(8,128)(2,1)} %get-tuple-element.646.a0.x0, bf16[5,512,256]{2,1,0:T(8,128)(2,1)} %get-tuple-element.645.a1.x1, bf16[5,512,256]{2,1,0:T(8,128)(2,1)} %get-tuple-element.644.b0.b1.x0.x1, ...), custom_call_target="tpu_custom_call" | custom-call | flops 1024 | bytes 1024 | tf_op jit(solution)/shard_map/gru_forward/pallas_call | solution.py:104
  129.9 16.5 %attend.1 = (bf16[512,768]{1,0:T(8,128)(2,1)}, f32[6,2,512]{2,1,0:T(2,128)}) custom-call(bf16[512,768]{1,0:T(8,128)(2,1)} %fusion.41.q, bf16[1024,768]{1,0:T(8,128)(2,1)} %get-tuple-element.607.k, bf16[1024,768]{1,0:T(8,128)(2,1)} %get-tuple-element.606.v, s32[1,512]{1,0:T(1,128)} %bitcast.300, s32[1024,1]{1,0:T(8,128)} %copy.134.seg_k), custom_call_target="tpu_custom_call" | custom-call | flops 1024 | bytes 1024 | tf_op jit(solution)/shard_map/attend/pallas_call | solution.py:517
  146.5 11.7 %collective-permute-done.9 = bf16[960,384]{1,0:T(8,128)(2,1)S(1)} collective-permute-done((bf16[960,384]{1,0:T(8,128)(2,1)}, bf16[960,384]{1,0:T(8,128)(2,1)S(1)}, u32[]{:S(2)}, u32[]{:S(2)}) %collective-permute-start.9) | collective-permute-done | bytes 737312 | tf_op jit(solution)/shard_map/ppermute | solution.py:658
  159.6 5.2 collective-permute-start.11
  169.0 6.8 join_halves.6
  179.0 11.4 %multiply_convert_fusion = (bf16[512,3072]{1,0:T(8,128)(2,1)}, f32[512,3072]{1,0:T(8,128)}) fusion(f32[3072]{0:T(1024)S(1)} %add.644, bf16[768,3072]{1,0:T(8,128)(2,1)S(1)} %copy-done.124, f32[512,768]{1,0:T(8,128)S(1)} %get-tuple-element.729, f32[768]{0:T(1024)S(1)} %add.641, f32[768]{0:T(1024)S(1)} %mul.456, f32[512]{0:T(512)S(1)} %fusion.109, ...), kind=kOutput, calls=%fused_computation.13 | convolution fusion | flops 2469789696 | bytes 15751168 | tf_op jit(solution)/shard_map/dot_general | solution.py:16
  199.7 7.5 join_halves.7
  209.5 6.2 convert_dynamic-update-slice_fusion
  219.4 5.9 fusion.124
  231.7 5.7 fusion.18
  244.6 5.1 convert_reduce_fusion.1
  259.3 4.5 fusion.135
  285.6 11.6 %constant_dynamic-update-slice_fusion.3 = (bf16[512,10752]{1,0:T(8,128)(2,1)}, bf16[512,3072]{1,0:T(8,128)(2,1)}) fusion(bf16[512,10752]{1,0:T(8,128)(2,1)} %get-tuple-element.737, f32[512,3072]{1,0:T(8,128)S(1)} %bitcast.315, f32[3072]{0:T(1024)S(1)} %add.644, bf16[3072,768]{1,0:T(8,128)(2,1)S(1)} %bitcast.313, f32[512,768]{1,0:T(8,128)S(1)} %get-tuple-element.738), kind=kOutput, calls=%fused_computation.272 | convolution fusion | flops 2476081152 | bytes 18886656 | tf_op jit(solution)/shard_map/rg,cg->rc/dot_general | solution.py:643
  302.6 6.4 multiply_reduce_fusion
  328.8 12.1 %block_terms.5 = bf16[3840,384]{1,0:T(8,128)(2,1)} custom-call(s32[2,10]{1,0:T(2,128)} %pad_add_fusion.10.table, bf16[512,10752]{1,0:T(8,128)(2,1)} %constant_dynamic-update-slice_fusion.2.a0.b0, bf16[512,10752]{1,0:T(8,128)(2,1)} %constant_dynamic-update-slice_fusion.2.a0.b0, bf16[512,10752]{1,0:T(8,128)(2,1)} %collective-permute-done.18.a1.b1, ...), custom_call_target="tpu_custom_call" | custom-call | flops 1024 | bytes 1024 | tf_op jit(solution)/shard_map/block_terms/pallas_call | solution.py:314
  340.9 12.1 %block_terms.4 = bf16[3840,384]{1,0:T(8,128)(2,1)} custom-call(s32[2,10]{1,0:T(2,128)} %pad_add_fusion.9.table, bf16[512,10752]{1,0:T(8,128)(2,1)} %constant_dynamic-update-slice_fusion.2.a0.b0, bf16[512,10752]{1,0:T(8,128)(2,1)} %constant_dynamic-update-slice_fusion.2.a0.b0, bf16[512,10752]{1,0:T(8,128)(2,1)} %collective-permute-done.18.a1.b1, ...), custom_call_target="tpu_custom_call" | custom-call | flops 1024 | bytes 1024 | tf_op jit(solution)/shard_map/block_terms/pallas_call | solution.py:314
  353.0 25.4 %attend_back.1 = (bf16[512,768]{1,0:T(8,128)(2,1)}, bf16[2,512,768]{2,1,0:T(8,128)(2,1)}, bf16[2,512,768]{2,1,0:T(8,128)(2,1)}) custom-call(bf16[512,768]{1,0:T(8,128)(2,1)} %fusion.41.q, bf16[1024,768]{1,0:T(8,128)(2,1)} %get-tuple-element.607.k, bf16[1024,768]{1,0:T(8,128)(2,1)} %get-tuple-element.606.v, s32[1,512]{1,0:T(1,128)} %bitcast.301, ...), custom_call_target="tpu_custom_call" | custom-call | flops 1024 | bytes 1024 | tf_op jit(solution)/shard_map/attend_back/pallas_call | solution.py:577
  390.5 42.4 %gru_backward.2 = (bf16[5,512,256]{2,1,0:T(8,128)(2,1)}, bf16[5,512,256]{2,1,0:T(8,128)(2,1)}, f32[2,512,384]{2,1,0:T(8,128)}, f32[2,256,1152]{2,1,0:T(8,128)}, ...) custom-call(bf16[5,512,256]{2,1,0:T(8,128)(2,1)} %get-tuple-element.644.b0.b1.x0.x1, ...), custom_call_target="tpu_custom_call" | custom-call | flops 1024 | bytes 1024 | tf_op jit(solution)/shard_map/gru_backward/pallas_call | solution.py:190
  461.6 6.3 block_terms.6
  467.8 6.2 block_terms.7
  483.0 43.2 %gru_backward.3 = (bf16[5,512,256]{2,1,0:T(8,128)(2,1)}, bf16[5,512,256]{2,1,0:T(8,128)(2,1)}, f32[2,512,384]{2,1,0:T(8,128)}, f32[2,256,1152]{2,1,0:T(8,128)}, ...) custom-call(bf16[5,512,256]{2,1,0:T(8,128)(2,1)} %get-tuple-element.646.a0.x0, ...), custom_call_target="tpu_custom_call" | custom-call | flops 1024 | bytes 1024 | tf_op jit(solution)/shard_map/gru_backward/pallas_call | solution.py:190
  526.2 6.1 collective-permute-done.23
  544.7 9.5 %table_terms.1 = f32[1024,256]{1,0:T(8,128)} custom-call(s32[3,5,512,1]{3,2,1,0:T(8,128)} %copy.142.ids, bf16[5,512,256]{2,1,0:T(8,128)(2,1)} %get-tuple-element.460.near0, bf16[5,512,256]{2,1,0:T(8,128)(2,1)} %get-tuple-element.461.near1, bf16[5,512,256]{2,1,0:T(8,128)(2,1)} %get-tuple-element.462.own0, bf16[5,512,256]{2,1,0:T(8,128)(2,1)} %get-tuple-element.463.own1), custom_call_target="tpu_custom_call" | custom-call | flops 1024 | bytes 1024 | tf_op jit(solution)/shard_map/table_terms/pallas_call | solution.py:288
  554.9 4.2 pack_gru_terms.2
  560.2 19.9 %collective-permute-done.37 = bf16[288,768]{1,0:T(8,128)(2,1)} collective-permute-done((bf16[288,768]{1,0:T(8,128)(2,1)S(1)}, bf16[288,768]{1,0:T(8,128)(2,1)}, u32[]{:S(2)}, u32[]{:S(2)}) %collective-permute-start.37) | collective-permute-done | bytes 442400 | tf_op jit(solution)/shard_map/ppermute | solution.py:658
  581.4 6.0 collective-permute-done.28
  596.4 6.4 collective-permute-done.32
  606.9 5.0 pack_gru_terms.3
  613.1 4.5 collective-permute-done.40
  623.9 7.7 collective-permute-done.53
  637.3 15.3 %collective-permute-done.55 = bf16[480,384]{1,0:T(8,128)(2,1)S(1)} collective-permute-done((bf16[480,384]{1,0:T(8,128)(2,1)S(1)}, bf16[480,384]{1,0:T(8,128)(2,1)S(1)}, u32[]{:S(2)}, u32[]{:S(2)}) %collective-permute-start.55) | collective-permute-done | bytes 368672 | tf_op jit(solution)/shard_map/ppermute | solution.py:658
  662.3 5.7 collective-permute-done.56
  668.0 6.1 collective-permute-done.57
  674.1 15.7 %collective-permute-done.58 = bf16[480,384]{1,0:T(8,128)(2,1)} collective-permute-done((bf16[480,384]{1,0:T(8,128)(2,1)S(1)}, bf16[480,384]{1,0:T(8,128)(2,1)}, u32[]{:S(2)}, u32[]{:S(2)}) %collective-permute-start.58) | collective-permute-done | bytes 368672 | tf_op jit(solution)/shard_map/ppermute | solution.py:658
  697.5 4.5 collective-permute-start.61
  702.0 19.7 %collective-permute-done.59 = bf16[1920,384]{1,0:T(8,128)(2,1)S(1)} collective-permute-done((bf16[1920,384]{1,0:T(8,128)(2,1)S(1)}, bf16[1920,384]{1,0:T(8,128)(2,1)S(1)}, u32[]{:S(2)}, u32[]{:S(2)}) %collective-permute-start.59) | collective-permute-done | bytes 1474592 | tf_op jit(solution)/shard_map/ppermute | solution.py:658
  721.7 10.5 %collective-permute-done.42 = bf16[640,384]{1,0:T(8,128)(2,1)S(1)} collective-permute-done((bf16[640,384]{1,0:T(8,128)(2,1)S(1)}, bf16[640,384]{1,0:T(8,128)(2,1)S(1)}, u32[]{:S(2)}, u32[]{:S(2)}) %collective-permute-start.42) | collective-permute-done | bytes 491552 | tf_op jit(solution)/shard_map/ppermute | solution.py:658
  740.9 5.7 collective-permute-done.47
  754.5 5.9 collective-permute-done.50
  766.2 5.3 collective-permute-done.51
  780.5 4.9 unpack_halves.4
  785.5 4.1 unpack_halves.5
  797.2 9.5 %unpack_halves.7 = f32[2304,1536]{1,0:T(8,128)} custom-call(s32[2]{0:T(128)} %pad_add_fusion.15.where, bf16[2304,768]{1,0:T(8,128)(2,1)} %copy-done.12, bf16[2304,768]{1,0:T(8,128)(2,1)} %collective-permute-done.61.other), custom_call_target="tpu_custom_call" | custom-call | flops 1024 | bytes 1024 | tf_op jit(solution)/shard_map/unpack_halves/pallas_call | solution.py:366
  806.8 8.4 %unpack_halves.6 = (f32[1536,768]{1,0:T(8,128)}, f32[384,3072]{1,0:T(8,128)}, f32[384,768]{1,0:T(8,128)}, f32[384,768]{1,0:T(8,128)}) custom-call(s32[2]{0:T(128)} %pad_add_fusion.15.where, bf16[3840,384]{1,0:T(8,128)(2,1)} %pad_maximum_fusion.3.mine, bf16[3840,384]{1,0:T(8,128)(2,1)} %collective-permute-done.60.other), custom_call_target="tpu_custom_call" | custom-call | flops 1024 | bytes 1024 | tf_op jit(solution)/shard_map/unpack_halves/pallas_call | solution.py:366
  (684 shorter events, 307.9 us)
Async XLA Ops:
  7.2 212.2 %all-gather.2.cloned.1.call-start = ((), (), s32[]{:S(2)}) async-start(), calls=%async_computation | async-start | bytes 15040512 | tf_op jit(solution)/shard_map/all_gather | solution.py:1031
  11.1 20.8 %collective-permute-start = (bf16[1152,384]{1,0:T(8,128)(2,1)}, bf16[1152,384]{1,0:T(8,128)(2,1)S(1)}, u32[]{:S(2)}, u32[]{:S(2)}) collective-permute-start(bf16[1152,384]{1,0:T(8,128)(2,1)} %pack_halves.4), channel_id=1, source_target_pairs={{0,1},{1,0},{2,3},{3,2},{4,5},{5,4},{6,7},{7,6},{8,9},{9,8},{10,11... | collective-permute-start | bytes 2654216 | tf_op jit(solution)/shard_map/ppermute | solution.py:663
  35.6 30.2 %collective-permute-start.1 = (bf16[960,384]{1,0:T(8,128)(2,1)}, bf16[960,384]{1,0:T(8,128)(2,1)}, u32[]{:S(2)}, u32[]{:S(2)}) collective-permute-start(bf16[960,384]{1,0:T(8,128)(2,1)} %pack_halves.5), channel_id=1, source_target_pairs={{0,1},{1,0},{2,3},{3,2},{4,5},{5,4},{6,7},{7,6},{8,9},{9,8},{10,11... | collective-permute-start | bytes 2211848 | tf_op jit(solution)/shard_map/ppermute | solution.py:663
  36.8 29.0 %collective-permute-start.5 = (bf16[3,48,1536]{2,1,0:T(8,128)(2,1)S(1)}, bf16[3,48,1536]{2,1,0:T(8,128)(2,1)}, u32[]{:S(2)}, u32[]{:S(2)}) collective-permute-start(bf16[3,48,1536]{2,1,0:T(8,128)(2,1)S(1)} %dynamic-slice_convert_fusion.1), channel_id=1, source_target_pairs={{0,1},{1,0},{2,3},{3,2},{4,5},{5,4},{6,7},{7,6},{8,9},{9,8},{10,11... | collective-permute-start | bytes 1327112 | tf_op jit(solution)/shard_map/ppermute | solution.py:663
  72.4 52.8 %collective-permute-start.8 = (bf16[512,1536]{1,0:T(8,128)(2,1)S(1)}, bf16[512,1536]{1,0:T(8,128)(2,1)}, u32[]{:S(2)}, u32[]{:S(2)}) collective-permute-start(bf16[512,1536]{1,0:T(8,128)(2,1)S(1)} %pad_maximum_fusion.18), channel_id=1, source_target_pairs={{0,1},{1,0},{2,3},{3,2},{4,5},{5,4},{6,7},{7,6},{8,9},{9,8},{10,11... | collective-permute-start | bytes 4718600 | tf_op jit(solution)/shard_map/ppermute | solution.py:663
  77.6 14.1 %collective-permute-start.7 = (bf16[960,384]{1,0:T(8,128)(2,1)}, bf16[960,384]{1,0:T(8,128)(2,1)}, u32[]{:S(2)}, u32[]{:S(2)}) collective-permute-start(bf16[960,384]{1,0:T(8,128)(2,1)} %collective-permute-done.1.refs_2_), channel_id=1, source_target_pairs={{0,2},{2,0},{1,3},{3,1},{4,6},{6,4},{5,7},{7,5},{8,10},{10,8},{9,1... | collective-permute-start | bytes 2211848 | tf_op jit(solution)/shard_map/ppermute | solution.py:656
  81.0 44.2 %collective-permute-start.6 = (bf16[960,384]{1,0:T(8,128)(2,1)}, bf16[960,384]{1,0:T(8,128)(2,1)}, u32[]{:S(2)}, u32[]{:S(2)}) collective-permute-start(bf16[960,384]{1,0:T(8,128)(2,1)} %constant_dynamic-slice_fusion.6), channel_id=1, source_target_pairs={{0,1},{1,0},{2,3},{3,2},{4,5},{5,4},{6,7},{7,6},{8,9},{9,8},{10,11... | collective-permute-start | bytes 2211848 | tf_op jit(solution)/shard_map/ppermute | solution.py:663
  88.9 57.6 %collective-permute-start.10 = (bf16[1152,384]{1,0:T(8,128)(2,1)}, bf16[1152,384]{1,0:T(8,128)(2,1)}, u32[]{:S(2)}, u32[]{:S(2)}) collective-permute-start(bf16[1152,384]{1,0:T(8,128)(2,1)} %constant_dynamic-slice_fusion.5), channel_id=1, source_target_pairs={{0,1},{1,0},{2,3},{3,2},{4,5},{5,4},{6,7},{7,6},{8,9},{9,8},{10,11... | collective-permute-start | bytes 2654216 | tf_op jit(solution)/shard_map/ppermute | solution.py:663
  125.2 33.0 %collective-permute-start.9 = (bf16[960,384]{1,0:T(8,128)(2,1)}, bf16[960,384]{1,0:T(8,128)(2,1)S(1)}, u32[]{:S(2)}, u32[]{:S(2)}) collective-permute-start(bf16[960,384]{1,0:T(8,128)(2,1)} %collective-permute-done.6), channel_id=1, source_target_pairs={{0,4},{4,0},{8,12},{12,8},{16,20},{20,16},{24,28},{28,24},{1,5},{5... | collective-permute-start | bytes 2211848 | tf_op jit(solution)/shard_map/ppermute | solution.py:658
  164.9 27.3 %collective-permute-start.12 = (bf16[1152,384]{1,0:T(8,128)(2,1)}, bf16[1152,384]{1,0:T(8,128)(2,1)}, u32[]{:S(2)}, u32[]{:S(2)}) collective-permute-start(bf16[1152,384]{1,0:T(8,128)(2,1)} %collective-permute-done.10), channel_id=1, source_target_pairs={{0,4},{4,0},{8,12},{12,8},{16,20},{20,16},{24,28},{28,24},{1,5},{5... | collective-permute-start | bytes 2654216 | tf_op jit(solution)/shard_map/ppermute | solution.py:658
  252.3 12.0 %collective-permute-start.15 = (bf16[514,2304]{1,0:T(8,128)(2,1)}, bf16[514,2304]{1,0:T(8,128)(2,1)}, u32[]{:S(2)}, u32[]{:S(2)}) collective-permute-start(bf16[514,2304]{1,0:T(8,128)(2,1)} %fusion.22), channel_id=1, source_target_pairs={{0,2},{2,0},{1,3},{3,1},{4,6},{6,4},{5,7},{7,5},{8,10},{10,8},{9,1... | collective-permute-start | bytes 7105544 | tf_op jit(solution)/shard_map/ppermute | solution.py:656
  298.5 30.3 %collective-permute-start.18 = (bf16[512,10752]{1,0:T(8,128)(2,1)}, bf16[512,10752]{1,0:T(8,128)(2,1)}, u32[]{:S(2)}, u32[]{:S(2)}) collective-permute-start(bf16[512,10752]{1,0:T(8,128)(2,1)} %constant_dynamic-update-slice_fusion.2.a0.b0), channel_id=1, source_target_pairs={{0,2},{2,0},{1,3},{3,1},{4,6},{6,4},{5,7},{7,5},{8,10},{10,8},{9,1... | collective-permute-start | bytes 33030152 | tf_op jit(solution)/shard_map/ppermute | solution.py:656
  300.2 78.2 %collective-permute-start.17 = (bf16[2304,768]{1,0:T(8,128)(2,1)}, bf16[2304,768]{1,0:T(8,128)(2,1)}, u32[]{:S(2)}, u32[]{:S(2)}) collective-permute-start(bf16[2304,768]{1,0:T(8,128)(2,1)} %pad_maximum_fusion), channel_id=1, source_target_pairs={{0,1},{1,0},{2,3},{3,2},{4,5},{5,4},{6,7},{7,6},{8,9},{9,8},{10,11... | collective-permute-start | bytes 10616840 | tf_op jit(solution)/shard_map/ppermute | solution.py:663
  386.6 46.4 %collective-permute-start.21 = (bf16[512,3072]{1,0:T(8,128)(2,1)S(1)}, bf16[512,3072]{1,0:T(8,128)(2,1)}, u32[]{:S(2)}, u32[]{:S(2)}) collective-permute-start(bf16[512,3072]{1,0:T(8,128)(2,1)S(1)} %pad_maximum_fusion.2.a0.b0), channel_id=1, source_target_pairs={{0,2},{2,0},{1,3},{3,1},{4,6},{6,4},{5,7},{7,5},{8,10},{10,8},{9,1... | collective-permute-start | bytes 9437192 | tf_op jit(solution)/shard_map/ppermute | solution.py:656
  387.7 45.3 %collective-permute-start.19 = (bf16[1152,768]{1,0:T(8,128)(2,1)}, bf16[1152,768]{1,0:T(8,128)(2,1)}, u32[]{:S(2)}, u32[]{:S(2)}) collective-permute-start(bf16[1152,768]{1,0:T(8,128)(2,1)} %constant_dynamic-slice_fusion.3), channel_id=1, source_target_pairs={{0,4},{4,0},{8,12},{12,8},{16,20},{20,16},{24,28},{28,24},{1,5},{5... | collective-permute-start | bytes 5308424 | tf_op jit(solution)/shard_map/ppermute | solution.py:658
  387.7 45.2 %collective-permute-start.20 = (bf16[2,512,768]{2,1,0:T(8,128)(2,1)}, bf16[2,512,768]{2,1,0:T(8,128)(2,1)}, u32[]{:S(2)}, u32[]{:S(2)}) collective-permute-start(bf16[2,512,768]{2,1,0:T(8,128)(2,1)} %get-tuple-element.389), channel_id=1, source_target_pairs={{0,1},{1,0},{2,3},{3,2},{4,5},{5,4},{6,7},{7,6},{8,9},{9,8},{10,11... | collective-permute-start | bytes 4718600 | tf_op jit(solution)/shard_map/ppermute | solution.py:663
  439.4 28.4 %collective-permute-start.22 = (bf16[2,512,768]{2,1,0:T(8,128)(2,1)S(1)}, bf16[2,512,768]{2,1,0:T(8,128)(2,1)}, u32[]{:S(2)}, u32[]{:S(2)}) collective-permute-start(bf16[2,512,768]{2,1,0:T(8,128)(2,1)S(1)} %add_convert_fusion.2.b0), channel_id=1, source_target_pairs={{0,2},{2,0},{1,3},{3,1},{4,6},{6,4},{5,7},{7,5},{8,10},{10,8},{9,1... | collective-permute-start | bytes 4718600 | tf_op jit(solution)/shard_map/ppermute | solution.py:656
  441.3 84.8 %collective-permute-start.27 = (bf16[3840,384]{1,0:T(8,128)(2,1)}, bf16[3840,384]{1,0:T(8,128)(2,1)}, u32[]{:S(2)}, u32[]{:S(2)}) collective-permute-start(bf16[3840,384]{1,0:T(8,128)(2,1)} %block_terms.4), channel_id=1, source_target_pairs={{0,1},{1,0},{2,3},{3,2},{4,5},{5,4},{6,7},{7,6},{8,9},{9,8},{10,11... | collective-permute-start | bytes 8847368 | tf_op jit(solution)/shard_map/ppermute | solution.py:663
  458.9 67.3 %collective-permute-start.24 = (bf16[288,768]{1,0:T(8,128)(2,1)}, bf16[288,768]{1,0:T(8,128)(2,1)}, u32[]{:S(2)}, u32[]{:S(2)}) collective-permute-start(bf16[288,768]{1,0:T(8,128)(2,1)} %get-tuple-element.424), channel_id=1, source_target_pairs={{0,8},{4,12},{8,0},{12,4},{16,24},{20,28},{24,16},{28,20},{1,9},{5... | collective-permute-start | bytes 1327112 | tf_op jit(solution)/shard_map/ppermute | solution.py:658
  460.2 66.0 %collective-permute-start.25 = (bf16[288,768]{1,0:T(8,128)(2,1)}, bf16[288,768]{1,0:T(8,128)(2,1)}, u32[]{:S(2)}, u32[]{:S(2)}) collective-permute-start(bf16[288,768]{1,0:T(8,128)(2,1)} %get-tuple-element.425), channel_id=1, source_target_pairs={{0,16},{4,20},{8,24},{12,28},{16,0},{20,4},{24,8},{28,12},{1,17},{... | collective-permute-start | bytes 1327112 | tf_op jit(solution)/shard_map/ppermute | solution.py:658
  460.4 65.8 %collective-permute-start.26 = (bf16[288,768]{1,0:T(8,128)(2,1)}, bf16[288,768]{1,0:T(8,128)(2,1)}, u32[]{:S(2)}, u32[]{:S(2)}) collective-permute-start(bf16[288,768]{1,0:T(8,128)(2,1)} %get-tuple-element.426), channel_id=1, source_target_pairs={{0,24},{4,28},{8,16},{12,20},{16,8},{20,12},{24,0},{28,4},{1,25},{... | collective-permute-start | bytes 1327112 | tf_op jit(solution)/shard_map/ppermute | solution.py:658
  477.0 55.4 %collective-permute-start.23 = (bf16[1536,384]{1,0:T(8,128)(2,1)}, bf16[1536,384]{1,0:T(8,128)(2,1)}, u32[]{:S(2)}, u32[]{:S(2)}) collective-permute-start(bf16[1536,384]{1,0:T(8,128)(2,1)} %pad_maximum_fusion.24), channel_id=1, source_target_pairs={{0,1},{1,0},{2,3},{3,2},{4,5},{5,4},{6,7},{7,6},{8,9},{9,8},{10,11... | collective-permute-start | bytes 3538952 | tf_op jit(solution)/shard_map/ppermute | solution.py:663
  539.8 19.3 %collective-permute-start.35 = (bf16[288,768]{1,0:T(8,128)(2,1)S(1)}, bf16[288,768]{1,0:T(8,128)(2,1)S(1)}, u32[]{:S(2)}, u32[]{:S(2)}) collective-permute-start(bf16[288,768]{1,0:T(8,128)(2,1)S(1)} %fusion.47), channel_id=1, source_target_pairs={{0,8},{4,12},{8,0},{12,4},{16,24},{20,28},{24,16},{28,20},{1,9},{5... | collective-permute-start | bytes 1327112 | tf_op jit(solution)/shard_map/ppermute | solution.py:658
  541.1 19.0 %collective-permute-start.36 = (bf16[288,768]{1,0:T(8,128)(2,1)S(1)}, bf16[288,768]{1,0:T(8,128)(2,1)}, u32[]{:S(2)}, u32[]{:S(2)}) collective-permute-start(bf16[288,768]{1,0:T(8,128)(2,1)S(1)} %fusion.47), channel_id=1, source_target_pairs={{0,16},{4,20},{8,24},{12,28},{16,0},{20,4},{24,8},{28,12},{1,17},{... | collective-permute-start | bytes 1327112 | tf_op jit(solution)/shard_map/ppermute | solution.py:658
  541.3 38.8 %collective-permute-start.37 = (bf16[288,768]{1,0:T(8,128)(2,1)S(1)}, bf16[288,768]{1,0:T(8,128)(2,1)}, u32[]{:S(2)}, u32[]{:S(2)}) collective-permute-start(bf16[288,768]{1,0:T(8,128)(2,1)S(1)} %fusion.47), channel_id=1, source_target_pairs={{0,24},{4,28},{8,16},{12,20},{16,8},{20,12},{24,0},{28,4},{1,25},{... | collective-permute-start | bytes 1327112 | tf_op jit(solution)/shard_map/ppermute | solution.py:658
  542.5 75.2 %collective-permute-start.33 = (bf16[1920,384]{1,0:T(8,128)(2,1)}, bf16[1920,384]{1,0:T(8,128)(2,1)}, u32[]{:S(2)}, u32[]{:S(2)}) collective-permute-start(bf16[1920,384]{1,0:T(8,128)(2,1)} %constant_dynamic-slice_fusion.1), channel_id=1, source_target_pairs={{0,4},{4,0},{8,12},{12,8},{16,20},{20,16},{24,28},{28,24},{1,5},{5... | collective-permute-start | bytes 4423688 | tf_op jit(solution)/shard_map/ppermute | solution.py:658
  544.5 43.0 %collective-permute-start.28 = (bf16[768,384]{1,0:T(8,128)(2,1)S(1)}, bf16[768,384]{1,0:T(8,128)(2,1)S(1)}, u32[]{:S(2)}, u32[]{:S(2)}) collective-permute-start(bf16[768,384]{1,0:T(8,128)(2,1)S(1)} %constant_dynamic-slice_fusion.2), channel_id=1, source_target_pairs={{0,4},{4,0},{8,12},{12,8},{16,20},{20,16},{24,28},{28,24},{1,5},{5... | collective-permute-start | bytes 1769480 | tf_op jit(solution)/shard_map/ppermute | solution.py:658
  590.0 12.8 %collective-permute-start.32 = (bf16[192,384]{1,0:T(8,128)(2,1)S(1)}, bf16[192,384]{1,0:T(8,128)(2,1)S(1)}, u32[]{:S(2)}, u32[]{:S(2)}) collective-permute-start(bf16[192,384]{1,0:T(8,128)(2,1)S(1)} %get-tuple-element.492), channel_id=1, source_target_pairs={{0,24},{4,28},{8,16},{12,20},{16,8},{20,12},{24,0},{28,4},{1,25},{... | collective-permute-start | bytes 442376 | tf_op jit(solution)/shard_map/ppermute | solution.py:658
  591.4 61.3 %collective-permute-start.29 = (bf16[2,1280,384]{2,1,0:T(8,128)(2,1)}, bf16[2,1280,384]{2,1,0:T(8,128)(2,1)}, u32[]{:S(2)}, u32[]{:S(2)}) collective-permute-start(bf16[2,1280,384]{2,1,0:T(8,128)(2,1)} %pack_gru_terms.2), channel_id=1, source_target_pairs={{0,2},{2,0},{1,3},{3,1},{4,6},{6,4},{5,7},{7,5},{8,10},{10,8},{9,1... | collective-permute-start | bytes 5898248 | tf_op jit(solution)/shard_map/ppermute | solution.py:656
  602.9 10.2 %collective-permute-start.39 = (bf16[192,384]{1,0:T(8,128)(2,1)S(1)}, bf16[192,384]{1,0:T(8,128)(2,1)}, u32[]{:S(2)}, u32[]{:S(2)}) collective-permute-start(bf16[192,384]{1,0:T(8,128)(2,1)S(1)} %fusion.87), channel_id=1, source_target_pairs={{0,16},{4,20},{8,24},{12,28},{16,0},{20,4},{24,8},{28,12},{1,17},{... | collective-permute-start | bytes 442376 | tf_op jit(solution)/shard_map/ppermute | solution.py:658
  604.7 12.9 %collective-permute-start.40 = (bf16[192,384]{1,0:T(8,128)(2,1)S(1)}, bf16[192,384]{1,0:T(8,128)(2,1)}, u32[]{:S(2)}, u32[]{:S(2)}) collective-permute-start(bf16[192,384]{1,0:T(8,128)(2,1)S(1)} %fusion.87), channel_id=1, source_target_pairs={{0,24},{4,28},{8,16},{12,20},{16,8},{20,12},{24,0},{28,4},{1,25},{... | collective-permute-start | bytes 442376 | tf_op jit(solution)/shard_map/ppermute | solution.py:658
  611.9 50.5 %collective-permute-start.41 = (bf16[1152,768]{1,0:T(8,128)(2,1)}, bf16[1152,768]{1,0:T(8,128)(2,1)}, u32[]{:S(2)}, u32[]{:S(2)}) collective-permute-start(bf16[1152,768]{1,0:T(8,128)(2,1)} %pad_maximum_fusion.7), channel_id=1, source_target_pairs={{0,4},{4,0},{8,12},{12,8},{16,20},{20,16},{24,28},{28,24},{1,5},{5... | collective-permute-start | bytes 5308424 | tf_op jit(solution)/shard_map/ppermute | solution.py:658
  620.0 11.7 %collective-permute-start.53 = (bf16[480,384]{1,0:T(8,128)(2,1)S(1)}, bf16[480,384]{1,0:T(8,128)(2,1)S(1)}, u32[]{:S(2)}, u32[]{:S(2)}) collective-permute-start(bf16[480,384]{1,0:T(8,128)(2,1)S(1)} %get-tuple-element.550), channel_id=1, source_target_pairs={{0,8},{4,12},{8,0},{12,4},{16,24},{20,28},{24,16},{28,20},{1,9},{5... | collective-permute-start | bytes 1105928 | tf_op jit(solution)/shard_map/ppermute | solution.py:658
  620.0 17.3 %collective-permute-start.54 = (bf16[480,384]{1,0:T(8,128)(2,1)S(1)}, bf16[480,384]{1,0:T(8,128)(2,1)S(1)}, u32[]{:S(2)}, u32[]{:S(2)}) collective-permute-start(bf16[480,384]{1,0:T(8,128)(2,1)S(1)} %get-tuple-element.551), channel_id=1, source_target_pairs={{0,16},{4,20},{8,24},{12,28},{16,0},{20,4},{24,8},{28,12},{1,17},{... | collective-permute-start | bytes 1105928 | tf_op jit(solution)/shard_map/ppermute | solution.py:658
  622.4 30.2 %collective-permute-start.55 = (bf16[480,384]{1,0:T(8,128)(2,1)S(1)}, bf16[480,384]{1,0:T(8,128)(2,1)S(1)}, u32[]{:S(2)}, u32[]{:S(2)}) collective-permute-start(bf16[480,384]{1,0:T(8,128)(2,1)S(1)} %get-tuple-element.552), channel_id=1, source_target_pairs={{0,24},{4,28},{8,16},{12,20},{16,8},{20,12},{24,0},{28,4},{1,25},{... | collective-permute-start | bytes 1105928 | tf_op jit(solution)/shard_map/ppermute | solution.py:658
  631.7 29.6 %collective-permute-start.43 = (bf16[768,384]{1,0:T(8,128)(2,1)S(1)}, bf16[768,384]{1,0:T(8,128)(2,1)}, u32[]{:S(2)}, u32[]{:S(2)}) collective-permute-start(bf16[768,384]{1,0:T(8,128)(2,1)S(1)} %pad_maximum_fusion.29), channel_id=1, source_target_pairs={{0,4},{4,0},{8,12},{12,8},{16,20},{20,16},{24,28},{28,24},{1,5},{5... | collective-permute-start | bytes 1769480 | tf_op jit(solution)/shard_map/ppermute | solution.py:658
  656.7 36.5 %collective-permute-start.34 = (bf16[1280,384]{1,0:T(8,128)(2,1)S(1)}, bf16[1280,384]{1,0:T(8,128)(2,1)S(1)}, u32[]{:S(2)}, u32[]{:S(2)}) collective-permute-start(bf16[1280,384]{1,0:T(8,128)(2,1)S(1)} %fusion.44), channel_id=1, source_target_pairs={{0,1},{1,0},{2,3},{3,2},{4,5},{5,4},{6,7},{7,6},{8,9},{9,8},{10,11... | collective-permute-start | bytes 2949128 | tf_op jit(solution)/shard_map/ppermute | solution.py:663
  657.4 10.6 %collective-permute-start.56 = (bf16[480,384]{1,0:T(8,128)(2,1)S(1)}, bf16[480,384]{1,0:T(8,128)(2,1)}, u32[]{:S(2)}, u32[]{:S(2)}) collective-permute-start(bf16[480,384]{1,0:T(8,128)(2,1)S(1)} %fusion.68), channel_id=1, source_target_pairs={{0,8},{4,12},{8,0},{12,4},{16,24},{20,28},{24,16},{28,20},{1,9},{5... | collective-permute-start | bytes 1105928 | tf_op jit(solution)/shard_map/ppermute | solution.py:658
  657.5 16.7 %collective-permute-start.57 = (bf16[480,384]{1,0:T(8,128)(2,1)S(1)}, bf16[480,384]{1,0:T(8,128)(2,1)}, u32[]{:S(2)}, u32[]{:S(2)}) collective-permute-start(bf16[480,384]{1,0:T(8,128)(2,1)S(1)} %fusion.68), channel_id=1, source_target_pairs={{0,16},{4,20},{8,24},{12,28},{16,0},{20,4},{24,8},{28,12},{1,17},{... | collective-permute-start | bytes 1105928 | tf_op jit(solution)/shard_map/ppermute | solution.py:658
  661.3 28.6 %collective-permute-start.58 = (bf16[480,384]{1,0:T(8,128)(2,1)S(1)}, bf16[480,384]{1,0:T(8,128)(2,1)}, u32[]{:S(2)}, u32[]{:S(2)}) collective-permute-start(bf16[480,384]{1,0:T(8,128)(2,1)S(1)} %fusion.68), channel_id=1, source_target_pairs={{0,24},{4,28},{8,16},{12,20},{16,8},{20,12},{24,0},{28,4},{1,25},{... | collective-permute-start | bytes 1105928 | tf_op jit(solution)/shard_map/ppermute | solution.py:658
  691.6 30.0 %collective-permute-start.59 = (bf16[1920,384]{1,0:T(8,128)(2,1)S(1)}, bf16[1920,384]{1,0:T(8,128)(2,1)S(1)}, u32[]{:S(2)}, u32[]{:S(2)}) collective-permute-start(bf16[1920,384]{1,0:T(8,128)(2,1)S(1)} %pad_maximum_fusion.23), channel_id=1, source_target_pairs={{0,4},{4,0},{8,12},{12,8},{16,20},{20,16},{24,28},{28,24},{1,5},{5... | collective-permute-start | bytes 4423688 | tf_op jit(solution)/shard_map/ppermute | solution.py:658
  693.7 38.5 %collective-permute-start.42 = (bf16[640,384]{1,0:T(8,128)(2,1)S(1)}, bf16[640,384]{1,0:T(8,128)(2,1)S(1)}, u32[]{:S(2)}, u32[]{:S(2)}) collective-permute-start(bf16[640,384]{1,0:T(8,128)(2,1)S(1)} %constant_dynamic-slice_fusion), channel_id=1, source_target_pairs={{0,4},{4,0},{8,12},{12,8},{16,20},{20,16},{24,28},{28,24},{1,5},{5... | collective-permute-start | bytes 1474568 | tf_op jit(solution)/shard_map/ppermute | solution.py:658
  697.5 99.1 %collective-permute-start.61 = (bf16[2304,768]{1,0:T(8,128)(2,1)S(1)}, bf16[2304,768]{1,0:T(8,128)(2,1)}, u32[]{:S(2)}, u32[]{:S(2)}) collective-permute-start(bf16[2304,768]{1,0:T(8,128)(2,1)S(1)} %pad_maximum_fusion.1.mine), channel_id=1, source_target_pairs={{0,2},{2,0},{1,3},{3,1},{4,6},{6,4},{5,7},{7,5},{8,10},{10,8},{9,1... | collective-permute-start | bytes 10616840 | tf_op jit(solution)/shard_map/ppermute | solution.py:656
  736.7 10.0 %collective-permute-start.47 = (bf16[160,384]{1,0:T(8,128)(2,1)S(1)}, bf16[160,384]{1,0:T(8,128)(2,1)S(1)}, u32[]{:S(2)}, u32[]{:S(2)}) collective-permute-start(bf16[160,384]{1,0:T(8,128)(2,1)S(1)} %get-tuple-element.537), channel_id=1, source_target_pairs={{0,24},{4,28},{8,16},{12,20},{16,8},{20,12},{24,0},{28,4},{1,25},{... | collective-permute-start | bytes 368648 | tf_op jit(solution)/shard_map/ppermute | solution.py:658
  748.7 11.7 %collective-permute-start.50 = (bf16[160,384]{1,0:T(8,128)(2,1)S(1)}, bf16[160,384]{1,0:T(8,128)(2,1)S(1)}, u32[]{:S(2)}, u32[]{:S(2)}) collective-permute-start(bf16[160,384]{1,0:T(8,128)(2,1)S(1)} %fusion.90), channel_id=1, source_target_pairs={{0,24},{4,28},{8,16},{12,20},{16,8},{20,12},{24,0},{28,4},{1,25},{... | collective-permute-start | bytes 368648 | tf_op jit(solution)/shard_map/ppermute | solution.py:658
  751.4 45.2 %collective-permute-start.60 = (bf16[3840,384]{1,0:T(8,128)(2,1)}, bf16[3840,384]{1,0:T(8,128)(2,1)}, u32[]{:S(2)}, u32[]{:S(2)}) collective-permute-start(bf16[3840,384]{1,0:T(8,128)(2,1)} %pad_maximum_fusion.3.mine), channel_id=1, source_target_pairs={{0,2},{2,0},{1,3},{3,1},{4,6},{6,4},{5,7},{7,5},{8,10},{10,8},{9,1... | collective-permute-start | bytes 8847368 | tf_op jit(solution)/shard_map/ppermute | solution.py:656
  760.6 10.9 %collective-permute-start.51 = (bf16[640,384]{1,0:T(8,128)(2,1)S(1)}, bf16[640,384]{1,0:T(8,128)(2,1)S(1)}, u32[]{:S(2)}, u32[]{:S(2)}) collective-permute-start(bf16[640,384]{1,0:T(8,128)(2,1)S(1)} %pad_maximum_fusion.33), channel_id=1, source_target_pairs={{0,4},{4,0},{8,12},{12,8},{16,20},{20,16},{24,28},{28,24},{1,5},{5... | collective-permute-start | bytes 1474568 | tf_op jit(solution)/shard_map/ppermute | solution.py:658
  762.2 14.8 %collective-permute-start.44 = (bf16[1536,384]{1,0:T(8,128)(2,1)S(1)}, bf16[1536,384]{1,0:T(8,128)(2,1)S(1)}, u32[]{:S(2)}, u32[]{:S(2)}) collective-permute-start(bf16[1536,384]{1,0:T(8,128)(2,1)S(1)} %pad_maximum_fusion.25.mine), channel_id=1, source_target_pairs={{0,2},{2,0},{1,3},{3,1},{4,6},{6,4},{5,7},{7,5},{8,10},{10,8},{9,1... | collective-permute-start | bytes 3538952 | tf_op jit(solution)/shard_map/ppermute | solution.py:656
  (151 other events, 1266.5 us)
Sparse Core Ops, SparseCore 0:
  68.1 134.2 all-gather.1

commit v3 on v2

--- a/solution.py
+++ b/solution.py
@@ -29,7 +29,7 @@
 
 
 def chunks(rows):
-    size = min(rows, 256)
+    size = min(rows, 512)
     return [slice(start, start + size) for start in range(0, rows, size)]
 
 
@@ -1316,9 +1316,15 @@
             (tail_rows, chars, "rows"), (vector_terms.shape[2], PACK, "stacked"),
         ],
     )
+    owned_shards = {}
     for name in TAIL + "abcd" * 16:
+        if name == "d" and len(gru_flow.stages) == 1 and not merging_flow.stages:
+            shards_now = weights_of(merging_flow.value, shapes["a"])
+            gru_flow.got, owned_shards["a"] = lax.optimization_barrier((gru_flow.got, shards_now))
         token, _ = turn(token, [flows[name]], [])
-    owned_shards = {name: weights_of(flow.value, shapes[name]) for name, flow in flows.items()}
+    for name, flow in flows.items():
+        if name not in owned_shards:
+            owned_shards[name] = weights_of(flow.value, shapes[name])
     (merging_out,) = owned_shards["a"]
     merging_out = merging_out.reshape(3, joint, 2 * width)
     shrink_out, expand_out, token_proj_out, char_proj_out = owned_shards["b"]

time: 834 us -> 834 us (level)
    unnamed x306 -> x286, local copies, waits for them, and re-layouts: 27.5 us -> 27.6 us
  transfers between devices with their start and end apart: 63 -> 63, of which waited for: 25 -> 26; matrix products, arithmetic and copies ran while one was open for 20% -> 21% of each run, Pallas kernels for 31% -> 32%
where the time goes in v3:
time: 834 us; the launch traced here: 822 us
  Pallas kernels  276 us (33%)
  waiting for transfers between devices  184 us (22%)
  matrix products  112 us (13%)
  local copies, waits for them, and re-layouts  79.6 us (10%)
  other arithmetic  79 us (9%)
  starting transfers between devices  74.9 us (9%)
  between operations  16.9 us (2%)
    ppermute x34, waiting for transfers between devices, flip(): lax.ppermute(value, 'pair', [(i, i ^ bit // 2) for i in range(count)])  163 us
    pallas_call x2, Pallas kernels, gru_backward(): pl.pallas_call(functools.partial(gru_backward_kernel, slots, last), grid=...  84.3 us
    dot_general x12, matrix products, dot(): return jnp.dot(left, right, preferred_element_type=F32)  45.7 us
    dot_general x11, matrix products, back_product(): return jnp.einsum('rg,cg->rc', grad, weight, preferred_element_type=F32)  41.9 us
    pallas_call x4, Pallas kernels, block_terms(): pl.pallas_call(block_terms_kernel, grid_spec=pltpu.PrefetchScalarGridSpec...  36.7 us
    ppermute x34, starting transfers between devices, flip(): lax.ppermute(value, 'pair', [(i, i ^ bit // 2) for i in range(count)])  31.8 us
    ppermute x13, starting transfers between devices, flip(): return lax.ppermute(value, 'core', [(0, 1), (1, 0)])  30 us
    pallas_call x1, Pallas kernels, gru_forward(): pl.pallas_call(functools.partial(gru_forward_kernel, slots), grid=(2 * sl...  28.4 us
  transfers between devices with their start and end apart: 63, of which 26 were waited for; matrix products, arithmetic and copies ran while one was open for 21% of the time, Pallas kernels for 32%

profile of v3, /device:TPU:17, one launch (start us, length us, event | category | flops | bytes accessed | tf_op | source)
XLA Modules:
  0.0 821.7 jit_solution(16485099703731998756)
XLA Ops:
  21.3 10.6 %collective-permute-done.refs_3_ = bf16[1152,384]{1,0:T(8,128)(2,1)S(1)} collective-permute-done((bf16[1152,384]{1,0:T(8,128)(2,1)}, bf16[1152,384]{1,0:T(8,128)(2,1)S(1)}, u32[]{:S(2)}, u32[]{:S(2)}) %collective-permute-start) | collective-permute-done | bytes 884768 | tf_op jit(solution)/shard_map/ppermute | solution.py:663
  41.9 5.3 join_halves.4
  50.5 4.0 pack_halves.7
  82.2 5.1 convolution_convert_fusion
  91.7 5.2 join_halves.5
  96.9 28.4 %gru_forward.1 = (f32[10,2,512,384]{3,2,1,0:T(8,128)}, bf16[512,768]{1,0:T(8,128)(2,1)}) custom-call(bf16[5,512,256]{2,1,0:T(8,128)(2,1)} %get-tuple-element.650.a0.x0, bf16[5,512,256]{2,1,0:T(8,128)(2,1)} %get-tuple-element.649.a1.x1, bf16[5,512,256]{2,1,0:T(8,128)(2,1)} %get-tuple-element.648.b0.b1.x0.x1, ...), custom_call_target="tpu_custom_call" | custom-call | flops 1024 | bytes 1024 | tf_op jit(solution)/shard_map/gru_forward/pallas_call | solution.py:104
  130.1 16.5 %attend.1 = (bf16[512,768]{1,0:T(8,128)(2,1)}, f32[6,2,512]{2,1,0:T(2,128)}) custom-call(bf16[512,768]{1,0:T(8,128)(2,1)} %fusion.41.q, bf16[1024,768]{1,0:T(8,128)(2,1)} %get-tuple-element.611.k, bf16[1024,768]{1,0:T(8,128)(2,1)} %get-tuple-element.610.v, s32[1,512]{1,0:T(1,128)} %bitcast.301, s32[1024,1]{1,0:T(8,128)} %copy.134.seg_k), custom_call_target="tpu_custom_call" | custom-call | flops 1024 | bytes 1024 | tf_op jit(solution)/shard_map/attend/pallas_call | solution.py:517
  146.6 11.8 %collective-permute-done.9 = bf16[960,384]{1,0:T(8,128)(2,1)S(1)} collective-permute-done((bf16[960,384]{1,0:T(8,128)(2,1)}, bf16[960,384]{1,0:T(8,128)(2,1)S(1)}, u32[]{:S(2)}, u32[]{:S(2)}) %collective-permute-start.9) | collective-permute-done | bytes 737312 | tf_op jit(solution)/shard_map/ppermute | solution.py:658
  159.8 5.1 collective-permute-start.11
  169.1 6.8 join_halves.6
  179.1 11.3 %multiply_convert_fusion = (bf16[512,3072]{1,0:T(8,128)(2,1)}, f32[512,3072]{1,0:T(8,128)}) fusion(f32[3072]{0:T(1024)S(1)} %add.644, bf16[768,3072]{1,0:T(8,128)(2,1)S(1)} %copy-done.114, f32[512,768]{1,0:T(8,128)S(1)} %get-tuple-element.733, f32[768]{0:T(1024)S(1)} %add.641, f32[768]{0:T(1024)S(1)} %mul.456, f32[512]{0:T(512)S(1)} %fusion.109, ...), kind=kOutput, calls=%fused_computation.13 | convolution fusion | flops 2469789696 | bytes 15751168 | tf_op jit(solution)/shard_map/dot_general | solution.py:16
  199.7 7.5 join_halves.7
  209.5 6.2 convert_dynamic-update-slice_fusion
  219.4 5.9 fusion.124
  231.7 5.7 fusion.18
  244.6 5.1 convert_reduce_fusion.1
  259.3 4.5 fusion.135
  285.7 11.6 %constant_dynamic-update-slice_fusion.3 = (bf16[512,10752]{1,0:T(8,128)(2,1)}, bf16[512,3072]{1,0:T(8,128)(2,1)}) fusion(bf16[512,10752]{1,0:T(8,128)(2,1)} %get-tuple-element.741, f32[512,3072]{1,0:T(8,128)S(1)} %bitcast.316, f32[3072]{0:T(1024)S(1)} %add.644, bf16[3072,768]{1,0:T(8,128)(2,1)S(1)} %bitcast.314, f32[512,768]{1,0:T(8,128)S(1)} %get-tuple-element.742), kind=kOutput, calls=%fused_computation.272 | convolution fusion | flops 2476081152 | bytes 18886656 | tf_op jit(solution)/shard_map/rg,cg->rc/dot_general | solution.py:643
  302.7 6.4 multiply_reduce_fusion
  328.9 12.1 %block_terms.5 = bf16[3840,384]{1,0:T(8,128)(2,1)} custom-call(s32[2,10]{1,0:T(2,128)} %pad_add_fusion.10.table, bf16[512,10752]{1,0:T(8,128)(2,1)} %constant_dynamic-update-slice_fusion.2.a0.b0, bf16[512,10752]{1,0:T(8,128)(2,1)} %constant_dynamic-update-slice_fusion.2.a0.b0, bf16[512,10752]{1,0:T(8,128)(2,1)} %collective-permute-done.18.a1.b1, ...), custom_call_target="tpu_custom_call" | custom-call | flops 1024 | bytes 1024 | tf_op jit(solution)/shard_map/block_terms/pallas_call | solution.py:314
  341.0 12.1 %block_terms.4 = bf16[3840,384]{1,0:T(8,128)(2,1)} custom-call(s32[2,10]{1,0:T(2,128)} %pad_add_fusion.9.table, bf16[512,10752]{1,0:T(8,128)(2,1)} %constant_dynamic-update-slice_fusion.2.a0.b0, bf16[512,10752]{1,0:T(8,128)(2,1)} %constant_dynamic-update-slice_fusion.2.a0.b0, bf16[512,10752]{1,0:T(8,128)(2,1)} %collective-permute-done.18.a1.b1, ...), custom_call_target="tpu_custom_call" | custom-call | flops 1024 | bytes 1024 | tf_op jit(solution)/shard_map/block_terms/pallas_call | solution.py:314
  353.2 25.4 %attend_back.1 = (bf16[512,768]{1,0:T(8,128)(2,1)}, bf16[2,512,768]{2,1,0:T(8,128)(2,1)}, bf16[2,512,768]{2,1,0:T(8,128)(2,1)}) custom-call(bf16[512,768]{1,0:T(8,128)(2,1)} %fusion.41.q, bf16[1024,768]{1,0:T(8,128)(2,1)} %get-tuple-element.611.k, bf16[1024,768]{1,0:T(8,128)(2,1)} %get-tuple-element.610.v, s32[1,512]{1,0:T(1,128)} %bitcast.302, ...), custom_call_target="tpu_custom_call" | custom-call | flops 1024 | bytes 1024 | tf_op jit(solution)/shard_map/attend_back/pallas_call | solution.py:577
  378.6 3.9 fusion.1
  390.6 41.7 %gru_backward.2 = (bf16[5,512,256]{2,1,0:T(8,128)(2,1)}, bf16[5,512,256]{2,1,0:T(8,128)(2,1)}, f32[2,512,384]{2,1,0:T(8,128)}, f32[2,256,1152]{2,1,0:T(8,128)}, ...) custom-call(bf16[5,512,256]{2,1,0:T(8,128)(2,1)} %get-tuple-element.648.b0.b1.x0.x1, ...), custom_call_target="tpu_custom_call" | custom-call | flops 1024 | bytes 1024 | tf_op jit(solution)/shard_map/gru_backward/pallas_call | solution.py:190
  460.9 6.3 block_terms.6
  467.2 6.2 block_terms.7
  482.3 42.6 %gru_backward.3 = (bf16[5,512,256]{2,1,0:T(8,128)(2,1)}, bf16[5,512,256]{2,1,0:T(8,128)(2,1)}, f32[2,512,384]{2,1,0:T(8,128)}, f32[2,256,1152]{2,1,0:T(8,128)}, ...) custom-call(bf16[5,512,256]{2,1,0:T(8,128)(2,1)} %get-tuple-element.650.a0.x0, ...), custom_call_target="tpu_custom_call" | custom-call | flops 1024 | bytes 1024 | tf_op jit(solution)/shard_map/gru_backward/pallas_call | solution.py:190
  525.0 6.7 collective-permute-done.23
  544.1 9.5 %table_terms.1 = f32[1024,256]{1,0:T(8,128)} custom-call(s32[3,5,512,1]{3,2,1,0:T(8,128)} %copy.142.ids, bf16[5,512,256]{2,1,0:T(8,128)(2,1)} %get-tuple-element.462.near0, bf16[5,512,256]{2,1,0:T(8,128)(2,1)} %get-tuple-element.463.near1, bf16[5,512,256]{2,1,0:T(8,128)(2,1)} %get-tuple-element.464.own0, bf16[5,512,256]{2,1,0:T(8,128)(2,1)} %get-tuple-element.465.own1), custom_call_target="tpu_custom_call" | custom-call | flops 1024 | bytes 1024 | tf_op jit(solution)/shard_map/table_terms/pallas_call | solution.py:288
  554.3 4.2 pack_gru_terms.2
  560.7 20.1 %collective-permute-done.37 = bf16[288,768]{1,0:T(8,128)(2,1)} collective-permute-done((bf16[288,768]{1,0:T(8,128)(2,1)S(1)}, bf16[288,768]{1,0:T(8,128)(2,1)}, u32[]{:S(2)}, u32[]{:S(2)}) %collective-permute-start.37) | collective-permute-done | bytes 442400 | tf_op jit(solution)/shard_map/ppermute | solution.py:658
  593.1 7.0 collective-permute-done.32
  604.3 5.0 pack_gru_terms.3
  611.1 4.8 collective-permute-done.40
  622.2 8.6 %collective-permute-done.54 = bf16[480,384]{1,0:T(8,128)(2,1)S(1)} collective-permute-done((bf16[480,384]{1,0:T(8,128)(2,1)S(1)}, bf16[480,384]{1,0:T(8,128)(2,1)S(1)}, u32[]{:S(2)}, u32[]{:S(2)}) %collective-permute-start.54) | collective-permute-done | bytes 368672 | tf_op jit(solution)/shard_map/ppermute | solution.py:658
  633.1 18.8 %collective-permute-done.56 = bf16[480,384]{1,0:T(8,128)(2,1)S(1)} collective-permute-done((bf16[480,384]{1,0:T(8,128)(2,1)S(1)}, bf16[480,384]{1,0:T(8,128)(2,1)S(1)}, u32[]{:S(2)}, u32[]{:S(2)}) %collective-permute-start.56) | collective-permute-done | bytes 368672 | tf_op jit(solution)/shard_map/ppermute | solution.py:658
  659.9 7.2 collective-permute-done.57
  670.6 18.6 %collective-permute-done.59 = bf16[480,384]{1,0:T(8,128)(2,1)} collective-permute-done((bf16[480,384]{1,0:T(8,128)(2,1)S(1)}, bf16[480,384]{1,0:T(8,128)(2,1)}, u32[]{:S(2)}, u32[]{:S(2)}) %collective-permute-start.59) | collective-permute-done | bytes 368672 | tf_op jit(solution)/shard_map/ppermute | solution.py:658
  702.2 20.2 %collective-permute-done.60 = bf16[1920,384]{1,0:T(8,128)(2,1)S(1)} collective-permute-done((bf16[1920,384]{1,0:T(8,128)(2,1)S(1)}, bf16[1920,384]{1,0:T(8,128)(2,1)S(1)}, u32[]{:S(2)}, u32[]{:S(2)}) %collective-permute-start.60) | collective-permute-done | bytes 1474592 | tf_op jit(solution)/shard_map/ppermute | solution.py:658
  722.4 10.5 %collective-permute-done.42 = bf16[640,384]{1,0:T(8,128)(2,1)S(1)} collective-permute-done((bf16[640,384]{1,0:T(8,128)(2,1)S(1)}, bf16[640,384]{1,0:T(8,128)(2,1)S(1)}, u32[]{:S(2)}, u32[]{:S(2)}) %collective-permute-start.42) | collective-permute-done | bytes 491552 | tf_op jit(solution)/shard_map/ppermute | solution.py:658
  738.1 7.3 collective-permute-done.47
  753.6 4.8 collective-permute-done.50
  763.4 6.0 collective-permute-done.51
  779.0 9.8 %unpack_halves.5 = f32[2304,1536]{1,0:T(8,128)} custom-call(s32[2]{0:T(128)} %pad_add_fusion.15.where, bf16[2304,768]{1,0:T(8,128)(2,1)} %copy-done.12, bf16[2304,768]{1,0:T(8,128)(2,1)} %copy-done.42), custom_call_target="tpu_custom_call" | custom-call | flops 1024 | bytes 1024 | tf_op jit(solution)/shard_map/unpack_halves/pallas_call | solution.py:366
  788.8 4.4 add_add_fusion.3
  793.3 4.7 unpack_halves.4
  798.0 4.1 unpack_halves.6
  806.1 8.4 %unpack_halves.7 = (f32[1536,768]{1,0:T(8,128)}, f32[384,3072]{1,0:T(8,128)}, f32[384,768]{1,0:T(8,128)}, f32[384,768]{1,0:T(8,128)}) custom-call(s32[2]{0:T(128)} %pad_add_fusion.15.where, bf16[3840,384]{1,0:T(8,128)(2,1)} %pad_maximum_fusion.3.mine, bf16[3840,384]{1,0:T(8,128)(2,1)} %collective-permute-done.61.other), custom_call_target="tpu_custom_call" | custom-call | flops 1024 | bytes 1024 | tf_op jit(solution)/shard_map/unpack_halves/pallas_call | solution.py:366
  (664 shorter events, 300.7 us)
Async XLA Ops:
  7.2 212.2 %all-gather.2.cloned.1.call-start = ((), (), s32[]{:S(2)}) async-start(), calls=%async_computation | async-start | bytes 15040512 | tf_op jit(solution)/shard_map/all_gather | solution.py:1031
  11.1 20.8 %collective-permute-start = (bf16[1152,384]{1,0:T(8,128)(2,1)}, bf16[1152,384]{1,0:T(8,128)(2,1)S(1)}, u32[]{:S(2)}, u32[]{:S(2)}) collective-permute-start(bf16[1152,384]{1,0:T(8,128)(2,1)} %pack_halves.4), channel_id=1, source_target_pairs={{0,1},{1,0},{2,3},{3,2},{4,5},{5,4},{6,7},{7,6},{8,9},{9,8},{10,11... | collective-permute-start | bytes 2654216 | tf_op jit(solution)/shard_map/ppermute | solution.py:663
  35.6 30.2 %collective-permute-start.1 = (bf16[960,384]{1,0:T(8,128)(2,1)}, bf16[960,384]{1,0:T(8,128)(2,1)}, u32[]{:S(2)}, u32[]{:S(2)}) collective-permute-start(bf16[960,384]{1,0:T(8,128)(2,1)} %pack_halves.5), channel_id=1, source_target_pairs={{0,1},{1,0},{2,3},{3,2},{4,5},{5,4},{6,7},{7,6},{8,9},{9,8},{10,11... | collective-permute-start | bytes 2211848 | tf_op jit(solution)/shard_map/ppermute | solution.py:663
  36.8 29.0 %collective-permute-start.5 = (bf16[3,48,1536]{2,1,0:T(8,128)(2,1)S(1)}, bf16[3,48,1536]{2,1,0:T(8,128)(2,1)}, u32[]{:S(2)}, u32[]{:S(2)}) collective-permute-start(bf16[3,48,1536]{2,1,0:T(8,128)(2,1)S(1)} %dynamic-slice_convert_fusion.1), channel_id=1, source_target_pairs={{0,1},{1,0},{2,3},{3,2},{4,5},{5,4},{6,7},{7,6},{8,9},{9,8},{10,11... | collective-permute-start | bytes 1327112 | tf_op jit(solution)/shard_map/ppermute | solution.py:663
  72.4 52.9 %collective-permute-start.8 = (bf16[512,1536]{1,0:T(8,128)(2,1)S(1)}, bf16[512,1536]{1,0:T(8,128)(2,1)}, u32[]{:S(2)}, u32[]{:S(2)}) collective-permute-start(bf16[512,1536]{1,0:T(8,128)(2,1)S(1)} %pad_maximum_fusion.18), channel_id=1, source_target_pairs={{0,1},{1,0},{2,3},{3,2},{4,5},{5,4},{6,7},{7,6},{8,9},{9,8},{10,11... | collective-permute-start | bytes 4718600 | tf_op jit(solution)/shard_map/ppermute | solution.py:663
  77.6 14.1 %collective-permute-start.7 = (bf16[960,384]{1,0:T(8,128)(2,1)}, bf16[960,384]{1,0:T(8,128)(2,1)}, u32[]{:S(2)}, u32[]{:S(2)}) collective-permute-start(bf16[960,384]{1,0:T(8,128)(2,1)} %collective-permute-done.1.refs_2_), channel_id=1, source_target_pairs={{0,2},{2,0},{1,3},{3,1},{4,6},{6,4},{5,7},{7,5},{8,10},{10,8},{9,1... | collective-permute-start | bytes 2211848 | tf_op jit(solution)/shard_map/ppermute | solution.py:656
  81.0 44.3 %collective-permute-start.6 = (bf16[960,384]{1,0:T(8,128)(2,1)}, bf16[960,384]{1,0:T(8,128)(2,1)}, u32[]{:S(2)}, u32[]{:S(2)}) collective-permute-start(bf16[960,384]{1,0:T(8,128)(2,1)} %constant_dynamic-slice_fusion.6), channel_id=1, source_target_pairs={{0,1},{1,0},{2,3},{3,2},{4,5},{5,4},{6,7},{7,6},{8,9},{9,8},{10,11... | collective-permute-start | bytes 2211848 | tf_op jit(solution)/shard_map/ppermute | solution.py:663
  88.9 57.7 %collective-permute-start.10 = (bf16[1152,384]{1,0:T(8,128)(2,1)}, bf16[1152,384]{1,0:T(8,128)(2,1)}, u32[]{:S(2)}, u32[]{:S(2)}) collective-permute-start(bf16[1152,384]{1,0:T(8,128)(2,1)} %constant_dynamic-slice_fusion.5), channel_id=1, source_target_pairs={{0,1},{1,0},{2,3},{3,2},{4,5},{5,4},{6,7},{7,6},{8,9},{9,8},{10,11... | collective-permute-start | bytes 2654216 | tf_op jit(solution)/shard_map/ppermute | solution.py:663
  125.3 33.1 %collective-permute-start.9 = (bf16[960,384]{1,0:T(8,128)(2,1)}, bf16[960,384]{1,0:T(8,128)(2,1)S(1)}, u32[]{:S(2)}, u32[]{:S(2)}) collective-permute-start(bf16[960,384]{1,0:T(8,128)(2,1)} %collective-permute-done.6), channel_id=1, source_target_pairs={{0,4},{4,0},{8,12},{12,8},{16,20},{20,16},{24,28},{28,24},{1,5},{5... | collective-permute-start | bytes 2211848 | tf_op jit(solution)/shard_map/ppermute | solution.py:658
  164.9 27.3 %collective-permute-start.12 = (bf16[1152,384]{1,0:T(8,128)(2,1)}, bf16[1152,384]{1,0:T(8,128)(2,1)}, u32[]{:S(2)}, u32[]{:S(2)}) collective-permute-start(bf16[1152,384]{1,0:T(8,128)(2,1)} %collective-permute-done.10), channel_id=1, source_target_pairs={{0,4},{4,0},{8,12},{12,8},{16,20},{20,16},{24,28},{28,24},{1,5},{5... | collective-permute-start | bytes 2654216 | tf_op jit(solution)/shard_map/ppermute | solution.py:658
  252.3 12.0 %collective-permute-start.15 = (bf16[514,2304]{1,0:T(8,128)(2,1)}, bf16[514,2304]{1,0:T(8,128)(2,1)}, u32[]{:S(2)}, u32[]{:S(2)}) collective-permute-start(bf16[514,2304]{1,0:T(8,128)(2,1)} %fusion.22), channel_id=1, source_target_pairs={{0,2},{2,0},{1,3},{3,1},{4,6},{6,4},{5,7},{7,5},{8,10},{10,8},{9,1... | collective-permute-start | bytes 7105544 | tf_op jit(solution)/shard_map/ppermute | solution.py:656
  298.5 30.4 %collective-permute-start.18 = (bf16[512,10752]{1,0:T(8,128)(2,1)}, bf16[512,10752]{1,0:T(8,128)(2,1)}, u32[]{:S(2)}, u32[]{:S(2)}) collective-permute-start(bf16[512,10752]{1,0:T(8,128)(2,1)} %constant_dynamic-update-slice_fusion.2.a0.b0), channel_id=1, source_target_pairs={{0,2},{2,0},{1,3},{3,1},{4,6},{6,4},{5,7},{7,5},{8,10},{10,8},{9,1... | collective-permute-start | bytes 33030152 | tf_op jit(solution)/shard_map/ppermute | solution.py:656
  300.3 78.3 %collective-permute-start.17 = (bf16[2304,768]{1,0:T(8,128)(2,1)}, bf16[2304,768]{1,0:T(8,128)(2,1)}, u32[]{:S(2)}, u32[]{:S(2)}) collective-permute-start(bf16[2304,768]{1,0:T(8,128)(2,1)} %pad_maximum_fusion), channel_id=1, source_target_pairs={{0,1},{1,0},{2,3},{3,2},{4,5},{5,4},{6,7},{7,6},{8,9},{9,8},{10,11... | collective-permute-start | bytes 10616840 | tf_op jit(solution)/shard_map/ppermute | solution.py:663
  386.7 45.6 %collective-permute-start.21 = (bf16[512,3072]{1,0:T(8,128)(2,1)S(1)}, bf16[512,3072]{1,0:T(8,128)(2,1)}, u32[]{:S(2)}, u32[]{:S(2)}) collective-permute-start(bf16[512,3072]{1,0:T(8,128)(2,1)S(1)} %pad_maximum_fusion.2.a0.b0), channel_id=1, source_target_pairs={{0,2},{2,0},{1,3},{3,1},{4,6},{6,4},{5,7},{7,5},{8,10},{10,8},{9,1... | collective-permute-start | bytes 9437192 | tf_op jit(solution)/shard_map/ppermute | solution.py:656
  387.7 44.6 %collective-permute-start.19 = (bf16[1152,768]{1,0:T(8,128)(2,1)}, bf16[1152,768]{1,0:T(8,128)(2,1)}, u32[]{:S(2)}, u32[]{:S(2)}) collective-permute-start(bf16[1152,768]{1,0:T(8,128)(2,1)} %constant_dynamic-slice_fusion.3), channel_id=1, source_target_pairs={{0,4},{4,0},{8,12},{12,8},{16,20},{20,16},{24,28},{28,24},{1,5},{5... | collective-permute-start | bytes 5308424 | tf_op jit(solution)/shard_map/ppermute | solution.py:658
  387.8 44.6 %collective-permute-start.20 = (bf16[2,512,768]{2,1,0:T(8,128)(2,1)}, bf16[2,512,768]{2,1,0:T(8,128)(2,1)}, u32[]{:S(2)}, u32[]{:S(2)}) collective-permute-start(bf16[2,512,768]{2,1,0:T(8,128)(2,1)} %get-tuple-element.391), channel_id=1, source_target_pairs={{0,1},{1,0},{2,3},{3,2},{4,5},{5,4},{6,7},{7,6},{8,9},{9,8},{10,11... | collective-permute-start | bytes 4718600 | tf_op jit(solution)/shard_map/ppermute | solution.py:663
  438.8 28.4 %collective-permute-start.22 = (bf16[2,512,768]{2,1,0:T(8,128)(2,1)S(1)}, bf16[2,512,768]{2,1,0:T(8,128)(2,1)}, u32[]{:S(2)}, u32[]{:S(2)}) collective-permute-start(bf16[2,512,768]{2,1,0:T(8,128)(2,1)S(1)} %add_convert_fusion.2.b0), channel_id=1, source_target_pairs={{0,2},{2,0},{1,3},{3,1},{4,6},{6,4},{5,7},{7,5},{8,10},{10,8},{9,1... | collective-permute-start | bytes 4718600 | tf_op jit(solution)/shard_map/ppermute | solution.py:656
  440.7 84.2 %collective-permute-start.27 = (bf16[3840,384]{1,0:T(8,128)(2,1)}, bf16[3840,384]{1,0:T(8,128)(2,1)}, u32[]{:S(2)}, u32[]{:S(2)}) collective-permute-start(bf16[3840,384]{1,0:T(8,128)(2,1)} %block_terms.4), channel_id=1, source_target_pairs={{0,1},{1,0},{2,3},{3,2},{4,5},{5,4},{6,7},{7,6},{8,9},{9,8},{10,11... | collective-permute-start | bytes 8847368 | tf_op jit(solution)/shard_map/ppermute | solution.py:663
  458.3 66.7 %collective-permute-start.24 = (bf16[288,768]{1,0:T(8,128)(2,1)}, bf16[288,768]{1,0:T(8,128)(2,1)}, u32[]{:S(2)}, u32[]{:S(2)}) collective-permute-start(bf16[288,768]{1,0:T(8,128)(2,1)} %get-tuple-element.426), channel_id=1, source_target_pairs={{0,8},{4,12},{8,0},{12,4},{16,24},{20,28},{24,16},{28,20},{1,9},{5... | collective-permute-start | bytes 1327112 | tf_op jit(solution)/shard_map/ppermute | solution.py:658
  459.7 65.3 %collective-permute-start.25 = (bf16[288,768]{1,0:T(8,128)(2,1)}, bf16[288,768]{1,0:T(8,128)(2,1)}, u32[]{:S(2)}, u32[]{:S(2)}) collective-permute-start(bf16[288,768]{1,0:T(8,128)(2,1)} %get-tuple-element.427), channel_id=1, source_target_pairs={{0,16},{4,20},{8,24},{12,28},{16,0},{20,4},{24,8},{28,12},{1,17},{... | collective-permute-start | bytes 1327112 | tf_op jit(solution)/shard_map/ppermute | solution.py:658
  459.8 65.2 %collective-permute-start.26 = (bf16[288,768]{1,0:T(8,128)(2,1)}, bf16[288,768]{1,0:T(8,128)(2,1)}, u32[]{:S(2)}, u32[]{:S(2)}) collective-permute-start(bf16[288,768]{1,0:T(8,128)(2,1)} %get-tuple-element.428), channel_id=1, source_target_pairs={{0,24},{4,28},{8,16},{12,20},{16,8},{20,12},{24,0},{28,4},{1,25},{... | collective-permute-start | bytes 1327112 | tf_op jit(solution)/shard_map/ppermute | solution.py:658
  476.3 55.3 %collective-permute-start.23 = (bf16[1536,384]{1,0:T(8,128)(2,1)}, bf16[1536,384]{1,0:T(8,128)(2,1)}, u32[]{:S(2)}, u32[]{:S(2)}) collective-permute-start(bf16[1536,384]{1,0:T(8,128)(2,1)} %pad_maximum_fusion.24), channel_id=1, source_target_pairs={{0,1},{1,0},{2,3},{3,2},{4,5},{5,4},{6,7},{7,6},{8,9},{9,8},{10,11... | collective-permute-start | bytes 3538952 | tf_op jit(solution)/shard_map/ppermute | solution.py:663
  539.1 76.8 %collective-permute-start.33 = (bf16[1920,384]{1,0:T(8,128)(2,1)}, bf16[1920,384]{1,0:T(8,128)(2,1)}, u32[]{:S(2)}, u32[]{:S(2)}) collective-permute-start(bf16[1920,384]{1,0:T(8,128)(2,1)} %constant_dynamic-slice_fusion.1), channel_id=1, source_target_pairs={{0,4},{4,0},{8,12},{12,8},{16,20},{20,16},{24,28},{28,24},{1,5},{5... | collective-permute-start | bytes 4423688 | tf_op jit(solution)/shard_map/ppermute | solution.py:658
  540.8 17.7 %collective-permute-start.35 = (bf16[288,768]{1,0:T(8,128)(2,1)S(1)}, bf16[288,768]{1,0:T(8,128)(2,1)S(1)}, u32[]{:S(2)}, u32[]{:S(2)}) collective-permute-start(bf16[288,768]{1,0:T(8,128)(2,1)S(1)} %fusion.47), channel_id=1, source_target_pairs={{0,8},{4,12},{8,0},{12,4},{16,24},{20,28},{24,16},{28,20},{1,9},{5... | collective-permute-start | bytes 1327112 | tf_op jit(solution)/shard_map/ppermute | solution.py:658
  541.6 19.1 %collective-permute-start.36 = (bf16[288,768]{1,0:T(8,128)(2,1)S(1)}, bf16[288,768]{1,0:T(8,128)(2,1)}, u32[]{:S(2)}, u32[]{:S(2)}) collective-permute-start(bf16[288,768]{1,0:T(8,128)(2,1)S(1)} %fusion.47), channel_id=1, source_target_pairs={{0,16},{4,20},{8,24},{12,28},{16,0},{20,4},{24,8},{28,12},{1,17},{... | collective-permute-start | bytes 1327112 | tf_op jit(solution)/shard_map/ppermute | solution.py:658
  542.1 38.7 %collective-permute-start.37 = (bf16[288,768]{1,0:T(8,128)(2,1)S(1)}, bf16[288,768]{1,0:T(8,128)(2,1)}, u32[]{:S(2)}, u32[]{:S(2)}) collective-permute-start(bf16[288,768]{1,0:T(8,128)(2,1)S(1)} %fusion.47), channel_id=1, source_target_pairs={{0,24},{4,28},{8,16},{12,20},{16,8},{20,12},{24,0},{28,4},{1,25},{... | collective-permute-start | bytes 1327112 | tf_op jit(solution)/shard_map/ppermute | solution.py:658
  543.9 41.2 %collective-permute-start.28 = (bf16[768,384]{1,0:T(8,128)(2,1)S(1)}, bf16[768,384]{1,0:T(8,128)(2,1)S(1)}, u32[]{:S(2)}, u32[]{:S(2)}) collective-permute-start(bf16[768,384]{1,0:T(8,128)(2,1)S(1)} %constant_dynamic-slice_fusion.2), channel_id=1, source_target_pairs={{0,4},{4,0},{8,12},{12,8},{16,20},{20,16},{24,28},{28,24},{1,5},{5... | collective-permute-start | bytes 1769480 | tf_op jit(solution)/shard_map/ppermute | solution.py:658
  586.8 13.3 %collective-permute-start.32 = (bf16[192,384]{1,0:T(8,128)(2,1)S(1)}, bf16[192,384]{1,0:T(8,128)(2,1)S(1)}, u32[]{:S(2)}, u32[]{:S(2)}) collective-permute-start(bf16[192,384]{1,0:T(8,128)(2,1)S(1)} %get-tuple-element.494), channel_id=1, source_target_pairs={{0,24},{4,28},{8,16},{12,20},{16,8},{20,12},{24,0},{28,4},{1,25},{... | collective-permute-start | bytes 442376 | tf_op jit(solution)/shard_map/ppermute | solution.py:658
  588.4 63.5 %collective-permute-start.29 = (bf16[2,1280,384]{2,1,0:T(8,128)(2,1)}, bf16[2,1280,384]{2,1,0:T(8,128)(2,1)}, u32[]{:S(2)}, u32[]{:S(2)}) collective-permute-start(bf16[2,1280,384]{2,1,0:T(8,128)(2,1)} %pack_gru_terms.2), channel_id=1, source_target_pairs={{0,2},{2,0},{1,3},{3,1},{4,6},{6,4},{5,7},{7,5},{8,10},{10,8},{9,1... | collective-permute-start | bytes 5898248 | tf_op jit(solution)/shard_map/ppermute | solution.py:656
  600.3 10.8 %collective-permute-start.39 = (bf16[192,384]{1,0:T(8,128)(2,1)S(1)}, bf16[192,384]{1,0:T(8,128)(2,1)}, u32[]{:S(2)}, u32[]{:S(2)}) collective-permute-start(bf16[192,384]{1,0:T(8,128)(2,1)S(1)} %fusion.87), channel_id=1, source_target_pairs={{0,16},{4,20},{8,24},{12,28},{16,0},{20,4},{24,8},{28,12},{1,17},{... | collective-permute-start | bytes 442376 | tf_op jit(solution)/shard_map/ppermute | solution.py:658
  601.4 14.5 %collective-permute-start.40 = (bf16[192,384]{1,0:T(8,128)(2,1)S(1)}, bf16[192,384]{1,0:T(8,128)(2,1)}, u32[]{:S(2)}, u32[]{:S(2)}) collective-permute-start(bf16[192,384]{1,0:T(8,128)(2,1)S(1)} %fusion.87), channel_id=1, source_target_pairs={{0,24},{4,28},{8,16},{12,20},{16,8},{20,12},{24,0},{28,4},{1,25},{... | collective-permute-start | bytes 442376 | tf_op jit(solution)/shard_map/ppermute | solution.py:658
  609.3 83.8 %collective-permute-start.41 = (bf16[1152,768]{1,0:T(8,128)(2,1)}, bf16[1152,768]{1,0:T(8,128)(2,1)}, u32[]{:S(2)}, u32[]{:S(2)}) collective-permute-start(bf16[1152,768]{1,0:T(8,128)(2,1)} %pad_maximum_fusion.7), channel_id=1, source_target_pairs={{0,4},{4,0},{8,12},{12,8},{16,20},{20,16},{24,28},{28,24},{1,5},{5... | collective-permute-start | bytes 5308424 | tf_op jit(solution)/shard_map/ppermute | solution.py:658
  618.3 12.5 %collective-permute-start.54 = (bf16[480,384]{1,0:T(8,128)(2,1)S(1)}, bf16[480,384]{1,0:T(8,128)(2,1)S(1)}, u32[]{:S(2)}, u32[]{:S(2)}) collective-permute-start(bf16[480,384]{1,0:T(8,128)(2,1)S(1)} %get-tuple-element.554), channel_id=1, source_target_pairs={{0,8},{4,12},{8,0},{12,4},{16,24},{20,28},{24,16},{28,20},{1,9},{5... | collective-permute-start | bytes 1105928 | tf_op jit(solution)/shard_map/ppermute | solution.py:658
  618.3 14.7 %collective-permute-start.55 = (bf16[480,384]{1,0:T(8,128)(2,1)S(1)}, bf16[480,384]{1,0:T(8,128)(2,1)S(1)}, u32[]{:S(2)}, u32[]{:S(2)}) collective-permute-start(bf16[480,384]{1,0:T(8,128)(2,1)S(1)} %get-tuple-element.555), channel_id=1, source_target_pairs={{0,16},{4,20},{8,24},{12,28},{16,0},{20,4},{24,8},{28,12},{1,17},{... | collective-permute-start | bytes 1105928 | tf_op jit(solution)/shard_map/ppermute | solution.py:658
  618.7 33.2 %collective-permute-start.56 = (bf16[480,384]{1,0:T(8,128)(2,1)S(1)}, bf16[480,384]{1,0:T(8,128)(2,1)S(1)}, u32[]{:S(2)}, u32[]{:S(2)}) collective-permute-start(bf16[480,384]{1,0:T(8,128)(2,1)S(1)} %get-tuple-element.556), channel_id=1, source_target_pairs={{0,24},{4,28},{8,16},{12,20},{16,8},{20,12},{24,0},{28,4},{1,25},{... | collective-permute-start | bytes 1105928 | tf_op jit(solution)/shard_map/ppermute | solution.py:658
  630.8 29.1 %collective-permute-start.43 = (bf16[768,384]{1,0:T(8,128)(2,1)S(1)}, bf16[768,384]{1,0:T(8,128)(2,1)}, u32[]{:S(2)}, u32[]{:S(2)}) collective-permute-start(bf16[768,384]{1,0:T(8,128)(2,1)S(1)} %pad_maximum_fusion.29), channel_id=1, source_target_pairs={{0,4},{4,0},{8,12},{12,8},{16,20},{20,16},{24,28},{28,24},{1,5},{5... | collective-permute-start | bytes 1769480 | tf_op jit(solution)/shard_map/ppermute | solution.py:658
  655.9 37.2 %collective-permute-start.34 = (bf16[1280,384]{1,0:T(8,128)(2,1)S(1)}, bf16[1280,384]{1,0:T(8,128)(2,1)}, u32[]{:S(2)}, u32[]{:S(2)}) collective-permute-start(bf16[1280,384]{1,0:T(8,128)(2,1)S(1)} %fusion.44), channel_id=1, source_target_pairs={{0,1},{1,0},{2,3},{3,2},{4,5},{5,4},{6,7},{7,6},{8,9},{9,8},{10,11... | collective-permute-start | bytes 2949128 | tf_op jit(solution)/shard_map/ppermute | solution.py:663
  656.5 14.1 %collective-permute-start.58 = (bf16[480,384]{1,0:T(8,128)(2,1)S(1)}, bf16[480,384]{1,0:T(8,128)(2,1)}, u32[]{:S(2)}, u32[]{:S(2)}) collective-permute-start(bf16[480,384]{1,0:T(8,128)(2,1)S(1)} %fusion.68), channel_id=1, source_target_pairs={{0,16},{4,20},{8,24},{12,28},{16,0},{20,4},{24,8},{28,12},{1,17},{... | collective-permute-start | bytes 1105928 | tf_op jit(solution)/shard_map/ppermute | solution.py:658
  659.9 29.4 %collective-permute-start.59 = (bf16[480,384]{1,0:T(8,128)(2,1)S(1)}, bf16[480,384]{1,0:T(8,128)(2,1)}, u32[]{:S(2)}, u32[]{:S(2)}) collective-permute-start(bf16[480,384]{1,0:T(8,128)(2,1)S(1)} %fusion.68), channel_id=1, source_target_pairs={{0,24},{4,28},{8,16},{12,20},{16,8},{20,12},{24,0},{28,4},{1,25},{... | collective-permute-start | bytes 1105928 | tf_op jit(solution)/shard_map/ppermute | solution.py:658
  691.0 31.4 %collective-permute-start.60 = (bf16[1920,384]{1,0:T(8,128)(2,1)S(1)}, bf16[1920,384]{1,0:T(8,128)(2,1)S(1)}, u32[]{:S(2)}, u32[]{:S(2)}) collective-permute-start(bf16[1920,384]{1,0:T(8,128)(2,1)S(1)} %pad_maximum_fusion.23), channel_id=1, source_target_pairs={{0,4},{4,0},{8,12},{12,8},{16,20},{20,16},{24,28},{28,24},{1,5},{5... | collective-permute-start | bytes 4423688 | tf_op jit(solution)/shard_map/ppermute | solution.py:658
  694.6 38.3 %collective-permute-start.42 = (bf16[640,384]{1,0:T(8,128)(2,1)S(1)}, bf16[640,384]{1,0:T(8,128)(2,1)S(1)}, u32[]{:S(2)}, u32[]{:S(2)}) collective-permute-start(bf16[640,384]{1,0:T(8,128)(2,1)S(1)} %constant_dynamic-slice_fusion), channel_id=1, source_target_pairs={{0,4},{4,0},{8,12},{12,8},{16,20},{20,16},{24,28},{28,24},{1,5},{5... | collective-permute-start | bytes 1474568 | tf_op jit(solution)/shard_map/ppermute | solution.py:658
  698.5 78.7 %collective-permute-start.53 = (bf16[2304,768]{1,0:T(8,128)(2,1)S(1)}, bf16[2304,768]{1,0:T(8,128)(2,1)S(1)}, u32[]{:S(2)}, u32[]{:S(2)}) collective-permute-start(bf16[2304,768]{1,0:T(8,128)(2,1)S(1)} %pad_maximum_fusion.1.mine), channel_id=1, source_target_pairs={{0,2},{2,0},{1,3},{3,1},{4,6},{6,4},{5,7},{7,5},{8,10},{10,8},{9,1... | collective-permute-start | bytes 10616840 | tf_op jit(solution)/shard_map/ppermute | solution.py:656
  733.7 11.8 %collective-permute-start.47 = (bf16[160,384]{1,0:T(8,128)(2,1)S(1)}, bf16[160,384]{1,0:T(8,128)(2,1)S(1)}, u32[]{:S(2)}, u32[]{:S(2)}) collective-permute-start(bf16[160,384]{1,0:T(8,128)(2,1)S(1)} %get-tuple-element.539), channel_id=1, source_target_pairs={{0,24},{4,28},{8,16},{12,20},{16,8},{20,12},{24,0},{28,4},{1,25},{... | collective-permute-start | bytes 368648 | tf_op jit(solution)/shard_map/ppermute | solution.py:658
  747.4 11.0 %collective-permute-start.50 = (bf16[160,384]{1,0:T(8,128)(2,1)S(1)}, bf16[160,384]{1,0:T(8,128)(2,1)S(1)}, u32[]{:S(2)}, u32[]{:S(2)}) collective-permute-start(bf16[160,384]{1,0:T(8,128)(2,1)S(1)} %fusion.90), channel_id=1, source_target_pairs={{0,24},{4,28},{8,16},{12,20},{16,8},{20,12},{24,0},{28,4},{1,25},{... | collective-permute-start | bytes 368648 | tf_op jit(solution)/shard_map/ppermute | solution.py:658
  750.2 55.2 %collective-permute-start.61 = (bf16[3840,384]{1,0:T(8,128)(2,1)}, bf16[3840,384]{1,0:T(8,128)(2,1)}, u32[]{:S(2)}, u32[]{:S(2)}) collective-permute-start(bf16[3840,384]{1,0:T(8,128)(2,1)} %pad_maximum_fusion.3.mine), channel_id=1, source_target_pairs={{0,2},{2,0},{1,3},{3,1},{4,6},{6,4},{5,7},{7,5},{8,10},{10,8},{9,1... | collective-permute-start | bytes 8847368 | tf_op jit(solution)/shard_map/ppermute | solution.py:656
  758.6 10.8 %collective-permute-start.51 = (bf16[640,384]{1,0:T(8,128)(2,1)S(1)}, bf16[640,384]{1,0:T(8,128)(2,1)S(1)}, u32[]{:S(2)}, u32[]{:S(2)}) collective-permute-start(bf16[640,384]{1,0:T(8,128)(2,1)S(1)} %pad_maximum_fusion.33), channel_id=1, source_target_pairs={{0,4},{4,0},{8,12},{12,8},{16,20},{20,16},{24,28},{28,24},{1,5},{5... | collective-permute-start | bytes 1474568 | tf_op jit(solution)/shard_map/ppermute | solution.py:658
  760.7 18.3 %collective-permute-start.44 = (bf16[1536,384]{1,0:T(8,128)(2,1)S(1)}, bf16[1536,384]{1,0:T(8,128)(2,1)}, u32[]{:S(2)}, u32[]{:S(2)}) collective-permute-start(bf16[1536,384]{1,0:T(8,128)(2,1)S(1)} %pad_maximum_fusion.25.mine), channel_id=1, source_target_pairs={{0,2},{2,0},{1,3},{3,1},{4,6},{6,4},{5,7},{7,5},{8,10},{10,8},{9,1... | collective-permute-start | bytes 3538952 | tf_op jit(solution)/shard_map/ppermute | solution.py:656
  769.7 19.1 %collective-permute-start.52 = (bf16[1280,384]{1,0:T(8,128)(2,1)S(1)}, bf16[1280,384]{1,0:T(8,128)(2,1)}, u32[]{:S(2)}, u32[]{:S(2)}) collective-permute-start(bf16[1280,384]{1,0:T(8,128)(2,1)S(1)} %pad_maximum_fusion.26.mine), channel_id=1, source_target_pairs={{0,2},{2,0},{1,3},{3,1},{4,6},{6,4},{5,7},{7,5},{8,10},{10,8},{9,1... | collective-permute-start | bytes 2949128 | tf_op jit(solution)/shard_map/ppermute | solution.py:656
  (141 other events, 1137.8 us)
Sparse Core Ops, SparseCore 0:
  68.1 134.2 all-gather.1
